TPU v7x, 32 devices: a whole 2x2x4 slice. The times are simulated.
32 devices in a mesh: row: 8 (over z, core), col: 4 (over y, x).
Axes of the slice: x: 2, y: 2, z: 4, core: 2. Of those that a mesh axis runs over, the one named last changes fastest.
Arguments:
- matrix_tiles: float32 [10, 8, 128, 20, 4, 128], P(None, 'row', None, None, 'col'), may hold values from -60715.73 to 60715.73
Outputs:
- reduced: float32 [10, 8, 128, 20, 4, 128], P(None, 'row', None, None, 'col')
All inputs are finite; a program needn't handle non-finite values.
Results may differ from a plain program's by a relative error of at most 0.0003.
Values sent between devices are 32-bit elements; how exact they have to be, the bound alone decides.
A program may use at most 128 MiB of HBM per device.

v0:
```python
import functools

import jax
import jax.numpy as jnp
from jax import lax
from jax.experimental import pallas as pl
from jax.experimental.pallas import tpu as pltpu
from jax.sharding import PartitionSpec as P

BAND = 256
PANELS = 2
BIG = 60 * 1024 * 1024
MESH = pl.DeviceIdType.MESH

HI = lax.Precision.HIGHEST
def mm(a, b, ca, cb):
    return lax.dot_general(a, b, (((ca,), (cb,)), ((), ())), precision=HI, preferred_element_type=jnp.float32)

def base_inverse(block):
    size = block.shape[0]
    wide = (8, 2 * size)
    group = 8
    places = lax.broadcasted_iota(jnp.int32, wide, 0)
    cols = lax.broadcasted_iota(jnp.int32, wide, 1)
    work = []
    for k in range(size // 8):
        unit = jnp.where(places + 8 * k == cols, 1.0, 0.0)[:, :size]
        work.append(jnp.concatenate([block[8 * k : 8 * k + 8], unit], 1))
    for start in range(0, size, group):
        own, offset = divmod(start, 8)
        rows = [jnp.broadcast_to(work[own][offset + i : offset + i + 1], wide) for i in range(group)]
        pivot = [
            [jnp.broadcast_to(rows[i][:, start + j : start + j + 1], wide) for j in range(group)]
            for i in range(group)
        ]
        first = own if offset + group < 8 else own + 1
        columns = [
            [jnp.broadcast_to(work[k][:, start + i : start + i + 1], wide) for i in range(group)]
            for k in range(first, len(work))
        ]
        scaled = []
        for i in range(group):
            inverse = 1.0 / pivot[i][i]
            scaled.append(rows[i] * inverse)
            for j in range(i + 1, group):
                ratio = pivot[i][j] * inverse
                for l in range(j, group):
                    pivot[j][l] = pivot[j][l] - ratio * pivot[i][l]
                rows[j] = rows[j] - ratio * rows[i]
                for column in columns:
                    column[j] = column[j] - ratio * column[i]
        for k, column in zip(range(first, len(work)), columns):
            change = column[0] * scaled[0]
            for i in range(1, group):
                change = change + column[i] * scaled[i]
            if k == own:
                change = jnp.where(places >= offset + group, change, 0.0)
            work[k] = work[k] - change
        for i in range(group):
            work[own] = jnp.where(places == offset + i, rows[i], work[own])
    result = []
    for k, value in enumerate(work):
        pivots = jnp.sum(jnp.where(places + 8 * k == cols, value, 0.0), axis=1, keepdims=True)
        result.append(value[:, size:] * (1.0 / jnp.sqrt(pivots)))
    return jnp.concatenate(result, 0)


def factor_inverse(matrix, base):
    size = matrix.shape[0]
    if size <= base:
        return base_inverse(matrix)
    half = size // 2
    first = factor_inverse(matrix[:half, :half], base)
    lower = mm(matrix[half:, :half], first, 1, 1)
    second = factor_inverse(matrix[half:, half:] - mm(lower, lower, 1, 1), base)
    corner = -mm(second, mm(lower, first, 1, 0), 1, 0)
    top = jnp.concatenate([first, jnp.zeros_like(first)], 1)
    return jnp.concatenate([top, jnp.concatenate([corner, second], 1)], 0)

def factor_kernel(gram_ref, top_ref, inverse_ref, shifted_ref, transform_ref, sign_ref):
    size = gram_ref.shape[0]
    inverse = factor_inverse(gram_ref[...], 64)
    inverse_ref[...] = inverse
    basis = mm(top_ref[...], inverse, 1, 1)
    rows = lax.broadcasted_iota(jnp.int32, (size, size), 0)
    cols = lax.broadcasted_iota(jnp.int32, (size, size), 1)
    on_diagonal = rows == cols
    sign_square = jnp.where(on_diagonal, jnp.where(basis >= 0, -1.0, 1.0), 0.0)
    shifted = basis - sign_square
    shifted_ref[...] = shifted
    outer = factor_inverse(mm(shifted, shifted, 0, 0), 64)
    sign_column = jnp.sum(sign_square, axis=1, keepdims=True)
    transform_ref[...] = -sign_column * mm(mm(shifted, outer, 1, 1), outer, 1, 0)
    sign_ref[...] = jnp.sum(sign_square, axis=0, keepdims=True)


def factors(gram, top):
    size = gram.shape[0]
    square = jax.ShapeDtypeStruct((size, size), jnp.float32)
    return pl.pallas_call(
        factor_kernel,
        out_shape=(square, square, square, jax.ShapeDtypeStruct((1, size), jnp.float32)),
    )(gram, top)


def multiply(first, second, first_dim=1, second_dim=0, precision=HI):
    return lax.dot_general(
        first,
        second,
        (((first_dim,), (second_dim,)), ((), ())),
        precision=precision,
        preferred_element_type=jnp.float32,
    )


def greet(axis, count):
    me = lax.axis_index(axis)
    barrier = pltpu.get_barrier_semaphore()
    for step in range(1, count):
        pl.semaphore_signal(
            barrier, inc=1, device_id={axis: lax.rem(me + step, count)}, device_id_type=MESH
        )
    pl.semaphore_wait(barrier, count - 1)
    return me


def all_reduce_kernel(axis, count, x_ref, out_ref, parts, send_sem, recv_sem, send_two, recv_two):
    me = greet(axis, count)
    copies = []
    for step in range(1, count):
        peer = lax.rem(me + step, count)
        copies.append(
            pltpu.make_async_remote_copy(
                src_ref=x_ref.at[peer],
                dst_ref=parts.at[step - 1],
                send_sem=send_sem.at[step - 1],
                recv_sem=recv_sem.at[step - 1],
                device_id={axis: peer},
                device_id_type=MESH,
            )
        )
        copies[-1].start()
    total = x_ref[me]
    for step in range(1, count):
        copies[step - 1].wait_recv()
        total = total + parts[step - 1]
    out_ref[me] = total
    second = []
    for step in range(1, count):
        peer = lax.rem(me + step, count)
        second.append(
            pltpu.make_async_remote_copy(
                src_ref=out_ref.at[me],
                dst_ref=out_ref.at[me],
                send_sem=send_two.at[step - 1],
                recv_sem=recv_two.at[step - 1],
                device_id={axis: peer},
                device_id_type=MESH,
            )
        )
        second[-1].start()
    for copy in copies:
        copy.wait_send()
    for copy in second:
        copy.wait()


def all_reduce(x, axis, collective_id):
    count = lax.axis_size(axis)
    rows, cols = x.shape
    pieces = (count, rows // count, cols)
    out = pl.pallas_call(
        functools.partial(all_reduce_kernel, axis, count),
        out_shape=jax.ShapeDtypeStruct(pieces, x.dtype),
        in_specs=[pl.BlockSpec(memory_space=pltpu.VMEM)],
        out_specs=pl.BlockSpec(memory_space=pltpu.VMEM),
        scratch_shapes=[pltpu.VMEM((count - 1,) + pieces[1:], x.dtype)]
        + [pltpu.SemaphoreType.DMA((count - 1,))] * 4,
        compiler_params=pltpu.CompilerParams(
            collective_id=collective_id, has_side_effects=True, vmem_limit_bytes=BIG
        ),
    )(x.reshape(pieces))
    return out.reshape(rows, cols)


def share_kernel(rows, cols, x_ref, out_ref, parts, send_sem, recv_sem, send_two, recv_two, send_col, recv_col):
    row_me = lax.axis_index("row")
    col_me = lax.axis_index("col")
    barrier = pltpu.get_barrier_semaphore()
    for axis, me, count in (("row", row_me, rows), ("col", col_me, cols)):
        for step in range(1, count):
            pl.semaphore_signal(
                barrier, inc=1, device_id={axis: lax.rem(me + step, count)}, device_id_type=MESH
            )
    pl.semaphore_wait(barrier, rows + cols - 2)

    def send(source, target, axis, peer, out_sem, in_sem):
        copy = pltpu.make_async_remote_copy(
            src_ref=source,
            dst_ref=target,
            send_sem=out_sem,
            recv_sem=in_sem,
            device_id={axis: peer},
            device_id_type=MESH,
        )
        copy.start()
        return copy

    first, second, third = [], [], []
    for step in range(1, rows):
        peer = lax.rem(row_me + step, rows)
        slot = step - 1
        first.append(
            send(x_ref.at[col_me, peer], parts.at[slot], "row", peer, send_sem.at[slot], recv_sem.at[slot])
        )
    total = x_ref[col_me, row_me]
    for step in range(1, rows):
        first[step - 1].wait_recv()
        total = total + parts[step - 1]
    out_ref[col_me, row_me] = total
    mine = out_ref.at[col_me, row_me]
    for step in range(1, rows):
        peer = lax.rem(row_me + step, rows)
        slot = step - 1
        second.append(send(mine, mine, "row", peer, send_two.at[slot], recv_two.at[slot]))
    for copy in second:
        copy.wait_recv()
    mine = out_ref.at[col_me]
    for step in range(1, cols):
        peer = lax.rem(col_me + step, cols)
        slot = step - 1
        third.append(send(mine, mine, "col", peer, send_col.at[slot], recv_col.at[slot]))
    for copy in first + second:
        copy.wait_send()
    for copy in third:
        copy.wait()


def share(x, collective_id):
    rows, cols = lax.axis_size("row"), lax.axis_size("col")
    size, width = x.shape
    pieces = (cols, rows, size // (rows * cols), width)
    out = pl.pallas_call(
        functools.partial(share_kernel, rows, cols),
        out_shape=jax.ShapeDtypeStruct(pieces, x.dtype),
        in_specs=[pl.BlockSpec(memory_space=pltpu.VMEM)],
        out_specs=pl.BlockSpec(memory_space=pltpu.VMEM),
        scratch_shapes=[pltpu.VMEM((rows - 1,) + pieces[2:], x.dtype)]
        + [pltpu.SemaphoreType.DMA((rows - 1,))] * 4
        + [pltpu.SemaphoreType.DMA((cols - 1,))] * 2,
        compiler_params=pltpu.CompilerParams(
            collective_id=collective_id, has_side_effects=True, vmem_limit_bytes=BIG
        ),
    )(x.reshape(pieces))
    return out.reshape(size, width)


def all_gather_kernel(axis, count, x_ref, out_ref, send_sem, recv_sem):
    me = greet(axis, count)
    copies = []
    for step in range(1, count):
        copies.append(
            pltpu.make_async_remote_copy(
                src_ref=x_ref,
                dst_ref=out_ref.at[me],
                send_sem=send_sem.at[step - 1],
                recv_sem=recv_sem.at[step - 1],
                device_id={axis: lax.rem(me + step, count)},
                device_id_type=MESH,
            )
        )
        copies[-1].start()
    out_ref[me] = x_ref[...]
    for copy in copies:
        copy.wait()


def all_gather(x, axis, collective_id):
    count = lax.axis_size(axis)
    return pl.pallas_call(
        functools.partial(all_gather_kernel, axis, count),
        out_shape=jax.ShapeDtypeStruct((count,) + x.shape, x.dtype),
        in_specs=[pl.BlockSpec(memory_space=pltpu.VMEM)],
        out_specs=pl.BlockSpec(memory_space=pltpu.VMEM),
        scratch_shapes=[pltpu.SemaphoreType.DMA((count - 1,))] * 2,
        compiler_params=pltpu.CompilerParams(
            collective_id=collective_id, has_side_effects=True, vmem_limit_bytes=BIG
        ),
    )(x)


def flatten_kernel(tiles, x_ref, out_ref):
    rows, size = out_ref.shape[0], x_ref.shape[1]
    for tile in range(tiles):
        out_ref[:, tile * size : (tile + 1) * size] = x_ref[pl.ds(tile, rows, stride=tiles), :]


def flatten(matrix_tiles):
    block_rows, _, tile_size, block_cols, _, width = matrix_tiles.shape
    flat = matrix_tiles.reshape(block_rows * tile_size * block_cols, width)
    return pl.pallas_call(
        functools.partial(flatten_kernel, block_cols),
        grid=(block_rows,),
        in_specs=[pl.BlockSpec((tile_size * block_cols, width), lambda i: (i, 0))],
        out_specs=pl.BlockSpec((tile_size, block_cols * width), lambda i: (i, 0)),
        out_shape=jax.ShapeDtypeStruct(
            (block_rows * tile_size, block_cols * width), matrix_tiles.dtype
        ),
        compiler_params=pltpu.CompilerParams(vmem_limit_bytes=BIG),
    )(flat)


def split(value):
    high = value.astype(jnp.bfloat16)
    return high, (value - high.astype(jnp.float32)).astype(jnp.bfloat16)


def update_kernel(tiles, flat, x_ref, left_ref, right_ref, out_ref, high_ref, low_ref):
    rows = x_ref.shape[0]
    size = x_ref.shape[1] // tiles

    @pl.when(pl.program_id(0) == 0)
    def _():
        high_ref[...], low_ref[...] = split(right_ref[...])

    left_high, left_low = split(left_ref[...])
    group = 2 if tiles % 2 == 0 else 1
    for first in range(0, tiles, group):
        part = slice(first * size, (first + group) * size)
        right_high, right_low = high_ref[part, :], low_ref[part, :]
        dot = lambda a, b: lax.dot_general(
            a, b, (((1,), (1,)), ((), ())), preferred_element_type=jnp.float32
        )
        product = dot(left_high, right_high) + (
            dot(left_high, right_low) + dot(left_low, right_high)
        )
        value = x_ref[:, part] - product
        if not flat:
            out_ref[:, part] = value
            continue
        for offset in range(group):
            out_ref[pl.ds(first + offset, rows, stride=tiles), :] = value[
                :, offset * size : (offset + 1) * size
            ]


def update(matrix, left, right, tiles, flat):
    row_count, col_count = matrix.shape
    size = col_count // tiles
    blocks = row_count // size
    rows = size * (2 if blocks % 2 == 0 else 1)
    depth = left.shape[1]
    wide = pl.BlockSpec((rows, col_count), lambda i: (i, 0))
    return pl.pallas_call(
        functools.partial(update_kernel, tiles, flat),
        grid=(row_count // rows,),
        in_specs=[
            wide,
            pl.BlockSpec((rows, depth), lambda i: (i, 0)),
            pl.BlockSpec((col_count, depth), lambda i: (0, 0), pipeline_mode=pl.Buffered(1)),
        ],
        out_specs=pl.BlockSpec((rows * tiles, size), lambda i: (i, 0)) if flat else wide,
        out_shape=jax.ShapeDtypeStruct(
            (row_count * tiles, size) if flat else matrix.shape, matrix.dtype
        ),
        scratch_shapes=[pltpu.VMEM((col_count, depth), jnp.bfloat16)] * 2,
        compiler_params=pltpu.CompilerParams(vmem_limit_bytes=BIG),
    )(matrix, left, right)


def mirror_order(pieces, block_rows, tile_size):
    stacked = jnp.stack(pieces, 0)
    stacked = stacked.reshape(len(pieces), block_rows, tile_size, stacked.shape[-1])
    return stacked.transpose(1, 0, 2, 3).reshape(-1, stacked.shape[-1])


def on_device(matrix_tiles):
    tile_shape = matrix_tiles.shape
    block_rows, _, tile_size, block_cols = tile_shape[:4]
    row_count = block_rows * tile_size
    col_count = block_cols * tile_size
    row_devices = lax.axis_size("row")
    col_devices = lax.axis_size("col")
    row_ratio = row_devices // col_devices
    row_index = lax.axis_index("row")
    col_index = lax.axis_index("col")

    def positions(count, devices, index):
        place = jnp.arange(count, dtype=jnp.int32)
        return (place // tile_size * devices + index) * tile_size + place % tile_size

    global_rows = positions(row_count, row_devices, row_index)
    global_cols = positions(col_count, col_devices, col_index)
    band_columns = jnp.arange(BAND, dtype=jnp.int32)
    panel_tiles = BAND // tile_size
    high = lax.Precision.HIGH

    def row_tiles(source, first):
        blocks = []
        for tile in range(first, first + panel_tiles):
            local_tile = tile // row_devices
            part = source[local_tile * tile_size : (local_tile + 1) * tile_size]
            blocks.append(jnp.where(row_index == tile % row_devices, part, 0.0))
        return jnp.concatenate(blocks, 0)

    matrix = flatten(matrix_tiles)
    held = -(-PANELS * panel_tiles // col_devices)
    gathered = all_gather(matrix[:, : held * tile_size], "col", 0)
    panels_rows, panels_cols = [], []
    for panel_index in range(PANELS):
        pieces = []
        for tile in range(panel_index * panel_tiles, (panel_index + 1) * panel_tiles):
            local_tile = tile // col_devices
            pieces.append(
                gathered[
                    tile % col_devices, :, local_tile * tile_size : (local_tile + 1) * tile_size
                ]
            )
        panels_rows.append(jnp.concatenate(pieces, 1))
        sent = row_tiles(matrix, panel_index * panel_tiles)
        if panels_cols:
            sent, panels_cols[-1] = lax.optimization_barrier((sent, panels_cols[-1]))
        panels_cols.append(lax.psum(sent, "row"))

    lefts, rights = [], []
    for panel_index in range(PANELS):
        below_start = (panel_index + 1) * BAND
        last = panel_index == PANELS - 1
        panel_rows = jnp.where((global_rows >= below_start)[:, None], panels_rows[panel_index], 0.0)
        stacked = jnp.concatenate(
            [
                multiply(panel_rows, panel_rows, 0, 0),
                row_tiles(panel_rows, below_start // tile_size),
            ],
            0,
        )
        stacked = share(stacked, 1)
        inverse, shifted, transform, signs = factors(stacked[:BAND], stacked[BAND:])

        def reflectors(panel, places):
            on_sign = (places[:, None] - below_start == band_columns[None, :]).astype(jnp.float32)
            return multiply(panel, inverse, 1, 1) - on_sign * signs

        vec_rows = reflectors(panel_rows, global_rows)
        panel_cols = jnp.where((global_cols >= below_start)[:, None], panels_cols[panel_index].T, 0.0)
        vec_cols = reflectors(panel_cols, global_cols)
        partial = multiply(matrix, vec_cols, precision=high)
        if lefts:
            left, right = jnp.concatenate(lefts, 1), jnp.concatenate(rights, 1)
            partial = partial - multiply(
                left, multiply(right, vec_cols, 0, 0, precision=high), precision=high
            )
        applied = multiply(all_reduce(partial, "col", 2), transform)
        moved = applied
        if not last:
            moved, panels_cols[panel_index + 1] = lax.optimization_barrier(
                (applied, panels_cols[panel_index + 1])
            )
        pieces = []
        for part_index in range(row_ratio):
            mine = row_index == col_index + col_devices * part_index
            pieces.append(lax.psum(jnp.where(mine, moved, 0.0), "row"))
        applied_cols = mirror_order(pieces, block_rows, tile_size)
        inner_part = multiply(vec_rows, applied, 0, 0)
        if last:
            inner = share(inner_part, 3)
        else:
            stacked = jnp.concatenate([inner_part, row_tiles(applied, below_start // tile_size)], 0)
            stacked = share(stacked, 1)
            inner = stacked[:BAND]
        half_inner = 0.5 * multiply(transform, inner, 0, 0)
        update_rows = applied - multiply(vec_rows, half_inner)
        update_cols = applied_cols - multiply(vec_cols, half_inner)
        lefts += [vec_rows, update_rows]
        rights += [update_cols, vec_cols]
        if not last:
            update_next = stacked[BAND:] - multiply(shifted, half_inner)
            panels_rows[panel_index + 1] = (
                panels_rows[panel_index + 1]
                - multiply(vec_rows, update_next, 1, 1)
                - multiply(update_rows, shifted, 1, 1)
            )
            panels_cols[panel_index + 1] = (
                panels_cols[panel_index + 1]
                - multiply(update_next, vec_cols, 1, 1)
                - multiply(shifted, update_cols, 1, 1)
            )
    early = len(lefts) - 2
    order = [index for index in range(len(lefts)) if index != early]
    matrix = update(
        matrix,
        jnp.concatenate([lefts[index] for index in order], 1),
        jnp.concatenate([rights[index] for index in order], 1),
        block_cols,
        False,
    )
    return update(matrix, lefts[early], rights[early], block_cols, True).reshape(tile_shape)


def solution(mesh):
    return jax.shard_map(
        on_device,
        mesh=mesh,
        in_specs=(P(None, "row", None, None, "col", None),),
        out_specs=P(None, "row", None, None, "col", None),
        check_vma=False,
    )
```

profile of v0, /device:TPU:0, one launch (start us, length us, event | category | flops | bytes accessed | tf_op | source)
XLA Modules:
  0.0 511.8 jit_solution(15272373750571349909)
XLA Ops:
  6.5 12.6 %shard_map.17.x_ref = f32[1280,2560]{1,0:T(8,128)} custom-call(f32[25600,128]{1,0:T(8,128)} %bitcast.94), custom_call_target="tpu_custom_call" | custom-call | tf_op jit(solution)/shard_map/pallas_call | solution.py:301
  19.1 2.7 slice_select_fusion.1
  24.1 2.0 slice.90.x_ref
  26.2 35.7 %shard_map.18 = f32[4,1280,128]{2,1,0:T(8,128)} custom-call(f32[1280,128]{1,0:T(8,128)} %slice.90.x_ref), custom_call_target="tpu_custom_call" | custom-call | tf_op jit(solution)/shard_map/pallas_call | solution.py:280
  61.9 2.7 slice_bitcast_fusion.1
  64.8 2.2 fusion.40
  67.9 25.3 %shard_map.19 = f32[4,8,16,256]{3,2,1,0:T(8,128)} custom-call(f32[4,8,16,256]{3,2,1,0:T(8,128)} %bitcast.105), custom_call_target="tpu_custom_call" | custom-call | tf_op jit(solution)/shard_map/pallas_call | solution.py:243
  93.3 1.9 fusion.39
  95.2 35.3 %shard_map.20 = (f32[256,256]{1,0:T(8,128)}, f32[256,256]{1,0:T(8,128)}, f32[256,256]{1,0:T(8,128)}, f32[1,256]{1,0:T(1,128)}) custom-call(f32[256,256]{1,0:T(8,128)} %bitcast.111, f32[256,256]{1,0:T(8,128)} %bitcast.110), custom_call_target="tpu_custom_call" | custom-call | tf_op jit(solution)/shard_map/pallas_call | solution.py:100
  132.3 3.4 convolution_subtract_fusion.12
  135.7 1.7 pad_maximum_fusion.2
  138.4 6.4 %convolution_subtract_fusion.5 = f32[2560,256]{1,0:T(8,128)S(1)} fusion(f32[256,256]{1,0:T(8,128)S(1)} %copy-done.26, f32[256,2560]{1,0:T(8,128)} %all-reduce.7.cloned.1.call-done, f32[256]{0:T(256)} %bitcast.117, s32[2560]{0:T(1024)} %broadcast_add_fusion.1, pred[2560]{0:T(1024)(128)(4,1)} %broadcast_compare_fusion.1), kind=kOutput, calls=%fused_computation.11 | convolution fusion | flops 2015887360 | bytes 5518848 | tf_op jit(solution)/shard_map/dot_general | solution.py:107
  144.8 15.0 %convolution_bitcast_fusion.1 = f32[1280,256]{0,1:T(8,128)} fusion(f32[2560,256]{1,0:T(8,128)S(1)} %convolution_subtract_fusion.5, f32[1280,2560]{1,0:T(8,128)} %shard_map.17.x_ref), kind=kOutput, calls=%fused_computation.22 | convolution fusion | flops 5033164800 | bytes 17039360 | tf_op jit(solution)/shard_map/dot_general | solution.py:107
  159.8 2.8 copy.21
  162.6 35.6 %shard_map.21 = f32[4,320,256]{2,1,0:T(8,128)} custom-call(f32[4,320,256]{2,1,0:T(8,128)} %bitcast.99), custom_call_target="tpu_custom_call" | custom-call | tf_op jit(solution)/shard_map/pallas_call | solution.py:172
  198.2 3.7 fusion.41
  201.9 2.8 copy.23
  204.7 3.9 fusion.42
  210.4 22.5 %shard_map.22 = f32[4,8,16,256]{3,2,1,0:T(8,128)} custom-call(f32[4,8,16,256]{3,2,1,0:T(8,128)} %bitcast.106), custom_call_target="tpu_custom_call" | custom-call | tf_op jit(solution)/shard_map/pallas_call | solution.py:243
  241.8 2.3 fusion.43
  244.1 3.0 copy.25
  247.1 2.9 broadcast_select_fusion.3
  251.9 23.8 %shard_map.23 = f32[4,8,16,256]{3,2,1,0:T(8,128)} custom-call(f32[4,8,16,256]{3,2,1,0:T(8,128)} %bitcast.107), custom_call_target="tpu_custom_call" | custom-call | tf_op jit(solution)/shard_map/pallas_call | solution.py:243
  275.7 1.9 fusion.37
  277.6 25.8 %shard_map.24 = (f32[256,256]{1,0:T(8,128)}, f32[256,256]{1,0:T(8,128)}, f32[256,256]{1,0:T(8,128)}, f32[1,256]{1,0:T(1,128)}) custom-call(f32[256,256]{1,0:T(8,128)} %bitcast.113, f32[256,256]{1,0:T(8,128)} %bitcast.112), custom_call_target="tpu_custom_call" | custom-call | tf_op jit(solution)/shard_map/pallas_call | solution.py:100
  303.5 3.9 convolution_subtract_fusion.7.left_ref
  307.4 4.0 convolution_subtract_fusion.4
  311.4 11.1 %all-reduce.13.cloned.1.call-done = (f32[1,10,128,256]{3,2,1,0:T(8,128)}, f32[1,10,128,256]{3,2,1,0:T(8,128)}) async-done(((f32[1,10,128,256]{3,2,1,0:T(8,128)}, f32[1,10,128,256]{3,2,1,0:T(8,128)}), (f32[1,10,128,256]{3,2,1,0:T(8,128)}, f32[1,10,128,256]{3,2,1,0:T(8,128)})) %all-reduce.13.cloned.1.call-update) | async-done | bytes 2621456 | tf_op jit(solution)/shard_map/psum | solution.py:462
  322.5 2.0 maximum_bitcast_fusion
  324.7 2.3 convolution_subtract_fusion.3
  327.1 2.7 fusion.4
  329.9 5.1 %convolution_subtract_fusion.1 = f32[2560,256]{1,0:T(8,128)S(1)} fusion(f32[256,2560]{1,0:T(8,128)S(1)} %fusion.4, f32[256,256]{1,0:T(8,128)S(1)} %copy-done.27, f32[256]{0:T(256)S(1)} %bitcast.119, s32[2560]{0:T(1024)S(1)} %broadcast_add_fusion), kind=kOutput, calls=%fused_computation.6 | convolution fusion | flops 2015232000 | bytes 5516288 | tf_op jit(solution)/shard_map/dot_general | solution.py:107
  335.1 4.4 fusion
  339.6 11.1 %convolution_bitcast_fusion = f32[1280,256]{0,1:T(8,128)S(1)} fusion(f32[2560,256]{1,0:T(8,128)S(1)} %convolution_subtract_fusion.1, f32[1280,2560]{1,0:T(8,128)S(1)} %bitcast.93), kind=kOutput, calls=%fused_computation.21 | convolution fusion | flops 5033164800 | bytes 17039360 | tf_op jit(solution)/shard_map/dot_general | solution.py:107
  350.7 2.4 convolution_subtract_fusion.8
  353.2 2.8 copy.31
  356.0 33.9 %shard_map.25 = f32[4,320,256]{2,1,0:T(8,128)} custom-call(f32[4,320,256]{2,1,0:T(8,128)} %bitcast.101), custom_call_target="tpu_custom_call" | custom-call | tf_op jit(solution)/shard_map/pallas_call | solution.py:172
  389.9 4.1 broadcast_select_fusion.1
  394.0 3.0 fusion.44
  397.0 18.3 %shard_map.26 = f32[4,8,8,256]{3,2,1,0:T(8,128)} custom-call(f32[4,8,8,256]{3,2,1,0:T(8,128)} %bitcast.115), custom_call_target="tpu_custom_call" | custom-call | tf_op jit(solution)/shard_map/pallas_call | solution.py:243
  417.1 3.1 convolution_subtract_fusion.6
  420.3 2.3 pad_maximum_fusion.1.left_ref
  424.3 3.4 pad_maximum_fusion.right_ref
  427.7 23.7 %shard_map.27.x_ref = f32[1280,2560]{1,0:T(8,128)} custom-call(f32[1280,2560]{1,0:T(8,128)} %shard_map.17.x_ref, f32[1280,768]{1,0:T(8,128)} %pad_maximum_fusion.1.left_ref, f32[2560,768]{1,0:T(8,128)} %pad_maximum_fusion.right_ref), custom_call_target="tpu_custom_call" | custom-call | tf_op jit(solution)/shard_map/pallas_call | solution.py:354
  451.3 31.7 %all-reduce.11.cloned.1.call-done = (f32[1,10,128,256]{3,2,0,1:T(8,128)}, f32[1,10,128,256]{3,2,0,1:T(8,128)}) async-done(((f32[1,10,128,256]{3,2,0,1:T(8,128)}, f32[1,10,128,256]{3,2,0,1:T(8,128)}), (f32[1,10,128,256]{3,2,0,1:T(8,128)}, f32[1,10,128,256]{3,2,0,1:T(8,128)})) %all-reduce.11.cloned.1.call-update) | async-done | bytes 2621456 | tf_op jit(solution)/shard_map/psum | solution.py:462
  483.1 2.1 pad_maximum_fusion.4
  485.6 3.7 convolution_subtract_fusion.right_ref
  489.3 15.5 %shard_map.28 = f32[25600,128]{1,0:T(8,128)} custom-call(f32[1280,2560]{1,0:T(8,128)} %shard_map.27.x_ref, f32[1280,256]{1,0:T(8,128)} %convolution_subtract_fusion.7.left_ref, f32[2560,256]{1,0:T(8,128)} %convolution_subtract_fusion.right_ref), custom_call_target="tpu_custom_call" | custom-call | tf_op jit(solution)/shard_map/pallas_call | solution.py:354
  (103 shorter events, 22.7 us)
Async XLA Ops:
  6.5 130.9 %all-reduce.7.cloned.1.call-start = ((), (), s32[]{:S(2)}) async-start(), calls=%async_computation | async-start | bytes 5242880 | tf_op jit(solution)/shard_map/psum | solution.py:423
  23.5 220.6 %all-reduce.9.cloned.1.call-start = ((), (), s32[]{:S(2)}) async-start(), calls=%async_computation.1 | async-start | bytes 5242880 | tf_op jit(solution)/shard_map/psum | solution.py:423
  132.3 3.4 copy-start.16
  137.5 0.9 copy-start.26
  137.5 185.0 %all-reduce.13.cloned.1.call-start = ((), (), s32[]{:S(2)}) async-start(), calls=%async_computation.3 | async-start | bytes 5242880 | tf_op jit(solution)/shard_map/psum | solution.py:462
  162.6 35.6 %copy-start.25 = (f32[256,256]{1,0:T(8,128)S(1)}, f32[256,256]{1,0:T(8,128)}, u32[]{:S(2)}) copy-start(f32[256,256]{1,0:T(8,128)} %get-tuple-element.19) | copy-start | bytes 786436
  210.4 25.3 %copy-start.21 = (f32[256,256]{1,0:T(8,128)S(1)}, f32[256,256]{1,0:T(8,128)}, u32[]{:S(2)}) copy-start(f32[256,256]{1,0:T(8,128)} %get-tuple-element.22) | copy-start | bytes 786436
  232.9 3.9 copy-start
  232.9 3.9 copy-start.18
  236.1 0.7 copy-start.19
  236.8 1.3 copy-start.15
  238.1 1.2 copy-start.29
  239.4 1.3 copy-start.10
  240.7 1.1 copy-start.8
  250.1 233.0 %all-reduce.11.cloned.1.call-start = ((), (), s32[]{:S(2)}) async-start(), calls=%async_computation.2 | async-start | bytes 5242880 | tf_op jit(solution)/shard_map/psum | solution.py:462
  251.9 51.5 %copy-start.28 = (s32[1280]{0:T(1024)S(1)}, s32[1280]{0:T(1024)}, u32[]{:S(2)}) copy-start(s32[1280]{0:T(1024)} %get-tuple-element.56) | copy-start | bytes 15364
  303.5 3.9 copy-start.17
  303.5 3.9 copy-start.20
  324.5 2.6 copy-start.14
  324.5 2.6 copy-start.22
  324.7 14.8 %slice-start = ((s8[13107200]{0:T(1024)(128)(4,1)}), s8[4194304]{0:T(1024)(128)(4,1)S(1)}, s32[]{:S(2)}) async-start(s8[13107200]{0:T(1024)(128)(4,1)} %bitcast.92), calls=%async_computation.4 | async-start | bytes 8388608
  324.7 14.8 %slice-start.1 = ((s8[13107200]{0:T(1024)(128)(4,1)}), s8[4194304]{0:T(1024)(128)(4,1)S(1)}, s32[]{:S(2)}) async-start(s8[13107200]{0:T(1024)(128)(4,1)} %bitcast.92), calls=%async_computation.5 | async-start | bytes 8388608
  327.1 7.9 %copy-start.6 = (f32[2560,256]{1,0:T(8,128)}, f32[2560,256]{1,0:T(8,128)S(1)}, u32[]{:S(2)}) copy-start(f32[2560,256]{1,0:T(8,128)S(1)} %convolution_subtract_fusion.3) | copy-start | bytes 7864324
  327.1 2.8 copy-start.27
  327.1 2.8 copy-start.30
  327.1 12.4 %slice-start.2 = ((s8[13107200]{0:T(1024)(128)(4,1)}), s8[4194304]{0:T(1024)(128)(4,1)S(1)}, s32[]{:S(2)}) async-start(s8[13107200]{0:T(1024)(128)(4,1)} %bitcast.92), calls=%async_computation.6 | async-start | bytes 8388608
  335.0 4.5 copy-start.3
  335.0 4.5 slice-start.3
  339.6 11.2 %copy-start.1 = (f32[1280,256]{1,0:T(8,128)S(1)}, f32[1280,256]{1,0:T(8,128)}, u32[]{:S(2)}) copy-start(f32[1280,256]{1,0:T(8,128)} %convolution_subtract_fusion.12) | copy-start | bytes 3932164
  339.6 11.2 %copy-start.11 = (f32[1280,256]{1,0:T(8,128)S(1)}, f32[1280,256]{1,0:T(8,128)}, u32[]{:S(2)}) copy-start(f32[1280,256]{1,0:T(8,128)} %copy-done.10) | copy-start | bytes 3932164
  355.9 34.0 %copy-start.23 = (f32[256,256]{1,0:T(8,128)S(1)}, f32[256,256]{1,0:T(8,128)}, u32[]{:S(2)}) copy-start(f32[256,256]{1,0:T(8,128)} %get-tuple-element.26) | copy-start | bytes 786436
  389.9 4.1 copy-start.9
  394.0 3.0 copy-start.13
  415.3 1.0 copy-start.24
  417.1 3.1 copy-start.2
  417.1 3.1 copy-start.12
  420.3 3.0 copy-start.4
  420.3 4.0 copy-start.7
  483.1 2.5 copy-start.5
Sparse Core Ops, SparseCore 0:
  23.6 77.3 all-reduce.6
  137.6 68.9 all-reduce.8
  250.2 72.2 all-reduce.12
  415.5 67.5 all-reduce.10
where the time goes:
time: 522 us; the launch traced here: 512 us
  Pallas kernels  308 us (59%)
  matrix products  93.6 us (18%)
  waiting for transfers between devices  43 us (8%)
  local copies, waits for them, and re-layouts  27.1 us (5%)
  other arithmetic  25.8 us (5%)
  between operations  14.2 us (3%)
    dot_general x25, matrix products, multiply(): lax.dot_general(first, second, (((first_dim,), (second_dim,)), ((), ())),...  93.6 us
    pallas_call x4, Pallas kernels, share(): pl.pallas_call(functools.partial(share_kernel, rows, cols), out_shape=jax...  90 us
    pallas_call x2, Pallas kernels, all_reduce(): pl.pallas_call(functools.partial(all_reduce_kernel, axis, count), out_sha...  69.5 us
    pallas_call x2, Pallas kernels, factors(): pl.pallas_call(factor_kernel, out_shape=(square, square, square, jax.Shap...  61.2 us
    psum x2, waiting for transfers between devices, on_device(): pieces.append(lax.psum(jnp.where(mine, moved, 0.0), 'row'))  42.9 us
    pallas_call x2, Pallas kernels, update(): pl.pallas_call(functools.partial(update_kernel, tiles, flat), grid=(row_c...  39.1 us
    pallas_call x1, Pallas kernels, all_gather(): pl.pallas_call(functools.partial(all_gather_kernel, axis, count), out_sha...  35.7 us
    pallas_call x1, Pallas kernels, flatten(): pl.pallas_call(functools.partial(flatten_kernel, block_cols), grid=(block...  12.6 us
  transfers between devices with their start and end apart: 4, of which 2 were waited for; matrix products, arithmetic and copies ran while one was open for 16% of the time, Pallas kernels for 45%

commit v1 on v0

v1 whole, which is shorter than its diff:
```python
import functools

import jax
import jax.numpy as jnp
from jax import lax
from jax.experimental import pallas as pl
from jax.experimental.pallas import tpu as pltpu
from jax.sharding import PartitionSpec as P

BAND = 256
PANELS = 2
BIG = 60 * 1024 * 1024
SMALL = 32 * 1024 * 1024
MESH = pl.DeviceIdType.MESH

HI = lax.Precision.HIGHEST
def mm(a, b, ca, cb):
    return lax.dot_general(a, b, (((ca,), (cb,)), ((), ())), precision=HI, preferred_element_type=jnp.float32)

def base_inverse(block, hook):
    size = block.shape[0]
    wide = (8, 2 * size)
    group = 8
    places = lax.broadcasted_iota(jnp.int32, wide, 0)
    cols = lax.broadcasted_iota(jnp.int32, wide, 1)
    work = []
    for k in range(size // 8):
        unit = jnp.where(places + 8 * k == cols, 1.0, 0.0)[:, :size]
        work.append(jnp.concatenate([block[8 * k : 8 * k + 8], unit], 1))
    for start in range(0, size, group):
        own, offset = divmod(start, 8)
        rows = [jnp.broadcast_to(work[own][offset + i : offset + i + 1], wide) for i in range(group)]
        pivot = [
            [jnp.broadcast_to(rows[i][:, start + j : start + j + 1], wide) for j in range(group)]
            for i in range(group)
        ]
        first = own if offset + group < 8 else own + 1
        columns = [
            [jnp.broadcast_to(work[k][:, start + i : start + i + 1], wide) for i in range(group)]
            for k in range(first, len(work))
        ]
        scaled = []
        for i in range(group):
            inverse = 1.0 / pivot[i][i]
            scaled.append(rows[i] * inverse)
            for j in range(i + 1, group):
                ratio = pivot[i][j] * inverse
                for l in range(j, group):
                    pivot[j][l] = pivot[j][l] - ratio * pivot[i][l]
                rows[j] = rows[j] - ratio * rows[i]
                for column in columns:
                    column[j] = column[j] - ratio * column[i]
        for k, column in zip(range(first, len(work)), columns):
            change = column[0] * scaled[0]
            for i in range(1, group):
                change = change + column[i] * scaled[i]
            if k == own:
                change = jnp.where(places >= offset + group, change, 0.0)
            work[k] = work[k] - change
        for i in range(group):
            work[own] = jnp.where(places == offset + i, rows[i], work[own])
        hook()
    result = []
    for k, value in enumerate(work):
        pivots = jnp.sum(jnp.where(places + 8 * k == cols, value, 0.0), axis=1, keepdims=True)
        result.append(value[:, size:] * (1.0 / jnp.sqrt(pivots)))
    return jnp.concatenate(result, 0)


def factor_inverse(matrix, base, hook):
    size = matrix.shape[0]
    if size <= base:
        return base_inverse(matrix, hook)
    half = size // 2
    first = factor_inverse(matrix[:half, :half], base, hook)
    lower = mm(matrix[half:, :half], first, 1, 1)
    second = factor_inverse(matrix[half:, half:] - mm(lower, lower, 1, 1), base, hook)
    corner = -mm(second, mm(lower, first, 1, 0), 1, 0)
    top = jnp.concatenate([first, jnp.zeros_like(first)], 1)
    return jnp.concatenate([top, jnp.concatenate([corner, second], 1)], 0)

def factor_body(gram, top, inverse_ref, shifted_ref, transform_ref, sign_ref, hook):
    size = gram.shape[0]
    inverse = factor_inverse(gram, 64, hook)
    inverse_ref[...] = inverse
    basis = mm(top, inverse, 0, 1)
    rows = lax.broadcasted_iota(jnp.int32, (size, size), 0)
    cols = lax.broadcasted_iota(jnp.int32, (size, size), 1)
    on_diagonal = rows == cols
    sign_square = jnp.where(on_diagonal, jnp.where(basis >= 0, -1.0, 1.0), 0.0)
    shifted = basis - sign_square
    shifted_ref[...] = shifted
    outer = factor_inverse(mm(shifted, shifted, 0, 0), 64, hook)
    sign_column = jnp.sum(sign_square, axis=1, keepdims=True)
    transform_ref[...] = -sign_column * mm(mm(shifted, outer, 1, 1), outer, 1, 0)
    sign_ref[...] = jnp.sum(sign_square, axis=0, keepdims=True)


def multiply(first, second, first_dim=1, second_dim=0, precision=HI):
    return lax.dot_general(
        first,
        second,
        (((first_dim,), (second_dim,)), ((), ())),
        precision=precision,
        preferred_element_type=jnp.float32,
    )


def remote(source, target, send_sem, recv_sem, row, col):
    return pltpu.make_async_remote_copy(
        src_ref=source,
        dst_ref=target,
        send_sem=send_sem,
        recv_sem=recv_sem,
        device_id={"row": row, "col": col},
        device_id_type=MESH,
    )


class Place:
    def __init__(self, rows, cols):
        self.rows, self.cols, self.planes = rows, cols, rows // 2
        row = lax.axis_index("row")
        self.col = lax.axis_index("col")
        self.plane = row // 2
        self.core = row % 2
        self.row = row
        self.other = 2 * self.plane + (1 - self.core)
        self.me = self.core * cols + self.col

    def peers(self):
        found = []
        for core_step in range(2):
            for col_step in range(self.cols):
                if core_step or col_step:
                    core = lax.rem(self.core + core_step, 2)
                    col = lax.rem(self.col + col_step, self.cols)
                    found.append((2 * self.plane + core, col, core * self.cols + col))
        return found

    def greet(self, line=True):
        barrier = pltpu.get_barrier_semaphore()
        count = 0
        for row, col, _ in self.peers():
            pl.semaphore_signal(
                barrier, inc=1, device_id={"row": row, "col": col}, device_id_type=MESH
            )
            count += 1
        for step in range(1, self.planes) if line else ():
            row = lax.rem(self.row + 2 * step, self.rows)
            pl.semaphore_signal(
                barrier, inc=1, device_id={"row": row, "col": self.col}, device_id_type=MESH
            )
            count += 1
        pl.semaphore_wait(barrier, count)


def plane_scatter(place, x_ref, parts, out_ref, send_sem, recv_sem):
    copies = []
    for slot, (row, col, piece) in enumerate(place.peers()):
        copies.append(
            remote(
                x_ref.at[piece], parts.at[slot], send_sem.at[slot], recv_sem.at[slot], row, col
            )
        )
        copies[-1].start()
    total = x_ref[place.me]
    for slot, copy in enumerate(copies):
        copy.wait_recv()
        total = total + parts[slot]
    out_ref[place.me] = total
    for copy in copies:
        copy.wait_send()


def plane_gather(place, out_ref, send_sem, recv_sem):
    mine = out_ref.at[place.me]
    copies = []
    for slot, (row, col, _) in enumerate(place.peers()):
        copies.append(remote(mine, mine, send_sem.at[slot], recv_sem.at[slot], row, col))
        copies[-1].start()
    return copies


def plane_kernel(rows, cols, x_ref, out_ref, parts, send_one, recv_one, send_two, recv_two):
    place = Place(rows, cols)
    place.greet(False)
    plane_scatter(place, x_ref, parts, out_ref, send_one, recv_one)
    for copy in plane_gather(place, out_ref, send_two, recv_two):
        copy.wait()


def plane_sum(x, collective_id):
    rows, cols = lax.axis_size("row"), lax.axis_size("col")
    size, width = x.shape
    count = 2 * cols
    pieces = (count, size // count, width)
    vmem = pl.BlockSpec(memory_space=pltpu.VMEM)
    out = pl.pallas_call(
        functools.partial(plane_kernel, rows, cols),
        out_shape=jax.ShapeDtypeStruct(pieces, x.dtype),
        in_specs=[vmem],
        out_specs=vmem,
        scratch_shapes=[pltpu.VMEM((count - 1,) + pieces[1:], x.dtype)]
        + [pltpu.SemaphoreType.DMA((count - 1,))] * 4,
        compiler_params=pltpu.CompilerParams(
            collective_id=collective_id, has_side_effects=True, vmem_limit_bytes=SMALL
        ),
    )(x.reshape(pieces))
    return out.reshape(size, width)


class Chain:
    def __init__(self, place, source, x_ref, panel_ref, sems):
        self.place, self.source, self.x_ref, self.ref = place, source, x_ref, panel_ref
        self.load, self.sends, self.recv, self.share_send, self.share_recv = sems
        self.tile = x_ref.shape[-1]
        self.tiles = x_ref.shape[1]
        self.chunks = self.recv.shape[0]
        self.width = panel_ref.shape[1] // self.chunks
        self.at_source = place.plane == source

    def loads(self):
        start = pl.multiple_of(self.place.core * self.tile, self.tile)
        for tile in range(self.tiles):
            yield pltpu.make_async_copy(
                self.x_ref.at[pl.ds(0, self.tile), tile, 0, :],
                self.ref.at[pl.ds(start, self.tile), pl.ds(tile * self.tile, self.tile)],
                self.load.at[tile],
            )

    def part(self, chunk):
        start = pl.multiple_of(self.place.core * self.tile, self.tile)
        return self.ref.at[pl.ds(start, self.tile), pl.ds(chunk * self.width, self.width)]

    def hop(self, chunk, step, sem):
        part = self.part(chunk)
        row = lax.rem(self.place.row + 2 * step + self.place.rows, self.place.rows)
        return remote(part, part, self.sends.at[sem, chunk], self.recv.at[chunk], row, self.place.col)

    def shared(self, chunk):
        part = self.part(chunk)
        return remote(
            part,
            part,
            self.share_send.at[chunk],
            self.share_recv.at[chunk],
            self.place.other,
            self.place.col,
        )

    def start(self):
        @pl.when(self.at_source)
        def _():
            for copy in self.loads():
                copy.start()

    def send(self):
        @pl.when(self.at_source)
        def _():
            for copy in self.loads():
                copy.wait()
            for chunk in range(self.chunks):
                self.shared(chunk).start()
                if self.source < self.place.planes - 1:
                    self.hop(chunk, 1, 0).start()
                if self.source > 0:
                    self.hop(chunk, -1, 1).start()

    def step(self, chunk):
        place = self.place
        for step, sem, away, more in (
            (1, 0, place.plane > self.source, place.plane < place.planes - 1),
            (-1, 1, place.plane < self.source, place.plane > 0),
        ):
            if step < 0 and self.source == 0 or step > 0 and self.source == place.planes - 1:
                continue

            @pl.when(away)
            def _():
                self.hop(chunk, step, sem).wait_recv()

                @pl.when(more)
                def _():
                    self.hop(chunk, step, sem).start()

                self.shared(chunk).start()

    def finish(self):
        place = self.place
        for chunk in range(self.chunks):
            self.shared(chunk).wait()
        for step, sem, sent in (
            (1, 0, (place.plane >= self.source) & (place.plane < place.planes - 1)),
            (-1, 1, (place.plane <= self.source) & (place.plane > 0)),
        ):

            @pl.when(sent)
            def _():
                for chunk in range(self.chunks):
                    self.hop(chunk, step, sem).wait_send()

    @staticmethod
    def semaphores(tiles, chunks):
        dma = pltpu.SemaphoreType.DMA
        return [dma((tiles,)), dma((2, chunks)), dma((chunks,)), dma((chunks,)), dma((chunks,))]


def gram_kernel(rows, cols, below, x_ref, out_ref, later_ref, panel, stack, parts, *sems):
    place = Place(rows, cols)
    tile, tiles = x_ref.shape[-1], x_ref.shape[1]
    load, swap_send, swap_recv, send_one, recv_one, line_send, line_recv, send_two, recv_two = sems[:9]
    later = Chain(place, 1, x_ref, later_ref, sems[9:])
    first = place.plane == 0
    start = pl.multiple_of(place.core * tile, tile)
    own = panel.at[pl.ds(start, tile), :]

    def loads():
        for index in range(tiles):
            yield pltpu.make_async_copy(
                x_ref.at[pl.ds(0, tile), index, 0, :],
                panel.at[pl.ds(start, tile), pl.ds(index * tile, tile)],
                load.at[index],
            )

    @pl.when(first)
    def _():
        for copy in loads():
            copy.start()

    later.start()
    place.greet()
    later.send()
    line = [
        remote(
            out_ref.at[place.me],
            out_ref.at[place.me],
            line_send.at[step - 1],
            line_recv.at[0],
            lax.rem(place.row + 2 * step, rows),
            place.col,
        )
        for step in range(1, place.planes)
    ]

    @pl.when(first)
    def _():
        for copy in loads():
            copy.wait()
        swap = remote(own, own, swap_send.at[0], swap_recv.at[0], place.other, place.col)
        swap.start()
        swap.wait()
        width = tile * tiles // 2
        offset = place.core * width
        lanes = lax.broadcasted_iota(jnp.int32, (panel.shape[0], width), 1) + offset
        begin = below // tile
        limit = jnp.where(place.col < begin, tile, 0)
        value = panel[:, pl.ds(pl.multiple_of(offset, tile), width)]
        value = jnp.where(lanes >= limit, value, 0.0)
        gram = mm(value, value, 1, 1)
        size = stack.shape[1]
        per = panel.shape[0] // size
        for piece in range(per):
            stack[piece] = gram[piece * size : (piece + 1) * size]
        for index in range(panel.shape[0] // tile):
            number = begin + index
            local = number // cols
            mine = (place.col == number % cols) & (place.core == 0)
            block = jnp.where(mine, panel[:, local * tile : (local + 1) * tile], 0.0)
            for piece in range(per):
                stack[per + piece, :, index * tile : (index + 1) * tile] = block[
                    piece * size : (piece + 1) * size
                ]
        plane_scatter(place, stack, parts, out_ref, send_one, recv_one)
        for copy in line:
            copy.start()

    @pl.when(place.plane > 0)
    def _():
        line[0].wait_recv()

    gathers = plane_gather(place, out_ref, send_two, recv_two)
    for chunk in range(later.chunks):
        later.step(chunk)

    @pl.when(first)
    def _():
        for copy in line:
            copy.wait_send()

    for copy in gathers:
        copy.wait()
    later.finish()


CHUNK = 256


def gram(x4, collective_id):
    rows, cols = lax.axis_size("row"), lax.axis_size("col")
    _, tiles, _, tile = x4.shape
    width = tiles * tile
    count = 2 * cols
    pieces = (count, 2 * BAND // count, BAND)
    vmem = pl.BlockSpec(memory_space=pltpu.VMEM)
    dma = pltpu.SemaphoreType.DMA
    one, later = pl.pallas_call(
        functools.partial(gram_kernel, rows, cols, BAND),
        out_shape=(
            jax.ShapeDtypeStruct(pieces, x4.dtype),
            jax.ShapeDtypeStruct((BAND, width), x4.dtype),
        ),
        in_specs=[pl.BlockSpec(memory_space=pl.ANY)],
        out_specs=(vmem, vmem),
        scratch_shapes=[
            pltpu.VMEM((BAND, width), x4.dtype),
            pltpu.VMEM(pieces, x4.dtype),
            pltpu.VMEM((count - 1,) + pieces[1:], x4.dtype),
            dma((tiles,)),
            dma((1,)),
            dma((1,)),
            dma((count - 1,)),
            dma((count - 1,)),
            dma((rows // 2 - 1,)),
            dma((1,)),
            dma((count - 1,)),
            dma((count - 1,)),
        ]
        + Chain.semaphores(tiles, width // CHUNK),
        compiler_params=pltpu.CompilerParams(
            collective_id=collective_id, has_side_effects=True, vmem_limit_bytes=SMALL
        ),
    )(x4)
    return one.reshape(2 * BAND, BAND), later


def factor_move_kernel(
    rows, cols, stack_ref, x_ref, inverse_ref, shifted_ref, transform_ref, sign_ref, rows_ref, cols_ref, *sems
):
    place = Place(rows, cols)
    tile = x_ref.shape[-1]
    load, send_row, recv_row = sems[:3]
    chain = Chain(place, 0, x_ref, cols_ref, sems[3:])
    held = PANELS * BAND // tile
    panel_tiles = BAND // tile

    def spot(col):
        start = pl.multiple_of(lax.rem(col, panel_tiles) * tile, tile)
        return rows_ref.at[col // panel_tiles, :, pl.ds(start, tile)]

    has = place.col < held
    own = spot(lax.rem(place.col, held))
    fill = pltpu.make_async_copy(x_ref.at[:, 0, 0, :], own, load.at[0])

    @pl.when(has)
    def _():
        fill.start()

    chain.start()
    place.greet()
    chain.send()
    copies = [
        remote(
            own,
            own,
            send_row.at[step - 1],
            recv_row.at[lax.rem(place.col, held)],
            place.row,
            lax.rem(place.col + step, cols),
        )
        for step in range(1, cols)
    ]

    @pl.when(has)
    def _():
        fill.wait()
        for copy in copies:
            copy.start()

    count = [0]

    def hook():
        count[0] += 1
        chunk = count[0] // 2 - 2
        if count[0] % 2 == 0 and 0 <= chunk < chain.chunks:
            chain.step(chunk)

    size = inverse_ref.shape[0]
    factor_body(
        stack_ref[:size], stack_ref[size:], inverse_ref, shifted_ref, transform_ref, sign_ref, hook
    )

    @pl.when(has)
    def _():
        for copy in copies:
            copy.wait_send()

    for col in range(held):
        @pl.when(place.col != col)
        def _():
            remote(spot(col), spot(col), send_row.at[0], recv_row.at[col], place.row, place.col).wait_recv()

    chain.finish()


def factor_kernel(stack_ref, inverse_ref, shifted_ref, transform_ref, sign_ref):
    size = inverse_ref.shape[0]
    factor_body(
        stack_ref[:size],
        stack_ref[size:],
        inverse_ref,
        shifted_ref,
        transform_ref,
        sign_ref,
        lambda: None,
    )


def factor_shapes(size):
    square = jax.ShapeDtypeStruct((size, size), jnp.float32)
    return (square, square, square, jax.ShapeDtypeStruct((1, size), jnp.float32))


def factors(stack):
    return pl.pallas_call(
        factor_kernel,
        out_shape=factor_shapes(stack.shape[1]),
        compiler_params=pltpu.CompilerParams(vmem_limit_bytes=SMALL),
    )(stack)


def factors_move(stack, x4, collective_id):
    rows, cols = lax.axis_size("row"), lax.axis_size("col")
    row_count, tiles, _, tile = x4.shape
    vmem = pl.BlockSpec(memory_space=pltpu.VMEM)
    dma = pltpu.SemaphoreType.DMA
    return pl.pallas_call(
        functools.partial(factor_move_kernel, rows, cols),
        out_shape=factor_shapes(BAND)
        + (
            jax.ShapeDtypeStruct((PANELS, row_count, BAND), jnp.float32),
            jax.ShapeDtypeStruct((BAND, tiles * tile), jnp.float32),
        ),
        in_specs=[vmem, pl.BlockSpec(memory_space=pl.ANY)],
        out_specs=(vmem,) * 6,
        scratch_shapes=[dma((1,)), dma((cols - 1,)), dma((PANELS * BAND // tile,))]
        + Chain.semaphores(tiles, tiles * tile // CHUNK),
        compiler_params=pltpu.CompilerParams(
            collective_id=collective_id, has_side_effects=True, vmem_limit_bytes=SMALL
        ),
    )(stack, x4)


def split(value):
    high = value.astype(jnp.bfloat16)
    return high, (value - high.astype(jnp.float32)).astype(jnp.bfloat16)


def split_outside(value):
    high = lax.reduce_precision(value, 8, 7)
    return high.astype(jnp.bfloat16), (value - high).astype(jnp.bfloat16)


def dot(a, b):
    return jnp.dot(a, b, preferred_element_type=jnp.float32)


def apply_kernel(rows, cols, fixed, *refs):
    place = Place(rows, cols)
    x_ref, left_ref = refs[:2]
    more = refs[2 : 2 + fixed]
    out_ref, row_ref = refs[2 + fixed : 4 + fixed]
    block, part, near, pair, left_in, right_in, left_out, right_out = refs[4 + fixed : 12 + fixed]
    (
        load, near_send, near_recv, left_send, left_recv, right_send, right_recv,
        both_send, both_recv, row_send, row_recv,
    ) = refs[12 + fixed :]
    plane, core, planes = place.plane, place.core, place.planes
    tile = x_ref.shape[-1]
    chunks = block.shape[0]
    half = left_ref.shape[0] // 2

    def load_of(chunk, index):
        return pltpu.make_async_copy(
            x_ref.at[:, 2 * chunk + index, 0, :],
            block.at[chunk, :, pl.ds(index * tile, tile)],
            load.at[chunk, index],
        )

    for chunk in range(chunks):
        for index in range(2):
            load_of(chunk, index).start()
    place.greet()

    def near_of(chunk):
        return remote(
            part.at[chunk, 1 - core],
            near.at[chunk],
            near_send.at[chunk],
            near_recv.at[chunk],
            place.other,
            place.col,
        )

    def rightward(source, chunk):
        return remote(
            source.at[chunk], left_in.at[chunk], right_send.at[chunk], left_recv.at[chunk],
            lax.rem(place.row + 2, rows), place.col,
        )

    def leftward(source, chunk):
        return remote(
            source.at[chunk], right_in.at[chunk], left_send.at[chunk], right_recv.at[chunk],
            lax.rem(place.row + rows - 2, rows), place.col,
        )

    def joined(chunk):
        near_of(chunk).wait_recv()
        pair[chunk] = part[chunk, core] + near[chunk]

        @pl.when(plane == 0)
        def _():
            rightward(pair, chunk).start()

        @pl.when(plane == planes - 1)
        def _():
            leftward(pair, chunk).start()

    def product(chunk, carry):
        for index in range(2):
            load_of(chunk, index).wait()
        high, low = split(block[chunk])
        value = dot(left_ref[...], high)
        value = value[:half] + (value[half:] + dot(left_ref[:half], low))
        if fixed:
            factor_ref, high_ref, low_ref = more
            here = pl.ds(pl.multiple_of(chunk * 2 * tile, 2 * tile), 2 * tile)
            other = dot(factor_ref[...], high_ref[:, here])
            other = other[:half] + (other[half:] + dot(factor_ref[:half], low_ref[:, here]))
            value = value - other
        part[chunk, 0] = value[:, :tile]
        part[chunk, 1] = value[:, tile:]
        near_of(chunk).start()

        @pl.when(chunk > 0)
        def _():
            joined(chunk - 1)

        return carry

    lax.fori_loop(0, chunks, product, 0)
    joined(chunks - 1)

    left_lag = jnp.maximum(plane - 1, 0)
    right_lag = jnp.maximum(planes - 2 - plane, 0)
    last_lag = jnp.maximum(left_lag, right_lag)
    held = cols * core + place.col
    source = held // 2 == plane
    target_row = 2 * plane + lax.rem(place.col, 2)
    to_self = target_row == place.row

    def spot(chunk):
        start = pl.multiple_of((2 * chunk + core) * tile, tile)
        return out_ref.at[:, pl.ds(start, tile)]

    def both_of(chunk):
        return remote(
            spot(chunk), spot(chunk), both_send.at[chunk], both_recv.at[chunk], place.other, place.col
        )

    def row_of(chunk, step):
        start = pl.multiple_of(chunk * tile, tile)
        return remote(
            spot(chunk),
            row_ref.at[:, pl.ds(start, tile)],
            row_send.at[chunk, step],
            row_recv.at[chunk],
            target_row,
            lax.rem(place.col + step, cols),
        )

    def chain(step, carry):
        index = step - left_lag

        @pl.when((plane > 0) & (index >= 0) & (index < chunks))
        def _():
            rightward(pair, index).wait_recv()

            @pl.when(plane < planes - 1)
            def _():
                right_out[index] = left_in[index] + pair[index]
                rightward(right_out, index).start()

        other = step - right_lag

        @pl.when((plane < planes - 1) & (other >= 0) & (other < chunks))
        def _():
            leftward(pair, other).wait_recv()

            @pl.when(plane > 0)
            def _():
                left_out[other] = right_in[other] + pair[other]
                leftward(left_out, other).start()

        done = step - last_lag

        @pl.when((done >= 0) & (done < chunks))
        def _():
            here = pl.ds(pl.multiple_of((2 * done + core) * tile, tile), tile)

            @pl.when(plane == 0)
            def _():
                out_ref[:, here] = pair[done] + right_in[done]

            @pl.when(plane == planes - 1)
            def _():
                out_ref[:, here] = left_in[done] + pair[done]

            @pl.when((plane > 0) & (plane < planes - 1))
            def _():
                out_ref[:, here] = right_out[done] + right_in[done]

            both_of(done).start()

            @pl.when(source)
            def _():
                for step in range(1, cols):
                    row_of(done, step).start()

                @pl.when(to_self)
                def _():
                    there = pl.ds(pl.multiple_of(done * tile, tile), tile)
                    row_ref[:, there] = out_ref[:, here]

                @pl.when(jnp.logical_not(to_self))
                def _():
                    row_of(done, 0).start()

        return carry

    lax.fori_loop(0, chunks + planes - 2, chain, 0)

    gets = jnp.logical_not(source & to_self)

    def drain(chunk, carry):
        near_of(chunk).wait_send()
        both_of(chunk).wait()

        @pl.when(plane < planes - 1)
        def _():
            rightward(pair, chunk).wait_send()

        @pl.when(plane > 0)
        def _():
            leftward(pair, chunk).wait_send()

        @pl.when(source)
        def _():
            for step in range(1, cols):
                row_of(chunk, step).wait_send()

            @pl.when(jnp.logical_not(to_self))
            def _():
                row_of(chunk, 0).wait_send()

        @pl.when(gets)
        def _():
            row_of(chunk, 0).wait_recv()

        return carry

    lax.fori_loop(0, chunks, drain, 0)


def apply(x4, left, more, collective_id):
    rows, cols = lax.axis_size("row"), lax.axis_size("col")
    row_count, tiles, _, tile = x4.shape
    width = tiles * tile
    chunks = tiles // 2
    vmem = pl.BlockSpec(memory_space=pltpu.VMEM)
    dma = pltpu.SemaphoreType.DMA
    piece = (BAND, tile)
    return pl.pallas_call(
        functools.partial(apply_kernel, rows, cols, len(more)),
        out_shape=(
            jax.ShapeDtypeStruct((BAND, width), jnp.float32),
            jax.ShapeDtypeStruct((BAND, row_count), jnp.float32),
        ),
        in_specs=[pl.BlockSpec(memory_space=pl.ANY)] + [vmem] * (1 + len(more)),
        out_specs=(vmem, vmem),
        scratch_shapes=[
            pltpu.VMEM((chunks, row_count, 2 * tile), jnp.float32),
            pltpu.VMEM((chunks, 2) + piece, jnp.float32),
        ]
        + [pltpu.VMEM((chunks,) + piece, jnp.float32)] * 6
        + [dma((chunks, 2))]
        + [dma((chunks,))] * 8
        + [dma((chunks, cols)), dma((chunks,))],
        compiler_params=pltpu.CompilerParams(
            collective_id=collective_id, has_side_effects=True, vmem_limit_bytes=BIG
        ),
    )(x4, left, *more)


def update_kernel(x_ref, left_high, left_low, right_high, right_low, out_ref, block, result, load, store):
    tile = x_ref.shape[-1]
    chunks = x_ref.shape[1] // 2

    def load_of(chunk, index):
        return pltpu.make_async_copy(
            x_ref.at[:, 2 * chunk + index, 0, :],
            block.at[lax.rem(chunk, 2), :, pl.ds(index * tile, tile)],
            load.at[lax.rem(chunk, 2), index],
        )

    def store_of(chunk, index):
        return pltpu.make_async_copy(
            result.at[lax.rem(chunk, 2), :, pl.ds(index * tile, tile)],
            out_ref.at[:, 2 * chunk + index, 0, :],
            store.at[lax.rem(chunk, 2), index],
        )

    for chunk in range(2):
        for index in range(2):
            load_of(chunk, index).start()

    rows = x_ref.shape[0]
    group = rows // 5 if rows % 40 == 0 else rows

    def body(chunk, carry):
        slot = lax.rem(chunk, 2)
        for index in range(2):
            load_of(chunk, index).wait()

        @pl.when(chunk >= 2)
        def _():
            for index in range(2):
                store_of(chunk - 2, index).wait()

        here = pl.ds(pl.multiple_of(chunk * 2 * tile, 2 * tile), 2 * tile)

        def rows_of(number, inner):
            part = pl.ds(pl.multiple_of(number * group, 8), group)
            high, low = left_high[part, :], left_low[part, :]
            value = dot(high, right_high[:, here]) + (
                dot(low, right_high[:, here]) + dot(high, right_low[:, here])
            )
            result[slot, part, :] = block[slot, part, :] - value
            return inner

        lax.fori_loop(0, rows // group, rows_of, 0)
        for index in range(2):
            store_of(chunk, index).start()

        @pl.when(chunk + 2 < chunks)
        def _():
            for index in range(2):
                load_of(chunk + 2, index).start()

        return carry

    lax.fori_loop(0, chunks, body, 0)
    for chunk in range(chunks - 2, chunks):
        for index in range(2):
            store_of(chunk, index).wait()


def update(x4, lefts, rights):
    row_count, tiles, _, tile = x4.shape
    vmem = pl.BlockSpec(memory_space=pltpu.VMEM)
    hbm = pl.BlockSpec(memory_space=pl.ANY)
    dma = pltpu.SemaphoreType.DMA
    return pl.pallas_call(
        update_kernel,
        out_shape=jax.ShapeDtypeStruct(x4.shape, x4.dtype),
        in_specs=[hbm] + [vmem] * 4,
        out_specs=hbm,
        scratch_shapes=[pltpu.VMEM((2, row_count, 2 * tile), jnp.float32)] * 2
        + [dma((2, 2)), dma((2, 2))],
        compiler_params=pltpu.CompilerParams(vmem_limit_bytes=BIG),
    )(x4, *split_outside(jnp.concatenate(lefts, 1)), *split_outside(jnp.concatenate(rights, 0)))


def on_device(matrix_tiles):
    tile_shape = matrix_tiles.shape
    block_rows, _, tile_size, block_cols = tile_shape[:4]
    row_count = block_rows * tile_size
    col_count = block_cols * tile_size
    row_devices = lax.axis_size("row")
    col_devices = lax.axis_size("col")
    row_index = lax.axis_index("row")
    col_index = lax.axis_index("col")
    panel_tiles = BAND // tile_size
    assert row_devices == 2 * col_devices and PANELS * panel_tiles <= col_devices
    high = lax.Precision.HIGH
    x4 = matrix_tiles.reshape(row_count, block_cols, 1, tile_size)

    def positions(count, devices, index):
        place = jnp.arange(count, dtype=jnp.int32)
        return (place // tile_size * devices + index) * tile_size + place % tile_size

    global_rows = positions(row_count, row_devices, row_index)
    global_cols = positions(col_count, col_devices, col_index)
    band = jnp.arange(BAND, dtype=jnp.int32)
    own_half = jnp.where(row_index % 2 == 0, 1.0, 0.0)

    def next_rows(panel, start):
        blocks = []
        for tile in range(start // tile_size, (start + BAND) // tile_size):
            local = tile // col_devices
            part = panel[:, local * tile_size : (local + 1) * tile_size]
            blocks.append(jnp.where(col_index == tile % col_devices, part * own_half, 0.0))
        return jnp.concatenate(blocks, 1)

    stacked, later_cols = gram(x4, 0)
    lefts, rights = [], []
    panel_cols = panel_rows = rows_held = None
    for panel_index in range(PANELS):
        below = (panel_index + 1) * BAND
        last = panel_index == PANELS - 1
        if panel_index == 0:
            inverse, shifted, transform, signs, rows_held, panel_cols = factors_move(stacked, x4, 1)
            panel_rows = rows_held[0]
        else:
            inverse, shifted, transform, signs = factors(stacked)
        panel_rows = jnp.where((global_rows >= below)[:, None], panel_rows, 0.0)
        panel_cols = jnp.where((global_cols >= below)[None, :], panel_cols, 0.0)
        unit_rows = (global_rows[:, None] - below == band[None, :]).astype(jnp.float32)
        unit_rows_t = (band[:, None] == global_rows[None, :] - below).astype(jnp.float32)
        unit_cols = (band[:, None] == global_cols[None, :] - below).astype(jnp.float32)
        signs_t = signs.reshape(BAND, 1)
        vec_rows = multiply(panel_rows, inverse, 1, 1) - unit_rows * signs
        vec_rows_t = multiply(inverse, panel_rows, 1, 1) - unit_rows_t * signs_t
        vec_cols = multiply(inverse, panel_cols) - unit_cols * signs_t
        more = ()
        if lefts:
            cross = jnp.concatenate([multiply(vec_rows_t, left, precision=high) for left in lefts], 1)
            more = (
                jnp.concatenate(split_outside(cross), 0),
                *split_outside(jnp.concatenate(rights, 0)),
            )
        sums, sums_rows = apply(x4, jnp.concatenate(split_outside(vec_rows_t), 0), more, 2 + panel_index)
        applied = multiply(transform, sums, 0, 0)
        applied_rows = multiply(sums_rows, transform, 0, 0)
        inner_part = 0.5 * multiply(vec_cols, applied, 1, 1)
        if last:
            inner = plane_sum(inner_part, 5)
        else:
            both = plane_sum(
                jnp.concatenate([inner_part, next_rows(applied, below)], 0), 4
            )
            inner = both[:BAND]
        half_inner = 0.5 * multiply(transform, inner, 0, 0)
        update_rows = applied_rows - multiply(vec_rows, half_inner)
        update_cols = applied - multiply(half_inner, vec_cols, 0, 0)
        lefts += [vec_rows, update_rows]
        rights += [update_cols, vec_cols]
        if not last:
            update_next = both[BAND:] - multiply(half_inner, shifted, 0, 1)
            panel_rows = (
                rows_held[panel_index + 1]
                - multiply(vec_rows, update_next)
                - multiply(update_rows, shifted, 1, 1)
            )
            panel_cols = (
                later_cols
                - multiply(update_next, vec_cols, 0, 0)
                - multiply(shifted, update_cols)
            )
            start = below + BAND
            kept = jnp.where((global_cols >= start)[None, :], panel_cols, 0.0)
            stacked = plane_sum(
                jnp.concatenate([0.5 * multiply(kept, kept, 1, 1), next_rows(panel_cols, start)], 0), 4
            )
    return update(x4, lefts, rights).reshape(tile_shape)


def solution(mesh):
    return jax.shard_map(
        on_device,
        mesh=mesh,
        in_specs=(P(None, "row", None, None, "col", None),),
        out_specs=P(None, "row", None, None, "col", None),
        check_vma=False,
    )
```

time: 522 us -> 439 us (0.84)
  waiting for transfers between devices: 43 us -> 0 us
  Pallas kernels: 308 us -> 345 us
  matrix products: 93.6 us -> 63.5 us
  local copies, waits for them, and re-layouts: 27.1 us -> 7.47 us
  between operations: 14.2 us -> 0.91 us
  other arithmetic: 25.8 us -> 14.7 us
    psum x4 -> x0, waiting for transfers between devices: 42.9 us -> none  [the longest x2 42.9 us: on_device(): pieces.append(lax.psum(jnp.where(mine, moved, 0.0), 'row'))]
    pallas_call x12 -> x9, Pallas kernels: 308 us -> 345 us  [the longest x2 147 us: apply(): pl.pallas_call(functools.partial(apply_kernel, rows, cols, len(more)), ou...]
    dot_general x25 -> x26, matrix products: 93.6 us -> 63.5 us  [multiply(): lax.dot_general(first, second, (((first_dim,), (second_dim,)), ((), ())),...]
    convert_element_type x0 -> x4, other arithmetic: none -> 11.4 us  [split_outside(): return (high.astype(jnp.bfloat16), (value - high).astype(jnp.bfloat16))]
    concatenate x7 -> x5, other arithmetic: 11.6 us -> 3.24 us  [the longest x2 2.33 us: on_device(): jnp.concatenate(split_outside(vec_rows_t), 0)]
    select_n x6 -> x2, other arithmetic: 7.76 us -> 0.04 us  [next_rows(): jnp.where(col_index == tile % col_devices, part * own_half, 0.0)]
    slice x4 -> x1, local copies, waits for them, and re-layouts: 7.04 us -> 0.04 us  [on_device(): inner = both[:BAND]]
    dot_general x2 -> x0, local copies, waits for them, and re-layouts: 5.61 us -> none  [multiply(): lax.dot_general(first, second, (((first_dim,), (second_dim,)), ((), ())),...]
  transfers between devices with their start and end apart: 4 -> 0, of which waited for: 2 -> 0; matrix products, arithmetic and copies ran while one was open for 16% -> 0% of each run, Pallas kernels for 45% -> 0%
where the time goes in v1:
time: 439 us; the launch traced here: 431 us
  Pallas kernels  345 us (79%)
  matrix products  63.5 us (14%)
  other arithmetic  14.7 us (3%)
  local copies, waits for them, and re-layouts  7.47 us (2%)
    pallas_call x2, Pallas kernels, apply(): pl.pallas_call(functools.partial(apply_kernel, rows, cols, len(more)), ou...  147 us
    dot_general x26, matrix products, multiply(): lax.dot_general(first, second, (((first_dim,), (second_dim,)), ((), ())),...  63.5 us
    pallas_call x1, Pallas kernels, factors_move(): pl.pallas_call(functools.partial(factor_move_kernel, rows, cols), out_sha...  50.8 us
    pallas_call x3, Pallas kernels, plane_sum(): pl.pallas_call(functools.partial(plane_kernel, rows, cols), out_shape=jax...  48.4 us
    pallas_call x1, Pallas kernels, gram(): pl.pallas_call(functools.partial(gram_kernel, rows, cols, BAND), out_shap...  37.6 us
    pallas_call x1, Pallas kernels, update(): pl.pallas_call(update_kernel, out_shape=jax.ShapeDtypeStruct(x4.shape, x4...  37.4 us
    pallas_call x1, Pallas kernels, factors(): pl.pallas_call(factor_kernel, out_shape=factor_shapes(stack.shape[1]), co...  23.9 us
    convert_element_type x4, other arithmetic, split_outside(): return (high.astype(jnp.bfloat16), (value - high).astype(jnp.bfloat16))  11.4 us

profile of v1, /device:TPU:0, one launch (start us, length us, event | category | flops | bytes accessed | tf_op | source)
XLA Modules:
  0.0 431.4 jit_solution(3407543905564579972)
XLA Ops:
  0.1 0.0 copy-start
  0.1 4.7 %copy-done = f32[10,1,128,20,1,128]{5,4,3,2,1,0:T(1,128)S(1)} copy-done((f32[10,1,128,20,1,128]{5,4,3,2,1,0:T(1,128)S(1)}, f32[10,1,128,20,1,128]{5,4,3,2,1,0:T(1,128)}, u32[]{:S(2)}) %copy-start) | copy-done | bytes 13107224
  4.8 37.6 %shard_map.17 = (f32[8,64,256]{2,1,0:T(8,128)S(1)}, f32[256,2560]{1,0:T(8,128)S(1)}) custom-call(f32[1280,20,1,128]{3,2,1,0:T(1,128)S(1)} %bitcast.69), custom_call_target="tpu_custom_call" | custom-call | tf_op jit(solution)/shard_map/pallas_call | solution.py:407
  42.4 50.8 %shard_map.18 = (f32[256,256]{1,0:T(8,128)S(1)}, f32[256,256]{1,0:T(8,128)S(1)}, f32[256,256]{1,0:T(8,128)S(1)}, f32[1,256]{1,0:T(1,128)S(1)}, f32[2,1280,256]{2,1,0:T(8,128)S(1)}, /*index=5*/f32[256,2560]{1,0:T(8,128)S(1)}) custom-call(f32[512,256]{1,0:T(8,128)S(1)} %bitcast.76, f32[1280,20,1,128]{3,2,1,0:T(1,128)S(1)} %bitcast.70), custom_call_target="tpu_custom_call" | custom-call | tf_op jit(solution)/shard_map/pallas_call | solution.py:537
  93.3 15.2 %convolution_subtract_fusion.5 = f32[256,2560]{1,0:T(8,128)} fusion(f32[256,256]{1,0:T(8,128)S(1)} %get-tuple-element.22, f32[256,2560]{1,0:T(8,128)S(1)} %get-tuple-element.26, f32[256]{0:T(256)S(1)} %bitcast.80, s32[2560]{0:T(1024)S(1)} %get-tuple-element.59, pred[2560]{0:T(1024)(128)(4,1)S(1)} %get-tuple-element.61), kind=kOutput, calls=%fused_computation.17 | convolution fusion | flops 2015887360 | bytes 5518848 | tf_op jit(solution)/shard_map/dot_general | solution.py:100
  108.5 2.7 convolution_subtract_fusion.13
  111.2 1.6 reduce-precision_convert_fusion.4
  112.8 1.2 pad_maximum_fusion.3.refs_1_
  113.9 84.8 %shard_map.19 = (f32[256,2560]{1,0:T(8,128)}, f32[256,1280]{1,0:T(8,128)}) custom-call(f32[1280,20,1,128]{3,2,1,0:T(1,128)} %bitcast.66, bf16[512,1280]{1,0:T(8,128)(2,1)} %pad_maximum_fusion.3.refs_1_), custom_call_target="tpu_custom_call" | custom-call | tf_op jit(solution)/shard_map/pallas_call | solution.py:783
  198.7 3.7 fusion.56
  202.4 2.4 fusion.57
  204.9 2.3 convolution_multiply_fusion.3
  207.2 18.3 %shard_map.20 = f32[8,64,256]{2,1,0:T(8,128)S(1)} custom-call(f32[8,64,256]{2,1,0:T(8,128)S(1)} %bitcast.72), custom_call_target="tpu_custom_call" | custom-call | tf_op jit(solution)/shard_map/pallas_call | solution.py:199
  225.6 0.6 convolution_multiply_fusion.1
  226.2 2.4 convolution_subtract_fusion.3
  228.6 1.2 convolution_subtract_fusion.11
  229.8 1.0 convolution_subtract_fusion.14
  230.8 0.9 copy-done.2
  231.8 1.2 convolution_subtract_fusion.10
  233.0 2.5 convolution_subtract_fusion.4
  235.5 1.3 fusion.3
  236.8 2.5 convolution_subtract_fusion.2
  239.3 2.4 fusion.16
  241.7 17.2 %shard_map.21 = f32[8,64,256]{2,1,0:T(8,128)S(1)} custom-call(f32[8,64,256]{2,1,0:T(8,128)S(1)} %bitcast.73), custom_call_target="tpu_custom_call" | custom-call | tf_op jit(solution)/shard_map/pallas_call | solution.py:199
  259.0 23.9 %shard_map.22 = (f32[256,256]{1,0:T(8,128)S(1)}, f32[256,256]{1,0:T(8,128)}, f32[256,256]{1,0:T(8,128)S(1)}, f32[1,256]{1,0:T(1,128)S(1)}) custom-call(f32[512,256]{1,0:T(8,128)S(1)} %bitcast.71), custom_call_target="tpu_custom_call" | custom-call | tf_op jit(solution)/shard_map/pallas_call | solution.py:525
  282.8 2.9 convolution_subtract_fusion.1
  285.8 2.3 convolution_subtract_fusion.8
  288.1 1.4 reduce-precision_convert_fusion.3
  289.5 1.2 pad_maximum_fusion.4.refs_1_
  290.7 0.7 fusion.59
  291.4 0.7 fusion.58
  292.2 0.1 reduce-precision_convert_fusion.5
  292.2 0.8 pad_maximum_fusion.6.refs_2_
  293.1 3.1 fusion.1
  296.1 61.9 %shard_map.23 = (f32[256,2560]{1,0:T(8,128)}, f32[256,1280]{1,0:T(8,128)}) custom-call(f32[1280,20,1,128]{3,2,1,0:T(1,128)} %bitcast.67, bf16[512,1280]{1,0:T(8,128)(2,1)} %pad_maximum_fusion.4.refs_1_, bf16[512,512]{1,0:T(8,128)(2,1)} %pad_maximum_fusion.6.refs_2_, bf16[512,2560]{1,0:T(8,128)(2,1)} %get-tuple-element.40.refs_3_, ...), custom_call_target="tpu_custom_call" | custom-call | tf_op jit(solution)/shard_map/pallas_call | solution.py:783
  358.0 3.7 fusion.60
  361.7 2.4 fusion.61
  364.1 2.3 convolution_multiply_fusion.2
  366.4 12.9 %shard_map.24 = f32[8,32,256]{2,1,0:T(8,128)S(1)} custom-call(f32[8,32,256]{2,1,0:T(8,128)S(1)} %bitcast.75), custom_call_target="tpu_custom_call" | custom-call | tf_op jit(solution)/shard_map/pallas_call | solution.py:199
  379.3 0.6 convolution_multiply_fusion
  379.9 2.4 convolution_subtract_fusion
  382.3 1.2 convolution_subtract_fusion.6
  383.5 0.1 copy-done.8
  383.6 0.4 copy-done.10
  384.0 3.2 fusion.2
  387.2 1.2 copy-done.6
  388.5 5.1 %fusion = (bf16[1024,2560]{1,0:T(8,128)(2,1)}, bf16[1024,2560]{1,0:T(8,128)(2,1)}) fusion(f32[256,2560]{1,0:T(8,128)S(1)} %convolution_subtract_fusion.1, f32[256,2560]{1,0:T(8,128)S(1)} %convolution_subtract_fusion, f32[256,2560]{1,0:T(8,128)S(1)} %copy-done.4, f32[256,2560]{1,0:T(8,128)S(1)} %copy-done.6), kind=kLoop, calls=%fused_computation.2 | loop fusion | flops 18350080 | bytes 20971520 | tf_op jit(solution)/shard_map/convert_element_type | solution.py:561
  393.6 37.4 %shard_map.25 = f32[1280,20,1,128]{3,2,1,0:T(1,128)} custom-call(f32[1280,20,1,128]{3,2,1,0:T(1,128)} %bitcast.68, bf16[1280,1024]{1,0:T(8,128)(2,1)} %get-tuple-element.38.left_high, bf16[1280,1024]{1,0:T(8,128)(2,1)} %get-tuple-element.37.left_low, bf16[1024,2560]{1,0:T(8,128)(2,1)} %get-tuple-element.36.right_high, ...), custom_call_target="tpu_custom_call" | custom-call | tf_op jit(solution)/shard_map/pallas_call | solution.py:873
  (31 shorter events, 0.2 us)
Async XLA Ops:
  0.1 4.7 %copy-start = (f32[10,1,128,20,1,128]{5,4,3,2,1,0:T(1,128)S(1)}, f32[10,1,128,20,1,128]{5,4,3,2,1,0:T(1,128)}, u32[]{:S(2)}) copy-start(f32[10,1,128,20,1,128]{5,4,3,2,1,0:T(1,128)} %param.1) | copy-start | bytes 39321604
  93.3 17.9 %copy-start.1 = (f32[2,1280,256]{2,1,0:T(8,128)}, f32[2,1280,256]{2,1,0:T(8,128)S(1)}, u32[]{:S(2)}) copy-start(f32[2,1280,256]{2,1,0:T(8,128)S(1)} %get-tuple-element.21) | copy-start | bytes 7864324
  198.7 3.7 copy-start.13
  202.4 2.4 copy-start.3
  226.2 2.4 copy-start.7
  228.6 64.5 %copy-start.5 = (f32[256,2560]{1,0:T(8,128)}, f32[256,2560]{1,0:T(8,128)S(1)}, u32[]{:S(2)}) copy-start(f32[256,2560]{1,0:T(8,128)S(1)} %convolution_subtract_fusion.3) | copy-start | bytes 7864324
  228.6 3.2 copy-start.2
  229.8 60.9 %copy-start.9 = (f32[1280,256]{1,0:T(8,128)}, f32[1280,256]{1,0:T(8,128)S(1)}, u32[]{:S(2)}) copy-start(f32[1280,256]{1,0:T(8,128)S(1)} %convolution_subtract_fusion.11) | copy-start | bytes 3932164
  358.0 3.7 copy-start.12
  379.9 2.4 copy-start.11
  382.3 1.3 copy-start.8
  382.3 1.7 copy-start.10
  384.0 3.2 copy-start.4
  384.0 4.4 %copy-start.6 = (f32[256,2560]{1,0:T(8,128)S(1)}, f32[256,2560]{1,0:T(8,128)}, u32[]{:S(2)}) copy-start(f32[256,2560]{1,0:T(8,128)} %copy-done.5) | copy-start | bytes 7864324

commit v2 on v1

--- a/solution.py
+++ b/solution.py
@@ -9,8 +9,9 @@
 
 BAND = 256
 PANELS = 2
-BIG = 60 * 1024 * 1024
-SMALL = 32 * 1024 * 1024
+MIB = 1024 * 1024
+SMALL = 24 * MIB
+TINY = 8 * MIB
 MESH = pl.DeviceIdType.MESH
 
 HI = lax.Precision.HIGHEST
@@ -79,21 +80,25 @@
     top = jnp.concatenate([first, jnp.zeros_like(first)], 1)
     return jnp.concatenate([top, jnp.concatenate([corner, second], 1)], 0)
 
-def factor_body(gram, top, inverse_ref, shifted_ref, transform_ref, sign_ref, hook):
+def orthogonal_top(gram, top, top_dim, inverse_ref, shifted_ref, sign_ref, hook):
     size = gram.shape[0]
     inverse = factor_inverse(gram, 64, hook)
     inverse_ref[...] = inverse
-    basis = mm(top, inverse, 0, 1)
+    basis = mm(top(), inverse, top_dim, 1)
     rows = lax.broadcasted_iota(jnp.int32, (size, size), 0)
     cols = lax.broadcasted_iota(jnp.int32, (size, size), 1)
-    on_diagonal = rows == cols
-    sign_square = jnp.where(on_diagonal, jnp.where(basis >= 0, -1.0, 1.0), 0.0)
-    shifted = basis - sign_square
-    shifted_ref[...] = shifted
+    sign_square = jnp.where(rows == cols, jnp.where(basis >= 0, -1.0, 1.0), 0.0)
+    shifted_ref[...] = basis - sign_square
+    sign_ref[...] = jnp.sum(sign_square, axis=0, keepdims=True)
+
+
+def block_transform(shifted, signs, hook):
+    size = shifted.shape[0]
     outer = factor_inverse(mm(shifted, shifted, 0, 0), 64, hook)
-    sign_column = jnp.sum(sign_square, axis=1, keepdims=True)
-    transform_ref[...] = -sign_column * mm(mm(shifted, outer, 1, 1), outer, 1, 0)
-    sign_ref[...] = jnp.sum(sign_square, axis=0, keepdims=True)
+    rows = lax.broadcasted_iota(jnp.int32, (size, size), 0)
+    cols = lax.broadcasted_iota(jnp.int32, (size, size), 1)
+    sign_column = jnp.sum(jnp.where(rows == cols, signs, 0.0), axis=1, keepdims=True)
+    return -sign_column * mm(mm(shifted, outer, 1, 1), outer, 1, 0)
 
 
 def multiply(first, second, first_dim=1, second_dim=0, precision=HI):
@@ -155,9 +160,9 @@
         pl.semaphore_wait(barrier, count)
 
 
-def plane_scatter(place, x_ref, parts, out_ref, send_sem, recv_sem):
+def plane_scatter(place, peers, x_ref, parts, out_ref, send_sem, recv_sem):
     copies = []
-    for slot, (row, col, piece) in enumerate(place.peers()):
+    for slot, (row, col, piece) in enumerate(peers):
         copies.append(
             remote(
                 x_ref.at[piece], parts.at[slot], send_sem.at[slot], recv_sem.at[slot], row, col
@@ -173,8 +178,7 @@
         copy.wait_send()
 
 
-def plane_gather(place, out_ref, send_sem, recv_sem):
-    mine = out_ref.at[place.me]
+def plane_gather(place, mine, send_sem, recv_sem):
     copies = []
     for slot, (row, col, _) in enumerate(place.peers()):
         copies.append(remote(mine, mine, send_sem.at[slot], recv_sem.at[slot], row, col))
@@ -182,32 +186,115 @@
     return copies
 
 
-def plane_kernel(rows, cols, x_ref, out_ref, parts, send_one, recv_one, send_two, recv_two):
+class Spread:
+    def __init__(self, place, source_ref, tiles, target_ref, send_sem, recv_sem):
+        self.place, self.source, self.tiles, self.target = place, source_ref, tiles, target_ref
+        self.send_sem, self.recv_sem = send_sem, recv_sem
+        self.tile = target_ref.shape[0] // 2
+
+    def refs(self, index, core):
+        start = pl.multiple_of(core * self.tile, self.tile)
+        local = self.tiles[index] // self.place.cols
+        return (
+            self.source.at[pl.ds(start, self.tile), pl.ds(local * self.tile, self.tile)],
+            self.target.at[pl.ds(start, self.tile), pl.ds(index * self.tile, self.tile)],
+        )
+
+    def holder(self, index):
+        return self.place.col == self.tiles[index] % self.place.cols
+
+    def copies(self, index):
+        source, target = self.refs(index, self.place.core)
+        return [
+            remote(
+                source,
+                target,
+                self.send_sem.at[index, slot],
+                self.recv_sem.at[index, self.place.core],
+                row,
+                col,
+            )
+            for slot, (row, col, _) in enumerate(self.place.peers())
+        ]
+
+    def send(self):
+        for index in range(len(self.tiles)):
+            @pl.when(self.holder(index))
+            def _():
+                for copy in self.copies(index):
+                    copy.start()
+                source, target = self.refs(index, self.place.core)
+                target[...] = source[...]
+
+    def wait(self):
+        for index in range(len(self.tiles)):
+            for core in range(2):
+                source, target = self.refs(index, core)
+
+                @pl.when(jnp.logical_not(self.holder(index) & (self.place.core == core)))
+                def _():
+                    remote(
+                        source,
+                        target,
+                        self.send_sem.at[index, 0],
+                        self.recv_sem.at[index, core],
+                        self.place.other,
+                        self.place.col,
+                    ).wait_recv()
+
+    def finish(self):
+        for index in range(len(self.tiles)):
+            @pl.when(self.holder(index))
+            def _():
+                for copy in self.copies(index):
+                    copy.wait_send()
+
+
+def plane_kernel(rows, cols, tiles, *refs):
     place = Place(rows, cols)
+    count = 2 if tiles else 1
+    x_ref, out_ref = refs[0], refs[count]
+    parts, send_one, recv_one, send_two, recv_two = refs[2 * count : 2 * count + 5]
     place.greet(False)
-    plane_scatter(place, x_ref, parts, out_ref, send_one, recv_one)
-    for copy in plane_gather(place, out_ref, send_two, recv_two):
+    same = [peer for peer in place.peers()[: cols - 1]]
+    plane_scatter(place, same, x_ref, parts, out_ref, send_one, recv_one)
+    copies = plane_gather(place, out_ref.at[place.me], send_two, recv_two)
+    if tiles:
+        spread = Spread(place, refs[1], tiles, refs[3], *refs[9:])
+        spread.send()
+    for copy in copies:
         copy.wait()
-
-
-def plane_sum(x, collective_id):
+    if tiles:
+        spread.wait()
+        spread.finish()
+
+
+def plane_sum(x, collective_id, panel=None, tiles=()):
     rows, cols = lax.axis_size("row"), lax.axis_size("col")
     size, width = x.shape
     count = 2 * cols
     pieces = (count, size // count, width)
     vmem = pl.BlockSpec(memory_space=pltpu.VMEM)
+    dma = pltpu.SemaphoreType.DMA
+    shapes = (jax.ShapeDtypeStruct(pieces, x.dtype),)
+    scratch = [pltpu.VMEM((cols - 1,) + pieces[1:], x.dtype)]
+    scratch += [dma((cols - 1,))] * 2 + [dma((count - 1,))] * 2
+    operands = (x.reshape(pieces),)
+    if tiles:
+        shapes += (jax.ShapeDtypeStruct((size, size), x.dtype),)
+        scratch += [dma((len(tiles), count - 1)), dma((len(tiles), 2))]
+        operands += (panel,)
     out = pl.pallas_call(
-        functools.partial(plane_kernel, rows, cols),
-        out_shape=jax.ShapeDtypeStruct(pieces, x.dtype),
-        in_specs=[vmem],
-        out_specs=vmem,
-        scratch_shapes=[pltpu.VMEM((count - 1,) + pieces[1:], x.dtype)]
-        + [pltpu.SemaphoreType.DMA((count - 1,))] * 4,
+        functools.partial(plane_kernel, rows, cols, tiles),
+        out_shape=shapes,
+        in_specs=[vmem] * len(operands),
+        out_specs=(vmem,) * len(shapes),
+        scratch_shapes=scratch,
         compiler_params=pltpu.CompilerParams(
-            collective_id=collective_id, has_side_effects=True, vmem_limit_bytes=SMALL
+            collective_id=collective_id, has_side_effects=True, vmem_limit_bytes=TINY
         ),
-    )(x.reshape(pieces))
-    return out.reshape(size, width)
+    )(*operands)
+    return (out[0].reshape(size, width),) + tuple(out[1:])
 
 
 class Chain:
@@ -255,13 +342,18 @@
             for copy in self.loads():
                 copy.start()
 
-    def send(self):
+    def share(self):
         @pl.when(self.at_source)
         def _():
             for copy in self.loads():
                 copy.wait()
             for chunk in range(self.chunks):
                 self.shared(chunk).start()
+
+    def spread(self, first, last):
+        @pl.when(self.at_source)
+        def _():
+            for chunk in range(first, last):
                 if self.source < self.place.planes - 1:
                     self.hop(chunk, 1, 0).start()
                 if self.source > 0:
@@ -286,10 +378,20 @@
 
                 self.shared(chunk).start()
 
-    def finish(self):
+    def join(self):
+        for chunk in range(self.chunks):
+            self.shared(chunk).wait_recv()
+
+    def finish(self, joined=False):
         place = self.place
+        if joined:
+            @pl.when(jnp.logical_not(self.at_source))
+            def _():
+                self.join()
+        else:
+            self.join()
         for chunk in range(self.chunks):
-            self.shared(chunk).wait()
+            self.shared(chunk).wait_send()
         for step, sem, sent in (
             (1, 0, (place.plane >= self.source) & (place.plane < place.planes - 1)),
             (-1, 1, (place.plane <= self.source) & (place.plane > 0)),
@@ -306,143 +408,37 @@
         return [dma((tiles,)), dma((2, chunks)), dma((chunks,)), dma((chunks,)), dma((chunks,))]
 
 
-def gram_kernel(rows, cols, below, x_ref, out_ref, later_ref, panel, stack, parts, *sems):
+CHUNK = 256
+
+
+def later_steps(chain, first, every):
+    count = [0]
+
+    def hook():
+        count[0] += 1
+        chunk = first + count[0] // every - 1
+        if count[0] % every == 0 and first <= chunk < chain.chunks:
+            chain.step(chunk)
+
+    return hook
+
+
+EARLY = 3
+
+
+def first_kernel(rows, cols, x_ref, inverse_ref, shifted_ref, sign_ref, rows_ref, cols_ref, *refs):
+    stack, parts, gram_ref, top_ref = refs[:4]
+    send_one, recv_one, line_send, line_recv, send_two, recv_two = refs[4:10]
+    load, send_row, recv_row, top_send, top_recv = refs[10:15]
     place = Place(rows, cols)
     tile, tiles = x_ref.shape[-1], x_ref.shape[1]
-    load, swap_send, swap_recv, send_one, recv_one, line_send, line_recv, send_two, recv_two = sems[:9]
-    later = Chain(place, 1, x_ref, later_ref, sems[9:])
+    panel_tiles = BAND // tile
+    held = PANELS * panel_tiles
+    chain = Chain(place, 0, x_ref, cols_ref, refs[15:])
+    spread = Spread(
+        place, cols_ref, tuple(range(panel_tiles, 2 * panel_tiles)), top_ref, top_send, top_recv
+    )
     first = place.plane == 0
-    start = pl.multiple_of(place.core * tile, tile)
-    own = panel.at[pl.ds(start, tile), :]
-
-    def loads():
-        for index in range(tiles):
-            yield pltpu.make_async_copy(
-                x_ref.at[pl.ds(0, tile), index, 0, :],
-                panel.at[pl.ds(start, tile), pl.ds(index * tile, tile)],
-                load.at[index],
-            )
-
-    @pl.when(first)
-    def _():
-        for copy in loads():
-            copy.start()
-
-    later.start()
-    place.greet()
-    later.send()
-    line = [
-        remote(
-            out_ref.at[place.me],
-            out_ref.at[place.me],
-            line_send.at[step - 1],
-            line_recv.at[0],
-            lax.rem(place.row + 2 * step, rows),
-            place.col,
-        )
-        for step in range(1, place.planes)
-    ]
-
-    @pl.when(first)
-    def _():
-        for copy in loads():
-            copy.wait()
-        swap = remote(own, own, swap_send.at[0], swap_recv.at[0], place.other, place.col)
-        swap.start()
-        swap.wait()
-        width = tile * tiles // 2
-        offset = place.core * width
-        lanes = lax.broadcasted_iota(jnp.int32, (panel.shape[0], width), 1) + offset
-        begin = below // tile
-        limit = jnp.where(place.col < begin, tile, 0)
-        value = panel[:, pl.ds(pl.multiple_of(offset, tile), width)]
-        value = jnp.where(lanes >= limit, value, 0.0)
-        gram = mm(value, value, 1, 1)
-        size = stack.shape[1]
-        per = panel.shape[0] // size
-        for piece in range(per):
-            stack[piece] = gram[piece * size : (piece + 1) * size]
-        for index in range(panel.shape[0] // tile):
-            number = begin + index
-            local = number // cols
-            mine = (place.col == number % cols) & (place.core == 0)
-            block = jnp.where(mine, panel[:, local * tile : (local + 1) * tile], 0.0)
-            for piece in range(per):
-                stack[per + piece, :, index * tile : (index + 1) * tile] = block[
-                    piece * size : (piece + 1) * size
-                ]
-        plane_scatter(place, stack, parts, out_ref, send_one, recv_one)
-        for copy in line:
-            copy.start()
-
-    @pl.when(place.plane > 0)
-    def _():
-        line[0].wait_recv()
-
-    gathers = plane_gather(place, out_ref, send_two, recv_two)
-    for chunk in range(later.chunks):
-        later.step(chunk)
-
-    @pl.when(first)
-    def _():
-        for copy in line:
-            copy.wait_send()
-
-    for copy in gathers:
-        copy.wait()
-    later.finish()
-
-
-CHUNK = 256
-
-
-def gram(x4, collective_id):
-    rows, cols = lax.axis_size("row"), lax.axis_size("col")
-    _, tiles, _, tile = x4.shape
-    width = tiles * tile
-    count = 2 * cols
-    pieces = (count, 2 * BAND // count, BAND)
-    vmem = pl.BlockSpec(memory_space=pltpu.VMEM)
-    dma = pltpu.SemaphoreType.DMA
-    one, later = pl.pallas_call(
-        functools.partial(gram_kernel, rows, cols, BAND),
-        out_shape=(
-            jax.ShapeDtypeStruct(pieces, x4.dtype),
-            jax.ShapeDtypeStruct((BAND, width), x4.dtype),
-        ),
-        in_specs=[pl.BlockSpec(memory_space=pl.ANY)],
-        out_specs=(vmem, vmem),
-        scratch_shapes=[
-            pltpu.VMEM((BAND, width), x4.dtype),
-            pltpu.VMEM(pieces, x4.dtype),
-            pltpu.VMEM((count - 1,) + pieces[1:], x4.dtype),
-            dma((tiles,)),
-            dma((1,)),
-            dma((1,)),
-            dma((count - 1,)),
-            dma((count - 1,)),
-            dma((rows // 2 - 1,)),
-            dma((1,)),
-            dma((count - 1,)),
-            dma((count - 1,)),
-        ]
-        + Chain.semaphores(tiles, width // CHUNK),
-        compiler_params=pltpu.CompilerParams(
-            collective_id=collective_id, has_side_effects=True, vmem_limit_bytes=SMALL
-        ),
-    )(x4)
-    return one.reshape(2 * BAND, BAND), later
-
-
-def factor_move_kernel(
-    rows, cols, stack_ref, x_ref, inverse_ref, shifted_ref, transform_ref, sign_ref, rows_ref, cols_ref, *sems
-):
-    place = Place(rows, cols)
-    tile = x_ref.shape[-1]
-    load, send_row, recv_row = sems[:3]
-    chain = Chain(place, 0, x_ref, cols_ref, sems[3:])
-    held = PANELS * BAND // tile
-    panel_tiles = BAND // tile
 
     def spot(col):
         start = pl.multiple_of(lax.rem(col, panel_tiles) * tile, tile)
@@ -458,7 +454,6 @@
 
     chain.start()
     place.greet()
-    chain.send()
     copies = [
         remote(
             own,
@@ -470,6 +465,46 @@
         )
         for step in range(1, cols)
     ]
+    line = [
+        remote(
+            gram_ref.at[place.me],
+            gram_ref.at[place.me],
+            line_send.at[step - 1],
+            line_recv.at[0],
+            lax.rem(place.row + 2 * step, rows),
+            place.col,
+        )
+        for step in range(1, place.planes)
+    ]
+    chain.share()
+    chain.spread(0, EARLY)
+
+    @pl.when(first)
+    def _():
+        chain.join()
+        width = tile * tiles // 2
+        offset = place.core * width
+        lanes = lax.broadcasted_iota(jnp.int32, (cols_ref.shape[0], width), 1) + offset
+        limit = jnp.where(place.col < panel_tiles, tile, 0)
+        value = cols_ref[:, pl.ds(pl.multiple_of(offset, tile), width)]
+        value = jnp.where(lanes >= limit, value, 0.0)
+        gram = mm(value, value, 1, 1)
+        size = stack.shape[1]
+        for piece in range(stack.shape[0]):
+            stack[piece] = gram[piece * size : (piece + 1) * size]
+        plane_scatter(place, place.peers(), stack, parts, gram_ref, send_one, recv_one)
+        for copy in line:
+            copy.start()
+
+    chain.spread(EARLY, chain.chunks)
+
+    @pl.when(place.plane > 0)
+    def _():
+        line[0].wait_recv()
+
+    gathers = plane_gather(place, gram_ref.at[place.me], send_two, recv_two)
+    chain.step(0)
+    spread.send()
 
     @pl.when(has)
     def _():
@@ -477,18 +512,25 @@
         for copy in copies:
             copy.start()
 
-    count = [0]
-
-    def hook():
-        count[0] += 1
-        chunk = count[0] // 2 - 2
-        if count[0] % 2 == 0 and 0 <= chunk < chain.chunks:
-            chain.step(chunk)
+    for copy in gathers:
+        copy.wait()
+
+    def top():
+        spread.wait()
+        return top_ref[...]
 
     size = inverse_ref.shape[0]
-    factor_body(
-        stack_ref[:size], stack_ref[size:], inverse_ref, shifted_ref, transform_ref, sign_ref, hook
+    orthogonal_top(
+        gram_ref[...].reshape(size, size), top, 0, inverse_ref, shifted_ref, sign_ref,
+        later_steps(chain, 1, 3),
     )
+
+    @pl.when(first)
+    def _():
+        for copy in line:
+            copy.wait_send()
+
+    spread.finish()
 
     @pl.when(has)
     def _():
@@ -500,55 +542,188 @@
         def _():
             remote(spot(col), spot(col), send_row.at[0], recv_row.at[col], place.row, place.col).wait_recv()
 
-    chain.finish()
-
-
-def factor_kernel(stack_ref, inverse_ref, shifted_ref, transform_ref, sign_ref):
-    size = inverse_ref.shape[0]
-    factor_body(
-        stack_ref[:size],
-        stack_ref[size:],
-        inverse_ref,
-        shifted_ref,
-        transform_ref,
-        sign_ref,
-        lambda: None,
-    )
-
-
-def factor_shapes(size):
-    square = jax.ShapeDtypeStruct((size, size), jnp.float32)
-    return (square, square, square, jax.ShapeDtypeStruct((1, size), jnp.float32))
-
-
-def factors(stack):
-    return pl.pallas_call(
-        factor_kernel,
-        out_shape=factor_shapes(stack.shape[1]),
-        compiler_params=pltpu.CompilerParams(vmem_limit_bytes=SMALL),
-    )(stack)
-
-
-def factors_move(stack, x4, collective_id):
+    chain.finish(True)
+
+
+def first_panel(x4, collective_id):
     rows, cols = lax.axis_size("row"), lax.axis_size("col")
     row_count, tiles, _, tile = x4.shape
+    width = tiles * tile
+    count = 2 * cols
+    pieces = (count, BAND // count, BAND)
     vmem = pl.BlockSpec(memory_space=pltpu.VMEM)
     dma = pltpu.SemaphoreType.DMA
+    panel_tiles = BAND // tile
+    square = jax.ShapeDtypeStruct((BAND, BAND), x4.dtype)
     return pl.pallas_call(
-        functools.partial(factor_move_kernel, rows, cols),
-        out_shape=factor_shapes(BAND)
-        + (
-            jax.ShapeDtypeStruct((PANELS, row_count, BAND), jnp.float32),
-            jax.ShapeDtypeStruct((BAND, tiles * tile), jnp.float32),
+        functools.partial(first_kernel, rows, cols),
+        out_shape=(
+            square,
+            square,
+            jax.ShapeDtypeStruct((1, BAND), x4.dtype),
+            jax.ShapeDtypeStruct((PANELS, row_count, BAND), x4.dtype),
+            jax.ShapeDtypeStruct((BAND, width), x4.dtype),
         ),
-        in_specs=[vmem, pl.BlockSpec(memory_space=pl.ANY)],
-        out_specs=(vmem,) * 6,
-        scratch_shapes=[dma((1,)), dma((cols - 1,)), dma((PANELS * BAND // tile,))]
-        + Chain.semaphores(tiles, tiles * tile // CHUNK),
+        in_specs=[pl.BlockSpec(memory_space=pltpu.HBM)],
+        out_specs=(vmem,) * 5,
+        scratch_shapes=[
+            pltpu.VMEM(pieces, x4.dtype),
+            pltpu.VMEM((count - 1,) + pieces[1:], x4.dtype),
+            pltpu.VMEM(pieces, x4.dtype),
+            pltpu.VMEM((BAND, BAND), x4.dtype),
+            dma((count - 1,)),
+            dma((count - 1,)),
+            dma((rows // 2 - 1,)),
+            dma((1,)),
+            dma((count - 1,)),
+            dma((count - 1,)),
+            dma((1,)),
+            dma((cols - 1,)),
+            dma((PANELS * panel_tiles,)),
+            dma((panel_tiles, count - 1)),
+            dma((panel_tiles, 2)),
+        ]
+        + Chain.semaphores(tiles, width // CHUNK),
         compiler_params=pltpu.CompilerParams(
             collective_id=collective_id, has_side_effects=True, vmem_limit_bytes=SMALL
         ),
-    )(stack, x4)
+    )(x4)
+
+
+def next_kernel(rows, cols, gram_in, panel_ref, x_ref, inverse_ref, shifted_ref, sign_ref, cols_ref, *refs):
+    near, near_sum, parts, gram_ref, top_ref = refs[:5]
+    near_send, near_recv, line_send, line_recv, send_two, recv_two = refs[5:11]
+    top_line_send, top_line_recv, top_send, top_recv = refs[11:15]
+    place = Place(rows, cols)
+    tile = x_ref.shape[-1]
+    panel_tiles = BAND // tile
+    number = 2 * panel_tiles
+    chain = Chain(place, 1, x_ref, cols_ref, refs[15:])
+    chain.start()
+    place.greet()
+    swap = remote(
+        gram_in.at[place.col, 1 - place.core], near.at[0], near_send.at[0], near_recv.at[0],
+        place.other, place.col,
+    )
+    swap.start()
+
+    top_plane = number % rows // 2
+    start = pl.multiple_of(place.core * tile, tile)
+    local = number // rows * tile
+    block = panel_ref.at[pl.ds(local, tile), :]
+    target = top_ref.at[pl.ds(start, tile), :]
+    at_top = place.plane == top_plane
+
+    def top_line(step):
+        return remote(
+            block, target, top_line_send.at[step - 1], top_line_recv.at[0],
+            lax.rem(place.row + 2 * step, rows), place.col,
+        )
+
+    top_near = remote(target, target, top_send.at[0], top_recv.at[0], place.other, place.col)
+    top_first = remote(block, target, top_send.at[0], top_recv.at[0], place.other, place.col)
+
+    swap.wait_recv()
+    near_sum[0] = gram_in[place.col, place.core] + near[0]
+    line = [
+        remote(
+            near_sum.at[0], parts.at[step - 1], line_send.at[step - 1], line_recv.at[step - 1],
+            lax.rem(place.row + 2 * step, rows), place.col,
+        )
+        for step in range(1, place.planes)
+    ]
+    for copy in line:
+        copy.start()
+
+    @pl.when(at_top)
+    def _():
+        for step in range(1, place.planes):
+            top_line(step).start()
+        top_first.start()
+        target[...] = block[...]
+
+    chain.share()
+    chain.spread(0, chain.chunks)
+    total = near_sum[0]
+    for slot, copy in enumerate(line):
+        copy.wait_recv()
+        total = total + parts[slot]
+    piece = 2 * place.col + place.core
+    gram_ref[piece] = total
+    gathers = plane_gather(place, gram_ref.at[piece], send_two, recv_two)
+
+    @pl.when(jnp.logical_not(at_top))
+    def _():
+        top_line(1).wait_recv()
+        top_near.start()
+
+    for copy in gathers:
+        copy.wait()
+
+    def top():
+        top_near.wait_recv()
+        return top_ref[...]
+
+    size = inverse_ref.shape[0]
+    orthogonal_top(
+        gram_ref[...].reshape(size, size), top, 1, inverse_ref, shifted_ref, sign_ref,
+        later_steps(chain, 0, 3),
+    )
+    swap.wait_send()
+    for copy in line:
+        copy.wait_send()
+    top_near.wait_send()
+
+    @pl.when(at_top)
+    def _():
+        for step in range(1, place.planes):
+            top_line(step).wait_send()
+
+    chain.finish()
+
+
+def next_panel(gram, panel_rows, x4, collective_id):
+    rows, cols = lax.axis_size("row"), lax.axis_size("col")
+    _, tiles, _, tile = x4.shape
+    width = tiles * tile
+    count = 2 * cols
+    piece = (BAND // count, BAND)
+    planes = rows // 2
+    vmem = pl.BlockSpec(memory_space=pltpu.VMEM)
+    dma = pltpu.SemaphoreType.DMA
+    square = jax.ShapeDtypeStruct((BAND, BAND), x4.dtype)
+    return pl.pallas_call(
+        functools.partial(next_kernel, rows, cols),
+        out_shape=(
+            square,
+            square,
+            jax.ShapeDtypeStruct((1, BAND), x4.dtype),
+            jax.ShapeDtypeStruct((BAND, width), x4.dtype),
+        ),
+        in_specs=[vmem, vmem, pl.BlockSpec(memory_space=pltpu.HBM)],
+        out_specs=(vmem,) * 4,
+        scratch_shapes=[
+            pltpu.VMEM((1,) + piece, x4.dtype),
+            pltpu.VMEM((1,) + piece, x4.dtype),
+            pltpu.VMEM((planes - 1,) + piece, x4.dtype),
+            pltpu.VMEM((count,) + piece, x4.dtype),
+            pltpu.VMEM((BAND, BAND), x4.dtype),
+            dma((1,)),
+            dma((1,)),
+            dma((planes - 1,)),
+            dma((planes - 1,)),
+            dma((count - 1,)),
+            dma((count - 1,)),
+            dma((planes - 1,)),
+            dma((1,)),
+            dma((1,)),
+            dma((1,)),
+        ]
+        + Chain.semaphores(tiles, width // CHUNK),
+        compiler_params=pltpu.CompilerParams(
+            collective_id=collective_id, has_side_effects=True, vmem_limit_bytes=SMALL
+        ),
+    )(gram.reshape((cols, 2) + piece), panel_rows, x4)
 
 
 def split(value):
@@ -567,14 +742,18 @@
 
 def apply_kernel(rows, cols, fixed, *refs):
     place = Place(rows, cols)
-    x_ref, left_ref = refs[:2]
-    more = refs[2 : 2 + fixed]
-    out_ref, row_ref = refs[2 + fixed : 4 + fixed]
-    block, part, near, pair, left_in, right_in, left_out, right_out = refs[4 + fixed : 12 + fixed]
+    x_ref, left_ref, shifted_ref, sign_ref = refs[:4]
+    if fixed:
+        old_high, old_low, new_high, new_low = refs[4:8]
+        kept_ref, store = refs[11], refs[-1]
+        refs = refs[:8] + refs[8:11] + refs[12:-1]
+    refs = refs[8 if fixed else 4 :]
+    out_ref, row_ref, transform_ref = refs[:3]
+    block, part, near, pair, left_in, right_in, left_out, right_out = refs[3:11]
     (
         load, near_send, near_recv, left_send, left_recv, right_send, right_recv,
         both_send, both_recv, row_send, row_recv,
-    ) = refs[12 + fixed :]
+    ) = refs[11:]
     plane, core, planes = place.plane, place.core, place.planes
     tile = x_ref.shape[-1]
     chunks = block.shape[0]
@@ -585,6 +764,16 @@
             x_ref.at[:, 2 * chunk + index, 0, :],
             block.at[chunk, :, pl.ds(index * tile, tile)],
             load.at[chunk, index],
+        )
+
+    row_count = x_ref.shape[0]
+    group = row_count // 5 if row_count % 40 == 0 else row_count
+
+    def store_of(chunk, index):
+        return pltpu.make_async_copy(
+            block.at[chunk, :, pl.ds(index * tile, tile)],
+            kept_ref.at[:, 2 * chunk + index, 0, :],
+            store.at[chunk, index],
         )
 
     for chunk in range(chunks):
@@ -629,15 +818,24 @@
     def product(chunk, carry):
         for index in range(2):
             load_of(chunk, index).wait()
+        if fixed:
+            here = pl.ds(pl.multiple_of(chunk * 2 * tile, 2 * tile), 2 * tile)
+
+            def rows_of(number, inner):
+                rows_here = pl.ds(pl.multiple_of(number * group, 8), group)
+                high, low = old_high[rows_here, :], old_low[rows_here, :]
+                change = dot(high, new_high[:, here]) + (
+                    dot(low, new_high[:, here]) + dot(high, new_low[:, here])
+                )
+                block[chunk, rows_here, :] = block[chunk, rows_here, :] - change
+                return inner
+
+            lax.fori_loop(0, row_count // group, rows_of, 0)
+            for index in range(2):
+                store_of(chunk, index).start()
         high, low = split(block[chunk])
         value = dot(left_ref[...], high)
         value = value[:half] + (value[half:] + dot(left_ref[:half], low))
-        if fixed:
-            factor_ref, high_ref, low_ref = more
-            here = pl.ds(pl.multiple_of(chunk * 2 * tile, 2 * tile), 2 * tile)
-            other = dot(factor_ref[...], high_ref[:, here])
-            other = other[:half] + (other[half:] + dot(factor_ref[:half], low_ref[:, here]))
-            value = value - other
         part[chunk, 0] = value[:, :tile]
         part[chunk, 1] = value[:, tile:]
         near_of(chunk).start()
@@ -738,11 +936,25 @@
 
         return carry
 
-    lax.fori_loop(0, chunks + planes - 2, chain, 0)
+    steps = chunks + planes - 2
+    count = [0, 0]
+
+    def hook():
+        count[0] += 1
+        if count[0] % 2 == 0 and count[1] < steps:
+            chain(count[1], 0)
+            count[1] += 1
+
+    transform_ref[...] = block_transform(shifted_ref[...], sign_ref[...], hook)
+    if count[1] < steps:
+        lax.fori_loop(count[1], steps, chain, 0)
 
     gets = jnp.logical_not(source & to_self)
 
     def drain(chunk, carry):
+        if fixed:
+            for index in range(2):
+                store_of(chunk, index).wait()
         near_of(chunk).wait_send()
         both_of(chunk).wait()
 
@@ -772,22 +984,26 @@
     lax.fori_loop(0, chunks, drain, 0)
 
 
-def apply(x4, left, more, collective_id):
+def apply(x4, left, shifted, signs, more, collective_id):
     rows, cols = lax.axis_size("row"), lax.axis_size("col")
     row_count, tiles, _, tile = x4.shape
     width = tiles * tile
     chunks = tiles // 2
     vmem = pl.BlockSpec(memory_space=pltpu.VMEM)
+    hbm = pl.BlockSpec(memory_space=pltpu.HBM)
     dma = pltpu.SemaphoreType.DMA
     piece = (BAND, tile)
+    kept = bool(more)
+    shapes = (
+        jax.ShapeDtypeStruct((BAND, width), jnp.float32),
+        jax.ShapeDtypeStruct((BAND, row_count), jnp.float32),
+        jax.ShapeDtypeStruct((BAND, BAND), jnp.float32),
+    )
     return pl.pallas_call(
-        functools.partial(apply_kernel, rows, cols, len(more)),
-        out_shape=(
-            jax.ShapeDtypeStruct((BAND, width), jnp.float32),
-            jax.ShapeDtypeStruct((BAND, row_count), jnp.float32),
-        ),
-        in_specs=[pl.BlockSpec(memory_space=pl.ANY)] + [vmem] * (1 + len(more)),
-        out_specs=(vmem, vmem),
+        functools.partial(apply_kernel, rows, cols, kept),
+        out_shape=shapes + ((jax.ShapeDtypeStruct(x4.shape, x4.dtype),) if kept else ()),
+        in_specs=[hbm] + [vmem] * (3 + len(more)),
+        out_specs=(vmem,) * 3 + ((hbm,) if kept else ()),
         scratch_shapes=[
             pltpu.VMEM((chunks, row_count, 2 * tile), jnp.float32),
             pltpu.VMEM((chunks, 2) + piece, jnp.float32),
@@ -795,11 +1011,12 @@
         + [pltpu.VMEM((chunks,) + piece, jnp.float32)] * 6
         + [dma((chunks, 2))]
         + [dma((chunks,))] * 8
-        + [dma((chunks, cols)), dma((chunks,))],
+        + [dma((chunks, cols)), dma((chunks,))]
+        + ([dma((chunks, 2))] if kept else []),
         compiler_params=pltpu.CompilerParams(
-            collective_id=collective_id, has_side_effects=True, vmem_limit_bytes=BIG
+            collective_id=collective_id, has_side_effects=True, vmem_limit_bytes=(52 if kept else 40) * MIB
         ),
-    )(x4, left, *more)
+    )(x4, left, shifted, signs, *more)
 
 
 def update_kernel(x_ref, left_high, left_low, right_high, right_low, out_ref, block, result, load, store):
@@ -865,10 +1082,10 @@
             store_of(chunk, index).wait()
 
 
-def update(x4, lefts, rights):
+def update(x4, left, right):
     row_count, tiles, _, tile = x4.shape
     vmem = pl.BlockSpec(memory_space=pltpu.VMEM)
-    hbm = pl.BlockSpec(memory_space=pl.ANY)
+    hbm = pl.BlockSpec(memory_space=pltpu.HBM)
     dma = pltpu.SemaphoreType.DMA
     return pl.pallas_call(
         update_kernel,
@@ -877,8 +1094,8 @@
         out_specs=hbm,
         scratch_shapes=[pltpu.VMEM((2, row_count, 2 * tile), jnp.float32)] * 2
         + [dma((2, 2)), dma((2, 2))],
-        compiler_params=pltpu.CompilerParams(vmem_limit_bytes=BIG),
-    )(x4, *split_outside(jnp.concatenate(lefts, 1)), *split_outside(jnp.concatenate(rights, 0)))
+        compiler_params=pltpu.CompilerParams(vmem_limit_bytes=48 * MIB),
+    )(x4, *left, *right)
 
 
 def on_device(matrix_tiles):
@@ -902,27 +1119,12 @@
     global_rows = positions(row_count, row_devices, row_index)
     global_cols = positions(col_count, col_devices, col_index)
     band = jnp.arange(BAND, dtype=jnp.int32)
-    own_half = jnp.where(row_index % 2 == 0, 1.0, 0.0)
-
-    def next_rows(panel, start):
-        blocks = []
-        for tile in range(start // tile_size, (start + BAND) // tile_size):
-            local = tile // col_devices
-            part = panel[:, local * tile_size : (local + 1) * tile_size]
-            blocks.append(jnp.where(col_index == tile % col_devices, part * own_half, 0.0))
-        return jnp.concatenate(blocks, 1)
-
-    stacked, later_cols = gram(x4, 0)
-    lefts, rights = [], []
-    panel_cols = panel_rows = rows_held = None
+    inverse, shifted, signs, rows_held, panel_cols = first_panel(x4, 0)
+    panel_rows = rows_held[0]
+    kept, more = x4, ()
     for panel_index in range(PANELS):
         below = (panel_index + 1) * BAND
         last = panel_index == PANELS - 1
-        if panel_index == 0:
-            inverse, shifted, transform, signs, rows_held, panel_cols = factors_move(stacked, x4, 1)
-            panel_rows = rows_held[0]
-        else:
-            inverse, shifted, transform, signs = factors(stacked)
         panel_rows = jnp.where((global_rows >= below)[:, None], panel_rows, 0.0)
         panel_cols = jnp.where((global_cols >= below)[None, :], panel_cols, 0.0)
         unit_rows = (global_rows[:, None] - below == band[None, :]).astype(jnp.float32)
@@ -932,47 +1134,42 @@
         vec_rows = multiply(panel_rows, inverse, 1, 1) - unit_rows * signs
         vec_rows_t = multiply(inverse, panel_rows, 1, 1) - unit_rows_t * signs_t
         vec_cols = multiply(inverse, panel_cols) - unit_cols * signs_t
-        more = ()
-        if lefts:
-            cross = jnp.concatenate([multiply(vec_rows_t, left, precision=high) for left in lefts], 1)
-            more = (
-                jnp.concatenate(split_outside(cross), 0),
-                *split_outside(jnp.concatenate(rights, 0)),
-            )
-        sums, sums_rows = apply(x4, jnp.concatenate(split_outside(vec_rows_t), 0), more, 2 + panel_index)
+        sums, sums_rows, transform, *held = apply(
+            kept, jnp.concatenate(split_outside(vec_rows_t), 0), shifted, signs, more, 1 + panel_index
+        )
+        if held:
+            kept = held[0]
         applied = multiply(transform, sums, 0, 0)
         applied_rows = multiply(sums_rows, transform, 0, 0)
-        inner_part = 0.5 * multiply(vec_cols, applied, 1, 1)
+        inner_part = multiply(vec_cols, applied, 1, 1)
         if last:
-            inner = plane_sum(inner_part, 5)
+            (inner,) = plane_sum(inner_part, 5)
         else:
-            both = plane_sum(
-                jnp.concatenate([inner_part, next_rows(applied, below)], 0), 4
+            first = below // tile_size
+            inner, applied_next = plane_sum(
+                inner_part, 4, applied, tuple(range(first, first + panel_tiles))
             )
-            inner = both[:BAND]
         half_inner = 0.5 * multiply(transform, inner, 0, 0)
         update_rows = applied_rows - multiply(vec_rows, half_inner)
         update_cols = applied - multiply(half_inner, vec_cols, 0, 0)
-        lefts += [vec_rows, update_rows]
-        rights += [update_cols, vec_cols]
-        if not last:
-            update_next = both[BAND:] - multiply(half_inner, shifted, 0, 1)
-            panel_rows = (
-                rows_held[panel_index + 1]
-                - multiply(vec_rows, update_next)
-                - multiply(update_rows, shifted, 1, 1)
-            )
-            panel_cols = (
-                later_cols
-                - multiply(update_next, vec_cols, 0, 0)
-                - multiply(shifted, update_cols)
-            )
-            start = below + BAND
-            kept = jnp.where((global_cols >= start)[None, :], panel_cols, 0.0)
-            stacked = plane_sum(
-                jnp.concatenate([0.5 * multiply(kept, kept, 1, 1), next_rows(panel_cols, start)], 0), 4
-            )
-    return update(x4, lefts, rights).reshape(tile_shape)
+        left = split_outside(jnp.concatenate([vec_rows, update_rows], 1))
+        right = split_outside(jnp.concatenate([update_cols, vec_cols], 0))
+        if last:
+            return update(kept, left, right).reshape(tile_shape)
+        more = left + right
+        update_next = applied_next - multiply(half_inner, shifted, 0, 1)
+        panel_rows = (
+            rows_held[panel_index + 1]
+            - multiply(vec_rows, update_next)
+            - multiply(update_rows, shifted, 1, 1)
+        )
+        panel_rows = jnp.where((global_rows >= below + BAND)[:, None], panel_rows, 0.0)
+        gram = multiply(panel_rows, panel_rows, 0, 0)
+        old_shifted = shifted
+        inverse, shifted, signs, panel_cols = next_panel(gram, panel_rows, x4, 3)
+        panel_cols = (
+            panel_cols - multiply(update_next, vec_cols, 0, 0) - multiply(old_shifted, update_cols)
+        )
 
 
 def solution(mesh):

time: 439 us -> 366 us (0.83)
  Pallas kernels: 345 us -> 296 us
  matrix products: 63.5 us -> 46 us
    pallas_call x8 -> x6, Pallas kernels: 307 us -> 273 us  [the longest x2 152 us: apply(): pl.pallas_call(functools.partial(apply_kernel, rows, cols, kept), out_sha...]
    dot_general x26 -> x23, matrix products: 63.5 us -> 46 us  [multiply(): lax.dot_general(first, second, (((first_dim,), (second_dim,)), ((), ())),...]
    pallas_call x1, Pallas kernels: 37.4 us -> 23.2 us  [update(): pl.pallas_call(update_kernel, out_shape=jax.ShapeDtypeStruct(x4.shape, x4...]
where the time goes in v2:
time: 366 us; the launch traced here: 359 us
  Pallas kernels  296 us (81%)
  matrix products  46 us (13%)
  other arithmetic  10.5 us (3%)
  local copies, waits for them, and re-layouts  6.26 us (2%)
    pallas_call x2, Pallas kernels, apply(): pl.pallas_call(functools.partial(apply_kernel, rows, cols, kept), out_sha...  152 us
    pallas_call x1, Pallas kernels, first_panel(): pl.pallas_call(functools.partial(first_kernel, rows, cols), out_shape=(sq...  54.8 us
    dot_general x23, matrix products, multiply(): lax.dot_general(first, second, (((first_dim,), (second_dim,)), ((), ())),...  46 us
    pallas_call x1, Pallas kernels, next_panel(): pl.pallas_call(functools.partial(next_kernel, rows, cols), out_shape=(squ...  39.8 us
    pallas_call x2, Pallas kernels, plane_sum(): pl.pallas_call(functools.partial(plane_kernel, rows, cols, tiles), out_sh...  26.7 us
    pallas_call x1, Pallas kernels, update(): pl.pallas_call(update_kernel, out_shape=jax.ShapeDtypeStruct(x4.shape, x4...  23.2 us
    convert_element_type x4, other arithmetic, split_outside(): return (high.astype(jnp.bfloat16), (value - high).astype(jnp.bfloat16))  7.59 us

profile of v2, /device:TPU:0, one launch (start us, length us, event | category | flops | bytes accessed | tf_op | source)
XLA Modules:
  0.0 359.4 jit_solution(6164835317024862948)
XLA Ops:
  0.1 0.0 copy-start
  0.1 4.7 %copy-done = f32[10,1,128,20,1,128]{5,4,3,2,1,0:T(1,128)S(1)} copy-done((f32[10,1,128,20,1,128]{5,4,3,2,1,0:T(1,128)S(1)}, f32[10,1,128,20,1,128]{5,4,3,2,1,0:T(1,128)}, u32[]{:S(2)}) %copy-start) | copy-done | bytes 13107224
  4.8 54.8 %shard_map.17 = (f32[256,256]{1,0:T(8,128)S(1)}, f32[256,256]{1,0:T(8,128)S(1)}, f32[1,256]{1,0:T(1,128)S(1)}, f32[2,1280,256]{2,1,0:T(8,128)S(1)}, f32[256,2560]{1,0:T(8,128)S(1)}) custom-call(f32[1280,20,1,128]{3,2,1,0:T(1,128)S(1)} %bitcast.72), custom_call_target="tpu_custom_call" | custom-call | tf_op jit(solution)/shard_map/pallas_call | solution.py:558
  59.6 0.0 copy-start.1
  59.6 4.5 %fusion.4 = f32[256,2560]{1,0:T(8,128)} fusion(f32[256,256]{1,0:T(8,128)S(1)} %get-tuple-element.24, f32[256,2560]{1,0:T(8,128)S(1)} %get-tuple-element.26, f32[256]{0:T(256)S(1)} %bitcast.81, s32[2560]{0:T(1024)S(1)} %get-tuple-element.59, pred[2560]{0:T(1024)(128)(4,1)S(1)} %get-tuple-element.61), kind=kOutput, calls=%fused_computation.16 | convolution fusion | flops 2015887360 | bytes 5518848 | tf_op jit(solution)/shard_map/dot_general | solution.py:105
  64.1 1.6 reduce-precision_convert_fusion.5
  65.7 0.1 pad_maximum_fusion.4.refs_1_
  65.8 1.5 copy.2
  67.3 1.5 select_subtract_fusion
  68.8 65.3 %shard_map.18 = (f32[256,2560]{1,0:T(8,128)S(1)}, f32[256,1280]{1,0:T(8,128)S(1)}, f32[256,256]{1,0:T(8,128)S(1)}) custom-call(f32[1280,20,1,128]{3,2,1,0:T(1,128)} %bitcast.70, bf16[512,1280]{1,0:T(8,128)(2,1)S(1)} %pad_maximum_fusion.4.refs_1_, f32[256,256]{1,0:T(8,128)S(1)} %get-tuple-element.27.refs_2_, f32[1,256]{1,0:T(1,128)S(1)} %get-tuple-element.25.refs_3_), custom_call_target="tpu_custom_call" | custom-call | tf_op jit(solution)/shard_map/pallas_call | solution.py:1002
  134.1 0.0 copy-start.3
  134.1 2.4 fusion.49.refs_1_
  136.5 0.0 copy-done.3
  136.5 2.3 fusion.50
  138.8 15.8 %shard_map.19 = (f32[8,32,256]{2,1,0:T(8,128)S(1)}, f32[256,256]{1,0:T(8,128)S(1)}) custom-call(f32[8,32,256]{2,1,0:T(8,128)S(1)} %bitcast.79, f32[256,2560]{1,0:T(8,128)S(1)} %fusion.49.refs_1_), custom_call_target="tpu_custom_call" | custom-call | tf_op jit(solution)/shard_map/pallas_call | solution.py:287
  154.6 0.6 convolution_multiply_fusion.1
  155.2 2.2 fusion.51
  157.4 1.2 convolution_subtract_fusion.8
  158.6 0.0 copy-start.2
  158.6 2.4 convolution_subtract_fusion.3
  161.0 0.6 convolution_subtract_fusion.10
  161.6 1.2 convolution_subtract_fusion.9
  162.8 0.0 slice-start
  162.8 1.2 fusion.5.panel_ref
  164.0 0.0 slice-start.1
  164.0 1.9 fusion.6
  165.9 2.4 fusion.52
  168.3 0.0 slice-start.2
  168.3 4.0 %convolution_bitcast_fusion = f32[256,2560]{1,0:T(8,128)} fusion(f32[256,2560]{1,0:T(8,128)S(1)} %convolution_subtract_fusion.3, f32[256,256]{1,0:T(8,128)S(1)} %get-tuple-element.27.refs_2_), kind=kOutput, calls=%fused_computation.14 | convolution fusion | flops 2013265920 | bytes 5505024 | tf_op jit(solution)/shard_map/dot_general | solution.py:105
  172.4 3.1 fusion
  175.5 0.0 slice-done.2
  175.5 39.8 %shard_map.20 = (f32[256,256]{1,0:T(8,128)S(1)}, f32[256,256]{1,0:T(8,128)S(1)}, f32[1,256]{1,0:T(1,128)S(1)}, f32[256,2560]{1,0:T(8,128)S(1)}) custom-call(f32[4,2,32,256]{3,2,1,0:T(8,128)S(1)} %bitcast.76, f32[1280,256]{1,0:T(8,128)S(1)} %fusion.5.panel_ref, f32[1280,20,1,128]{3,2,1,0:T(1,128)S(1)} %bitcast.75), custom_call_target="tpu_custom_call" | custom-call | tf_op jit(solution)/shard_map/pallas_call | solution.py:695
  215.3 2.5 fusion.3
  217.9 2.7 convolution_subtract_fusion.1
  220.6 1.2 convolution_subtract_fusion.5
  221.9 1.6 reduce-precision_convert_fusion.4
  223.5 1.2 pad_maximum_fusion.5.refs_1_
  224.6 86.3 %shard_map.21 = (f32[256,2560]{1,0:T(8,128)}, f32[256,1280]{1,0:T(8,128)S(1)}, f32[256,256]{1,0:T(8,128)S(1)}, f32[1280,20,1,128]{3,2,1,0:T(1,128)}) custom-call(f32[1280,20,1,128]{3,2,1,0:T(1,128)} %bitcast.71, bf16[512,1280]{1,0:T(8,128)(2,1)} %pad_maximum_fusion.5.refs_1_, f32[256,256]{1,0:T(8,128)S(1)} %get-tuple-element.35.refs_2_, ...), custom_call_target="tpu_custom_call" | custom-call | tf_op jit(solution)/shard_map/pallas_call | solution.py:1002
  311.0 2.3 fusion.53
  313.3 2.5 fusion.54
  315.8 2.3 fusion.55
  318.1 10.9 %shard_map.22 = f32[8,32,256]{2,1,0:T(8,128)S(1)} custom-call(f32[8,32,256]{2,1,0:T(8,128)S(1)} %bitcast.78), custom_call_target="tpu_custom_call" | custom-call | tf_op jit(solution)/shard_map/pallas_call | solution.py:287
  329.0 0.6 convolution_multiply_fusion
  329.6 2.4 convolution_subtract_fusion
  332.1 1.2 convolution_subtract_fusion.4
  333.3 0.4 fusion.7
  333.7 2.2 fusion.1
  336.0 23.2 %shard_map.23 = f32[1280,20,1,128]{3,2,1,0:T(1,128)} custom-call(f32[1280,20,1,128]{3,2,1,0:T(1,128)} %get-tuple-element.36.x_ref, bf16[1280,512]{1,0:T(8,128)(2,1)S(1)} %get-tuple-element.46.left_high, bf16[1280,512]{1,0:T(8,128)(2,1)S(1)} %get-tuple-element.45.left_low, bf16[512,2560]{1,0:T(8,128)(2,1)S(1)} %get-tuple-element.42.right_high, ...), custom_call_target="tpu_custom_call" | custom-call | tf_op jit(solution)/shard_map/pallas_call | solution.py:1090
  (15 shorter events, 0.1 us)
Async XLA Ops:
  0.1 4.7 %copy-start = (f32[10,1,128,20,1,128]{5,4,3,2,1,0:T(1,128)S(1)}, f32[10,1,128,20,1,128]{5,4,3,2,1,0:T(1,128)}, u32[]{:S(2)}) copy-start(f32[10,1,128,20,1,128]{5,4,3,2,1,0:T(1,128)} %param.1) | copy-start | bytes 39321604
  59.6 4.5 %copy-start.1 = (f32[2,1280,256]{2,1,0:T(8,128)}, f32[2,1280,256]{2,1,0:T(8,128)S(1)}, u32[]{:S(2)}) copy-start(f32[2,1280,256]{2,1,0:T(8,128)S(1)} %get-tuple-element.23) | copy-start | bytes 7864324
  134.1 2.4 copy-start.3
  158.6 3.0 copy-start.2
  162.8 12.7 %slice-start = ((s8[13107200]{0:T(1024)(128)(4,1)}), s8[4194304]{0:T(1024)(128)(4,1)S(1)}, s32[]{:S(2)}) async-start(s8[13107200]{0:T(1024)(128)(4,1)} %bitcast.73), calls=%async_computation | async-start | bytes 8388608
  164.0 11.4 %slice-start.1 = ((s8[13107200]{0:T(1024)(128)(4,1)}), s8[4194304]{0:T(1024)(128)(4,1)S(1)}, s32[]{:S(2)}) async-start(s8[13107200]{0:T(1024)(128)(4,1)} %bitcast.73), calls=%async_computation.1 | async-start | bytes 8388608
  168.3 7.1 %slice-start.2 = ((s8[13107200]{0:T(1024)(128)(4,1)}), s8[4194304]{0:T(1024)(128)(4,1)S(1)}, s32[]{:S(2)}) async-start(s8[13107200]{0:T(1024)(128)(4,1)} %bitcast.73), calls=%async_computation.2 | async-start | bytes 8388608
  172.4 3.1 slice-start.3
  175.5 39.8 %copy-start.4 = (f32[256,2560]{1,0:T(8,128)S(1)}, f32[256,2560]{1,0:T(8,128)}, u32[]{:S(2)}) copy-start(f32[256,2560]{1,0:T(8,128)} %convolution_bitcast_fusion) | copy-start | bytes 7864324
  311.0 2.3 copy-start.5

commit v3 on v2

--- a/solution.py
+++ b/solution.py
@@ -10,8 +10,6 @@
 BAND = 256
 PANELS = 2
 MIB = 1024 * 1024
-SMALL = 24 * MIB
-TINY = 8 * MIB
 MESH = pl.DeviceIdType.MESH
 
 HI = lax.Precision.HIGHEST
@@ -250,53 +248,6 @@
                     copy.wait_send()
 
 
-def plane_kernel(rows, cols, tiles, *refs):
-    place = Place(rows, cols)
-    count = 2 if tiles else 1
-    x_ref, out_ref = refs[0], refs[count]
-    parts, send_one, recv_one, send_two, recv_two = refs[2 * count : 2 * count + 5]
-    place.greet(False)
-    same = [peer for peer in place.peers()[: cols - 1]]
-    plane_scatter(place, same, x_ref, parts, out_ref, send_one, recv_one)
-    copies = plane_gather(place, out_ref.at[place.me], send_two, recv_two)
-    if tiles:
-        spread = Spread(place, refs[1], tiles, refs[3], *refs[9:])
-        spread.send()
-    for copy in copies:
-        copy.wait()
-    if tiles:
-        spread.wait()
-        spread.finish()
-
-
-def plane_sum(x, collective_id, panel=None, tiles=()):
-    rows, cols = lax.axis_size("row"), lax.axis_size("col")
-    size, width = x.shape
-    count = 2 * cols
-    pieces = (count, size // count, width)
-    vmem = pl.BlockSpec(memory_space=pltpu.VMEM)
-    dma = pltpu.SemaphoreType.DMA
-    shapes = (jax.ShapeDtypeStruct(pieces, x.dtype),)
-    scratch = [pltpu.VMEM((cols - 1,) + pieces[1:], x.dtype)]
-    scratch += [dma((cols - 1,))] * 2 + [dma((count - 1,))] * 2
-    operands = (x.reshape(pieces),)
-    if tiles:
-        shapes += (jax.ShapeDtypeStruct((size, size), x.dtype),)
-        scratch += [dma((len(tiles), count - 1)), dma((len(tiles), 2))]
-        operands += (panel,)
-    out = pl.pallas_call(
-        functools.partial(plane_kernel, rows, cols, tiles),
-        out_shape=shapes,
-        in_specs=[vmem] * len(operands),
-        out_specs=(vmem,) * len(shapes),
-        scratch_shapes=scratch,
-        compiler_params=pltpu.CompilerParams(
-            collective_id=collective_id, has_side_effects=True, vmem_limit_bytes=TINY
-        ),
-    )(*operands)
-    return (out[0].reshape(size, width),) + tuple(out[1:])
-
-
 class Chain:
     def __init__(self, place, source, x_ref, panel_ref, sems):
         self.place, self.source, self.x_ref, self.ref = place, source, x_ref, panel_ref
@@ -353,7 +304,7 @@
     def spread(self, first, last):
         @pl.when(self.at_source)
         def _():
-            for chunk in range(first, last):
+            for chunk in range(first, min(last, self.chunks)):
                 if self.source < self.place.planes - 1:
                     self.hop(chunk, 1, 0).start()
                 if self.source > 0:
@@ -585,12 +536,21 @@
         ]
         + Chain.semaphores(tiles, width // CHUNK),
         compiler_params=pltpu.CompilerParams(
-            collective_id=collective_id, has_side_effects=True, vmem_limit_bytes=SMALL
+            collective_id=collective_id, has_side_effects=True, vmem_limit_bytes=56 * MIB
         ),
     )(x4)
 
 
-def next_kernel(rows, cols, gram_in, panel_ref, x_ref, inverse_ref, shifted_ref, sign_ref, cols_ref, *refs):
+def next_kernel(rows, cols, below, *refs):
+    refs = list(refs)
+    take = lambda count: [refs.pop(0) for _ in range(count)]
+    (
+        vec_rows, applied_rows, vec_cols, applied, transform_ref, inner_ref, applied_next,
+        old_ref, later_ref, x_ref,
+    ) = take(10)
+    inverse_ref, shifted_ref, sign_ref, panel_ref, cols_ref = take(5)
+    old_high, old_low, new_high, new_low, update_ref, ahead_ref = take(6)
+    gram_in, gram_sum = take(2)
     near, near_sum, parts, gram_ref, top_ref = refs[:5]
     near_send, near_recv, line_send, line_recv, send_two, recv_two = refs[5:11]
     top_line_send, top_line_recv, top_send, top_recv = refs[11:15]
@@ -601,6 +561,34 @@
     chain = Chain(place, 1, x_ref, cols_ref, refs[15:])
     chain.start()
     place.greet()
+    chain.share()
+    chain.spread(0, 2 * EARLY)
+    size = BAND
+    half = 0.5 * mm(transform_ref[...], inner_ref[...], 0, 0)
+    ahead_ref[...] = applied_next[...] - mm(half, old_ref[...], 0, 1)
+    gram_sum[...] = jnp.zeros_like(gram_sum)
+
+    def own_rows(index, carry):
+        here = pl.ds(pl.multiple_of(index * tile, tile), tile)
+        vec = vec_rows[here, :]
+        change = applied_rows[here, :] - mm(vec, half, 1, 0)
+        panel = later_ref[here, :] - mm(vec, ahead_ref[...], 1, 0) - mm(change, old_ref[...], 1, 1)
+        first = (index * rows + place.row) * tile
+        panel = jnp.where(first >= below + BAND, panel, 0.0)
+        panel_ref[here, :] = panel
+        gram_sum[...] += mm(panel, panel, 0, 0)
+        for start, value in ((0, vec), (size, change)):
+            high, low = split(value)
+            old_high[here, start : start + size] = high
+            old_low[here, start : start + size] = low
+        return carry
+
+    lax.fori_loop(0, panel_ref.shape[0] // tile, own_rows, 0)
+    height = gram_in.shape[2]
+    for col in range(cols):
+        for core in range(2):
+            start = (2 * col + core) * height
+            gram_in[col, core] = gram_sum[start : start + height, :]
     swap = remote(
         gram_in.at[place.col, 1 - place.core], near.at[0], near_send.at[0], near_recv.at[0],
         place.other, place.col,
@@ -642,8 +630,20 @@
         top_first.start()
         target[...] = block[...]
 
-    chain.share()
-    chain.spread(0, chain.chunks)
+    chain.spread(2 * EARLY, chain.chunks)
+
+    def own_cols(index, carry):
+        here = pl.ds(pl.multiple_of(index * 2 * tile, 2 * tile), 2 * tile)
+        vec = vec_cols[:, here]
+        change = applied[:, here] - mm(half, vec, 0, 0)
+        update_ref[:, here] = change
+        for start, value in ((0, change), (size, vec)):
+            high, low = split(value)
+            new_high[start : start + size, here] = high
+            new_low[start : start + size, here] = low
+        return carry
+
+    lax.fori_loop(0, x_ref.shape[1] // 2, own_cols, 0)
     total = near_sum[0]
     for slot, copy in enumerate(line):
         copy.wait_recv()
@@ -664,7 +664,6 @@
         top_near.wait_recv()
         return top_ref[...]
 
-    size = inverse_ref.shape[0]
     orthogonal_top(
         gram_ref[...].reshape(size, size), top, 1, inverse_ref, shifted_ref, sign_ref,
         later_steps(chain, 0, 3),
@@ -682,32 +681,43 @@
     chain.finish()
 
 
-def next_panel(gram, panel_rows, x4, collective_id):
+def next_panel(operands, x4, below, collective_id):
     rows, cols = lax.axis_size("row"), lax.axis_size("col")
-    _, tiles, _, tile = x4.shape
+    row_count, tiles, _, tile = x4.shape
     width = tiles * tile
     count = 2 * cols
     piece = (BAND // count, BAND)
     planes = rows // 2
     vmem = pl.BlockSpec(memory_space=pltpu.VMEM)
     dma = pltpu.SemaphoreType.DMA
-    square = jax.ShapeDtypeStruct((BAND, BAND), x4.dtype)
+    f32, bf16 = jnp.float32, jnp.bfloat16
+    shape = jax.ShapeDtypeStruct
+    square = shape((BAND, BAND), f32)
     return pl.pallas_call(
-        functools.partial(next_kernel, rows, cols),
+        functools.partial(next_kernel, rows, cols, below),
         out_shape=(
             square,
             square,
-            jax.ShapeDtypeStruct((1, BAND), x4.dtype),
-            jax.ShapeDtypeStruct((BAND, width), x4.dtype),
+            shape((1, BAND), f32),
+            shape((row_count, BAND), f32),
+            shape((BAND, width), f32),
+            shape((row_count, 2 * BAND), bf16),
+            shape((row_count, 2 * BAND), bf16),
+            shape((2 * BAND, width), bf16),
+            shape((2 * BAND, width), bf16),
+            shape((BAND, width), f32),
+            square,
         ),
-        in_specs=[vmem, vmem, pl.BlockSpec(memory_space=pltpu.HBM)],
-        out_specs=(vmem,) * 4,
+        in_specs=[vmem] * len(operands) + [pl.BlockSpec(memory_space=pltpu.HBM)],
+        out_specs=(vmem,) * 11,
         scratch_shapes=[
-            pltpu.VMEM((1,) + piece, x4.dtype),
-            pltpu.VMEM((1,) + piece, x4.dtype),
-            pltpu.VMEM((planes - 1,) + piece, x4.dtype),
-            pltpu.VMEM((count,) + piece, x4.dtype),
-            pltpu.VMEM((BAND, BAND), x4.dtype),
+            pltpu.VMEM((cols, 2) + piece, f32),
+            pltpu.VMEM((BAND, BAND), f32),
+            pltpu.VMEM((1,) + piece, f32),
+            pltpu.VMEM((1,) + piece, f32),
+            pltpu.VMEM((planes - 1,) + piece, f32),
+            pltpu.VMEM((count,) + piece, f32),
+            pltpu.VMEM((BAND, BAND), f32),
             dma((1,)),
             dma((1,)),
             dma((planes - 1,)),
@@ -721,9 +731,9 @@
         ]
         + Chain.semaphores(tiles, width // CHUNK),
         compiler_params=pltpu.CompilerParams(
-            collective_id=collective_id, has_side_effects=True, vmem_limit_bytes=SMALL
+            collective_id=collective_id, has_side_effects=True, vmem_limit_bytes=44 * MIB
         ),
-    )(gram.reshape((cols, 2) + piece), panel_rows, x4)
+    )(*operands, x4)
 
 
 def split(value):
@@ -740,24 +750,30 @@
     return jnp.dot(a, b, preferred_element_type=jnp.float32)
 
 
-def apply_kernel(rows, cols, fixed, *refs):
+def apply_kernel(rows, cols, below, tiles, fixed, *refs):
     place = Place(rows, cols)
-    x_ref, left_ref, shifted_ref, sign_ref = refs[:4]
-    if fixed:
-        old_high, old_low, new_high, new_low = refs[4:8]
-        kept_ref, store = refs[11], refs[-1]
-        refs = refs[:8] + refs[8:11] + refs[12:-1]
-    refs = refs[8 if fixed else 4 :]
-    out_ref, row_ref, transform_ref = refs[:3]
-    block, part, near, pair, left_in, right_in, left_out, right_out = refs[3:11]
+    refs = list(refs)
+    take = lambda count: [refs.pop(0) for _ in range(count)]
+    x_ref, left_ref, shifted_ref, sign_ref, inverse_ref, panel_ref = take(6)
+    old_high, old_low, new_high, new_low = take(4) if fixed else [None] * 4
+    row_ref, transform_ref, vec_ref, applied_ref, inner_ref = take(5)
+    next_ref = take(1)[0] if tiles else None
+    kept_ref = take(1)[0] if fixed else None
+    block, part, near, pair, left_in, right_in, left_out, right_out, out_ref = take(9)
+    total_ref, stack, parts = take(3)
     (
         load, near_send, near_recv, left_send, left_recv, right_send, right_recv,
-        both_send, both_recv, row_send, row_recv,
-    ) = refs[11:]
+        both_send, both_recv, row_send, row_recv, send_one, recv_one, send_two, recv_two,
+    ) = take(15)
+    next_sems = take(2) if tiles else None
+    store = take(1)[0] if fixed else None
     plane, core, planes = place.plane, place.core, place.planes
     tile = x_ref.shape[-1]
     chunks = block.shape[0]
-    half = left_ref.shape[0] // 2
+    pieces = pair.shape[0] // chunks
+    depth = pair.shape[1]
+    subs = chunks * pieces
+    size = left_ref.shape[0] // 2
 
     def load_of(chunk, index):
         return pltpu.make_async_copy(
@@ -765,9 +781,6 @@
             block.at[chunk, :, pl.ds(index * tile, tile)],
             load.at[chunk, index],
         )
-
-    row_count = x_ref.shape[0]
-    group = row_count // 5 if row_count % 40 == 0 else row_count
 
     def store_of(chunk, index):
         return pltpu.make_async_copy(
@@ -791,53 +804,52 @@
             place.col,
         )
 
-    def rightward(source, chunk):
+    def rightward(source, index):
         return remote(
-            source.at[chunk], left_in.at[chunk], right_send.at[chunk], left_recv.at[chunk],
+            source.at[index], left_in.at[index], right_send.at[index], left_recv.at[index],
             lax.rem(place.row + 2, rows), place.col,
         )
 
-    def leftward(source, chunk):
+    def leftward(source, index):
         return remote(
-            source.at[chunk], right_in.at[chunk], left_send.at[chunk], right_recv.at[chunk],
+            source.at[index], right_in.at[index], left_send.at[index], right_recv.at[index],
             lax.rem(place.row + rows - 2, rows), place.col,
         )
 
     def joined(chunk):
         near_of(chunk).wait_recv()
-        pair[chunk] = part[chunk, core] + near[chunk]
+        for piece in range(pieces):
+            pair[chunk * pieces + piece] = part[chunk, core, piece] + near[chunk, piece]
 
         @pl.when(plane == 0)
         def _():
-            rightward(pair, chunk).start()
+            for piece in range(pieces):
+                rightward(pair, chunk * pieces + piece).start()
 
         @pl.when(plane == planes - 1)
         def _():
-            leftward(pair, chunk).start()
+            for piece in range(pieces):
+                leftward(pair, chunk * pieces + piece).start()
 
     def product(chunk, carry):
         for index in range(2):
             load_of(chunk, index).wait()
         if fixed:
             here = pl.ds(pl.multiple_of(chunk * 2 * tile, 2 * tile), 2 * tile)
-
-            def rows_of(number, inner):
-                rows_here = pl.ds(pl.multiple_of(number * group, 8), group)
-                high, low = old_high[rows_here, :], old_low[rows_here, :]
-                change = dot(high, new_high[:, here]) + (
-                    dot(low, new_high[:, here]) + dot(high, new_low[:, here])
-                )
-                block[chunk, rows_here, :] = block[chunk, rows_here, :] - change
-                return inner
-
-            lax.fori_loop(0, row_count // group, rows_of, 0)
+            change = dot(old_high[...], new_high[:, here]) + (
+                dot(old_low[...], new_high[:, here]) + dot(old_high[...], new_low[:, here])
+            )
+            block[chunk] = block[chunk] - change
             for index in range(2):
                 store_of(chunk, index).start()
         high, low = split(block[chunk])
         value = dot(left_ref[...], high)
-        value = value[:half] + (value[half:] + dot(left_ref[:half], low))
-        part[chunk, 0] = value[:, :tile]
-        part[chunk, 1] = value[:, tile:]
+        value = value[:size] + (value[size:] + dot(left_ref[:size], low))
+        for index in range(2):
+            for piece in range(pieces):
+                part[chunk, index, piece] = value[
+                    piece * depth : (piece + 1) * depth, index * tile : (index + 1) * tile
+                ]
         near_of(chunk).start()
 
         @pl.when(chunk > 0)
@@ -857,22 +869,25 @@
     target_row = 2 * plane + lax.rem(place.col, 2)
     to_self = target_row == place.row
 
-    def spot(chunk):
-        start = pl.multiple_of((2 * chunk + core) * tile, tile)
-        return out_ref.at[:, pl.ds(start, tile)]
-
-    def both_of(chunk):
+    def depths(index):
+        return pl.ds(pl.multiple_of(lax.rem(index, pieces) * depth, depth), depth)
+
+    def lanes(index):
+        return pl.ds(pl.multiple_of((2 * (index // pieces) + core) * tile, tile), tile)
+
+    def row_lanes(index):
+        return pl.ds(pl.multiple_of(index // pieces * tile, tile), tile)
+
+    def both_of(index):
+        spot = out_ref.at[depths(index), lanes(index)]
+        return remote(spot, spot, both_send.at[index], both_recv.at[index], place.other, place.col)
+
+    def row_of(index, step):
         return remote(
-            spot(chunk), spot(chunk), both_send.at[chunk], both_recv.at[chunk], place.other, place.col
-        )
-
-    def row_of(chunk, step):
-        start = pl.multiple_of(chunk * tile, tile)
-        return remote(
-            spot(chunk),
-            row_ref.at[:, pl.ds(start, tile)],
-            row_send.at[chunk, step],
-            row_recv.at[chunk],
+            out_ref.at[depths(index), lanes(index)],
+            row_ref.at[depths(index), row_lanes(index)],
+            row_send.at[index, step],
+            row_recv.at[index],
             target_row,
             lax.rem(place.col + step, cols),
         )
@@ -880,7 +895,7 @@
     def chain(step, carry):
         index = step - left_lag
 
-        @pl.when((plane > 0) & (index >= 0) & (index < chunks))
+        @pl.when((plane > 0) & (index >= 0) & (index < subs))
         def _():
             rightward(pair, index).wait_recv()
 
@@ -891,7 +906,7 @@
 
         other = step - right_lag
 
-        @pl.when((plane < planes - 1) & (other >= 0) & (other < chunks))
+        @pl.when((plane < planes - 1) & (other >= 0) & (other < subs))
         def _():
             leftward(pair, other).wait_recv()
 
@@ -902,21 +917,19 @@
 
         done = step - last_lag
 
-        @pl.when((done >= 0) & (done < chunks))
-        def _():
-            here = pl.ds(pl.multiple_of((2 * done + core) * tile, tile), tile)
-
+        @pl.when((done >= 0) & (done < subs))
+        def _():
             @pl.when(plane == 0)
             def _():
-                out_ref[:, here] = pair[done] + right_in[done]
+                out_ref[depths(done), lanes(done)] = pair[done] + right_in[done]
 
             @pl.when(plane == planes - 1)
             def _():
-                out_ref[:, here] = left_in[done] + pair[done]
+                out_ref[depths(done), lanes(done)] = left_in[done] + pair[done]
 
             @pl.when((plane > 0) & (plane < planes - 1))
             def _():
-                out_ref[:, here] = right_out[done] + right_in[done]
+                out_ref[depths(done), lanes(done)] = right_out[done] + right_in[done]
 
             both_of(done).start()
 
@@ -927,8 +940,7 @@
 
                 @pl.when(to_self)
                 def _():
-                    there = pl.ds(pl.multiple_of(done * tile, tile), tile)
-                    row_ref[:, there] = out_ref[:, here]
+                    row_ref[depths(done), row_lanes(done)] = out_ref[depths(done), lanes(done)]
 
                 @pl.when(jnp.logical_not(to_self))
                 def _():
@@ -936,87 +948,169 @@
 
         return carry
 
-    steps = chunks + planes - 2
+    steps = subs + planes - 2
     count = [0, 0]
 
     def hook():
         count[0] += 1
-        if count[0] % 2 == 0 and count[1] < steps:
+        if count[0] % 3 == 0 and count[1] < steps:
             chain(count[1], 0)
             count[1] += 1
 
     transform_ref[...] = block_transform(shifted_ref[...], sign_ref[...], hook)
-    if count[1] < steps:
-        lax.fori_loop(count[1], steps, chain, 0)
-
+    total_ref[...] = jnp.zeros_like(total_ref)
+    diagonal = lax.broadcasted_iota(jnp.int32, (size, size), 0)
+    lane = lax.broadcasted_iota(jnp.int32, (size, 2 * tile), 1)
+    band = lax.broadcasted_iota(jnp.int32, (size, 2 * tile), 0)
+    sign_column = jnp.sum(
+        jnp.where(diagonal == lax.broadcasted_iota(jnp.int32, (size, size), 1), sign_ref[...], 0.0),
+        axis=1,
+        keepdims=True,
+    )
+
+    def finished(chunk):
+        for piece in range(pieces):
+            both_of(chunk * pieces + piece).wait_recv()
+        here = pl.ds(pl.multiple_of(chunk * 2 * tile, 2 * tile), 2 * tile)
+        second = jnp.where(lane >= tile, 1, 0)
+        place_of = ((2 * chunk + second) * cols + place.col) * tile + lane - second * tile - below
+        vec = mm(inverse_ref[...], jnp.where(place_of >= 0, panel_ref[:, here], 0.0), 1, 0)
+        vec = vec - jnp.where(place_of == band, sign_column, 0.0)
+        vec_ref[:, here] = vec
+        applied = mm(transform_ref[...], out_ref[:, here], 0, 0)
+        applied_ref[:, here] = applied
+        total_ref[...] += mm(vec, applied, 1, 1)
+
+    done_steps = count[1]
+    early = 0
+    while early < chunks and pieces * (early + 1) + planes - 2 <= done_steps + early + 1 and done_steps + early < steps:
+        early += 1
+
+    def paired(chunk, carry):
+        chain(done_steps + chunk, 0)
+        finished(chunk)
+        return carry
+
+    def alone(chunk, carry):
+        finished(chunk)
+        return carry
+
+    lax.fori_loop(0, early, paired, 0)
+    if done_steps + early < steps:
+        lax.fori_loop(done_steps + early, steps, chain, 0)
+    if early < chunks:
+        lax.fori_loop(early, chunks, alone, 0)
+
+    height = stack.shape[1]
+    for piece in range(stack.shape[0]):
+        stack[piece] = total_ref[piece * height : (piece + 1) * height, :]
+    if tiles:
+        spread = Spread(place, applied_ref, tiles, next_ref, *next_sems)
+        spread.send()
+    plane_scatter(place, place.peers()[: cols - 1], stack, parts, inner_ref, send_one, recv_one)
+    gathers = plane_gather(place, inner_ref.at[place.me], send_two, recv_two)
     gets = jnp.logical_not(source & to_self)
 
-    def drain(chunk, carry):
+    def drain(index, carry):
+        both_of(index).wait_send()
+
+        @pl.when(plane < planes - 1)
+        def _():
+            rightward(pair, index).wait_send()
+
+        @pl.when(plane > 0)
+        def _():
+            leftward(pair, index).wait_send()
+
+        @pl.when(source)
+        def _():
+            for step in range(1, cols):
+                row_of(index, step).wait_send()
+
+            @pl.when(jnp.logical_not(to_self))
+            def _():
+                row_of(index, 0).wait_send()
+
+        @pl.when(gets)
+        def _():
+            row_of(index, 0).wait_recv()
+
+        return carry
+
+    def drain_chunk(chunk, carry):
         if fixed:
             for index in range(2):
                 store_of(chunk, index).wait()
         near_of(chunk).wait_send()
-        both_of(chunk).wait()
-
-        @pl.when(plane < planes - 1)
-        def _():
-            rightward(pair, chunk).wait_send()
-
-        @pl.when(plane > 0)
-        def _():
-            leftward(pair, chunk).wait_send()
-
-        @pl.when(source)
-        def _():
-            for step in range(1, cols):
-                row_of(chunk, step).wait_send()
-
-            @pl.when(jnp.logical_not(to_self))
-            def _():
-                row_of(chunk, 0).wait_send()
-
-        @pl.when(gets)
-        def _():
-            row_of(chunk, 0).wait_recv()
-
         return carry
 
-    lax.fori_loop(0, chunks, drain, 0)
-
-
-def apply(x4, left, shifted, signs, more, collective_id):
+    lax.fori_loop(0, subs, drain, 0)
+    lax.fori_loop(0, chunks, drain_chunk, 0)
+    for copy in gathers:
+        copy.wait()
+    if tiles:
+        spread.wait()
+        spread.finish()
+
+
+PIECES = 2
+
+
+def apply(x4, left, shifted, signs, inverse, panel_cols, below, tiles, more, collective_id):
     rows, cols = lax.axis_size("row"), lax.axis_size("col")
-    row_count, tiles, _, tile = x4.shape
-    width = tiles * tile
-    chunks = tiles // 2
+    row_count, held_tiles, _, tile = x4.shape
+    width = held_tiles * tile
+    chunks = held_tiles // 2
+    count = 2 * cols
     vmem = pl.BlockSpec(memory_space=pltpu.VMEM)
     hbm = pl.BlockSpec(memory_space=pltpu.HBM)
     dma = pltpu.SemaphoreType.DMA
-    piece = (BAND, tile)
+    f32 = jnp.float32
+    piece = (BAND // PIECES, tile)
+    subs = PIECES * chunks
+    sums = (count, BAND // count, BAND)
     kept = bool(more)
+    square = jax.ShapeDtypeStruct((BAND, BAND), f32)
+    wide = jax.ShapeDtypeStruct((BAND, width), f32)
     shapes = (
-        jax.ShapeDtypeStruct((BAND, width), jnp.float32),
-        jax.ShapeDtypeStruct((BAND, row_count), jnp.float32),
-        jax.ShapeDtypeStruct((BAND, BAND), jnp.float32),
+        jax.ShapeDtypeStruct((BAND, row_count), f32),
+        square,
+        wide,
+        wide,
+        jax.ShapeDtypeStruct(sums, f32),
     )
-    return pl.pallas_call(
-        functools.partial(apply_kernel, rows, cols, kept),
+    shapes += (square,) if tiles else ()
+    out = pl.pallas_call(
+        functools.partial(apply_kernel, rows, cols, below, tiles, kept),
         out_shape=shapes + ((jax.ShapeDtypeStruct(x4.shape, x4.dtype),) if kept else ()),
-        in_specs=[hbm] + [vmem] * (3 + len(more)),
-        out_specs=(vmem,) * 3 + ((hbm,) if kept else ()),
+        in_specs=[hbm] + [vmem] * (5 + len(more)),
+        out_specs=(vmem,) * len(shapes) + ((hbm,) if kept else ()),
         scratch_shapes=[
-            pltpu.VMEM((chunks, row_count, 2 * tile), jnp.float32),
-            pltpu.VMEM((chunks, 2) + piece, jnp.float32),
+            pltpu.VMEM((chunks, row_count, 2 * tile), f32),
+            pltpu.VMEM((chunks, 2, PIECES) + piece, f32),
+            pltpu.VMEM((chunks, PIECES) + piece, f32),
         ]
-        + [pltpu.VMEM((chunks,) + piece, jnp.float32)] * 6
-        + [dma((chunks, 2))]
-        + [dma((chunks,))] * 8
-        + [dma((chunks, cols)), dma((chunks,))]
+        + [pltpu.VMEM((subs,) + piece, f32)] * 5
+        + [
+            pltpu.VMEM((BAND, width), f32),
+            pltpu.VMEM((BAND, BAND), f32),
+            pltpu.VMEM(sums, f32),
+            pltpu.VMEM((cols - 1,) + sums[1:], f32),
+        ]
+        + [dma((chunks, 2)), dma((chunks,)), dma((chunks,))]
+        + [dma((subs,))] * 6
+        + [dma((subs, cols)), dma((subs,))]
+        + [dma((cols - 1,))] * 2
+        + [dma((count - 1,))] * 2
+        + ([dma((len(tiles), count - 1)), dma((len(tiles), 2))] if tiles else [])
         + ([dma((chunks, 2))] if kept else []),
         compiler_params=pltpu.CompilerParams(
-            collective_id=collective_id, has_side_effects=True, vmem_limit_bytes=(52 if kept else 40) * MIB
+            collective_id=collective_id, has_side_effects=True, vmem_limit_bytes=(60 if kept else 48) * MIB
         ),
-    )(x4, left, shifted, signs, *more)
+    )(x4, left, shifted, signs, inverse, panel_cols, *more)
+    out = list(out)
+    out[4] = out[4].reshape(BAND, BAND)
+    return out
 
 
 def update_kernel(x_ref, left_high, left_low, right_high, right_low, out_ref, block, result, load, store):
@@ -1041,9 +1135,6 @@
         for index in range(2):
             load_of(chunk, index).start()
 
-    rows = x_ref.shape[0]
-    group = rows // 5 if rows % 40 == 0 else rows
-
     def body(chunk, carry):
         slot = lax.rem(chunk, 2)
         for index in range(2):
@@ -1055,17 +1146,10 @@
                 store_of(chunk - 2, index).wait()
 
         here = pl.ds(pl.multiple_of(chunk * 2 * tile, 2 * tile), 2 * tile)
-
-        def rows_of(number, inner):
-            part = pl.ds(pl.multiple_of(number * group, 8), group)
-            high, low = left_high[part, :], left_low[part, :]
-            value = dot(high, right_high[:, here]) + (
-                dot(low, right_high[:, here]) + dot(high, right_low[:, here])
-            )
-            result[slot, part, :] = block[slot, part, :] - value
-            return inner
-
-        lax.fori_loop(0, rows // group, rows_of, 0)
+        value = dot(left_high[...], right_high[:, here]) + (
+            dot(left_low[...], right_high[:, here]) + dot(left_high[...], right_low[:, here])
+        )
+        result[slot] = block[slot] - value
         for index in range(2):
             store_of(chunk, index).start()
 
@@ -1106,10 +1190,8 @@
     row_devices = lax.axis_size("row")
     col_devices = lax.axis_size("col")
     row_index = lax.axis_index("row")
-    col_index = lax.axis_index("col")
     panel_tiles = BAND // tile_size
     assert row_devices == 2 * col_devices and PANELS * panel_tiles <= col_devices
-    high = lax.Precision.HIGH
     x4 = matrix_tiles.reshape(row_count, block_cols, 1, tile_size)
 
     def positions(count, devices, index):
@@ -1117,7 +1199,6 @@
         return (place // tile_size * devices + index) * tile_size + place % tile_size
 
     global_rows = positions(row_count, row_devices, row_index)
-    global_cols = positions(col_count, col_devices, col_index)
     band = jnp.arange(BAND, dtype=jnp.int32)
     inverse, shifted, signs, rows_held, panel_cols = first_panel(x4, 0)
     panel_rows = rows_held[0]
@@ -1126,50 +1207,49 @@
         below = (panel_index + 1) * BAND
         last = panel_index == PANELS - 1
         panel_rows = jnp.where((global_rows >= below)[:, None], panel_rows, 0.0)
-        panel_cols = jnp.where((global_cols >= below)[None, :], panel_cols, 0.0)
         unit_rows = (global_rows[:, None] - below == band[None, :]).astype(jnp.float32)
         unit_rows_t = (band[:, None] == global_rows[None, :] - below).astype(jnp.float32)
-        unit_cols = (band[:, None] == global_cols[None, :] - below).astype(jnp.float32)
-        signs_t = signs.reshape(BAND, 1)
         vec_rows = multiply(panel_rows, inverse, 1, 1) - unit_rows * signs
-        vec_rows_t = multiply(inverse, panel_rows, 1, 1) - unit_rows_t * signs_t
-        vec_cols = multiply(inverse, panel_cols) - unit_cols * signs_t
-        sums, sums_rows, transform, *held = apply(
-            kept, jnp.concatenate(split_outside(vec_rows_t), 0), shifted, signs, more, 1 + panel_index
-        )
-        if held:
-            kept = held[0]
-        applied = multiply(transform, sums, 0, 0)
+        vec_rows_t = multiply(inverse, panel_rows, 1, 1) - unit_rows_t * signs.reshape(BAND, 1)
+        first = below // tile_size
+        sums_rows, transform, vec_cols, applied, inner, *rest = apply(
+            kept,
+            jnp.concatenate(split_outside(vec_rows_t), 0),
+            shifted,
+            signs,
+            inverse,
+            panel_cols,
+            below,
+            () if last else tuple(range(first, first + panel_tiles)),
+            more,
+            1 + panel_index,
+        )
         applied_rows = multiply(sums_rows, transform, 0, 0)
-        inner_part = multiply(vec_cols, applied, 1, 1)
         if last:
-            (inner,) = plane_sum(inner_part, 5)
-        else:
-            first = below // tile_size
-            inner, applied_next = plane_sum(
-                inner_part, 4, applied, tuple(range(first, first + panel_tiles))
-            )
-        half_inner = 0.5 * multiply(transform, inner, 0, 0)
-        update_rows = applied_rows - multiply(vec_rows, half_inner)
-        update_cols = applied - multiply(half_inner, vec_cols, 0, 0)
-        left = split_outside(jnp.concatenate([vec_rows, update_rows], 1))
-        right = split_outside(jnp.concatenate([update_cols, vec_cols], 0))
-        if last:
-            return update(kept, left, right).reshape(tile_shape)
-        more = left + right
-        update_next = applied_next - multiply(half_inner, shifted, 0, 1)
-        panel_rows = (
-            rows_held[panel_index + 1]
-            - multiply(vec_rows, update_next)
-            - multiply(update_rows, shifted, 1, 1)
-        )
-        panel_rows = jnp.where((global_rows >= below + BAND)[:, None], panel_rows, 0.0)
-        gram = multiply(panel_rows, panel_rows, 0, 0)
-        old_shifted = shifted
-        inverse, shifted, signs, panel_cols = next_panel(gram, panel_rows, x4, 3)
+            break
+        old_shifted, old_cols = shifted, vec_cols
+        (
+            inverse, shifted, signs, panel_rows, panel_cols,
+            old_high, old_low, new_high, new_low, update_cols, update_next,
+        ) = next_panel(
+            (
+                vec_rows, applied_rows, vec_cols, applied, transform, inner, rest[0], shifted,
+                rows_held[panel_index + 1],
+            ),
+            x4,
+            below,
+            3,
+        )
+        more = (old_high, old_low, new_high, new_low)
         panel_cols = (
-            panel_cols - multiply(update_next, vec_cols, 0, 0) - multiply(old_shifted, update_cols)
-        )
+            panel_cols - multiply(update_next, old_cols, 0, 0) - multiply(old_shifted, update_cols)
+        )
+    half_inner = 0.5 * multiply(transform, inner, 0, 0)
+    update_rows = applied_rows - multiply(vec_rows, half_inner)
+    update_cols = applied - multiply(half_inner, vec_cols, 0, 0)
+    left = split_outside(jnp.concatenate([vec_rows, update_rows], 1))
+    right = split_outside(jnp.concatenate([update_cols, vec_cols], 0))
+    return update(rest[0], left, right).reshape(tile_shape)
 
 
 def solution(mesh):

time: 366 us -> 398 us (1.087)
  Pallas kernels: 296 us -> 354 us
  matrix products: 46 us -> 24.5 us
  other arithmetic: 10.5 us -> 5.48 us
    pallas_call x5 -> x3, Pallas kernels: 218 us -> 279 us  [the longest x2 234 us: apply(): pl.pallas_call(functools.partial(apply_kernel, rows, cols, below, tiles,...]
    dot_general x23 -> x10, matrix products: 46 us -> 24.5 us  [multiply(): lax.dot_general(first, second, (((first_dim,), (second_dim,)), ((), ())),...]
    convert_element_type x4 -> x2, other arithmetic: 7.59 us -> 2.6 us  [split_outside(): return (high.astype(jnp.bfloat16), (value - high).astype(jnp.bfloat16))]
    pallas_call x1, Pallas kernels: 23.2 us -> 19 us  [update(): pl.pallas_call(update_kernel, out_shape=jax.ShapeDtypeStruct(x4.shape, x4...]
where the time goes in v3:
time: 398 us; the launch traced here: 392 us
  Pallas kernels  354 us (89%)
  matrix products  24.5 us (6%)
  local copies, waits for them, and re-layouts  6.91 us (2%)
  other arithmetic  5.48 us (1%)
    pallas_call x2, Pallas kernels, apply(): pl.pallas_call(functools.partial(apply_kernel, rows, cols, below, tiles,...  234 us
    pallas_call x1, Pallas kernels, first_panel(): pl.pallas_call(functools.partial(first_kernel, rows, cols), out_shape=(sq...  56.8 us
    pallas_call x1, Pallas kernels, next_panel(): pl.pallas_call(functools.partial(next_kernel, rows, cols, below), out_sha...  44.9 us
    dot_general x10, matrix products, multiply(): lax.dot_general(first, second, (((first_dim,), (second_dim,)), ((), ())),...  24.5 us
    pallas_call x1, Pallas kernels, update(): pl.pallas_call(update_kernel, out_shape=jax.ShapeDtypeStruct(x4.shape, x4...  19 us

profile of v3, /device:TPU:0, one launch (start us, length us, event | category | flops | bytes accessed | tf_op | source)
XLA Modules:
  0.0 392.0 jit_solution(7829388640939478024)
XLA Ops:
  0.0 56.8 %shard_map.17 = (f32[256,256]{1,0:T(8,128)}, f32[256,256]{1,0:T(8,128)}, f32[1,256]{1,0:T(1,128)}, f32[2,1280,256]{2,1,0:T(8,128)}, f32[256,2560]{1,0:T(8,128)}) custom-call(f32[1280,20,1,128]{3,2,1,0:T(1,128)} %bitcast.43), custom_call_target="tpu_custom_call" | custom-call | tf_op jit(solution)/shard_map/pallas_call | solution.py:509
  56.8 0.0 copy-start.4
  56.8 0.0 copy-start.6
  56.9 1.4 slice_bitcast_fusion.refs_8_
  58.3 0.0 copy-done.4
  58.3 0.0 copy-done.6
  58.3 4.0 %reduce-precision_convert_fusion.3 = (bf16[256,1280]{1,0:T(8,128)(2,1)S(1)}, bf16[256,1280]{1,0:T(8,128)(2,1)S(1)}, f32[1280,256]{0,1:T(8,128)}) fusion(f32[256]{0:T(256)S(1)} %bitcast.39, s32[1280]{0:T(1024)S(1)} %get-tuple-element.71, f32[256,256]{1,0:T(8,128)S(1)} %copy-done.4, f32[2,1280,256]{2,1,0:T(8,128)} %get-tuple-element.33, ...), kind=kOutput, calls=%fused_computation.18 | convolution fusion | flops 1009254400 | bytes 4201728 | tf_op jit(solution)/shard_map/dot_general | solution.py:103
  62.3 0.1 pad_maximum_fusion.2.refs_1_
  62.4 2.8 copy.2
  65.2 0.0 copy-start
  65.2 1.6 select_subtract_fusion.refs_0_
  66.8 0.0 copy-done
  66.8 101.6 %shard_map.18 = (f32[256,1280]{1,0:T(8,128)S(1)}, f32[256,256]{1,0:T(8,128)S(1)}, f32[256,2560]{1,0:T(8,128)}, f32[256,2560]{1,0:T(8,128)}, f32[8,32,256]{2,1,0:T(8,128)S(1)}, /*index=5*/f32[256,256]{1,0:T(8,128)S(1)}) custom-call(f32[1280,20,1,128]{3,2,1,0:T(1,128)} %bitcast.44, bf16[512,1280]{1,0:T(8,128)(2,1)S(1)} %pad_maximum_fusion.2.refs_1_, ...), custom_call_target="tpu_custom_call" | custom-call | tf_op jit(solution)/shard_map/pallas_call | solution.py:1083
  168.4 2.3 fusion.29.refs_1_
  170.6 44.9 %shard_map.19 = (f32[256,256]{1,0:T(8,128)S(1)}, f32[256,256]{1,0:T(8,128)S(1)}, f32[1,256]{1,0:T(1,128)S(1)}, f32[1280,256]{1,0:T(8,128)S(1)}, f32[256,2560]{1,...) custom-call(f32[1280,256]{1,0:T(8,128)S(1)} %select_subtract_fusion., ...), custom_call_target="tpu_custom_call" | custom-call | tf_op jit(solution)/shard_map/pallas_call | solution.py:696
  215.5 0.0 copy-start.5
  215.6 0.7 copy-done.5
  216.2 0.0 copy-start.1
  216.3 0.0 copy-start.2
  216.3 0.0 copy-start.3
  216.3 0.0 copy-start.7
  216.3 1.2 convolution_subtract_fusion.3
  217.5 0.0 copy-done.1
  217.5 0.3 copy-done.2
  217.8 0.1 copy-done.3
  217.9 0.0 copy-done.7
  217.9 1.6 reduce-precision_convert_fusion.2
  219.5 0.0 copy-start.10
  219.5 1.2 pad_maximum_fusion.3.refs_1_
  220.7 1.0 copy-done.10
  221.7 0.0 copy-start.9
  221.7 0.0 copy-start.12
  221.7 2.5 convolution_bitcast_fusion
  224.2 0.0 copy-done.9
  224.2 0.0 copy-done.12
  224.2 4.0 %fusion.1.refs_5_ = f32[256,2560]{1,0:T(8,128)} fusion(f32[256,2560]{1,0:T(8,128)S(1)} %convolution_bitcast_fusion, f32[256,2560]{1,0:T(8,128)S(1)} %copy-done.12, f32[256,256]{1,0:T(8,128)S(1)} %get-tuple-element.49, f32[256,2560]{1,0:T(8,128)S(1)} %copy-done.9), kind=kOutput, calls=%fused_computation.6 | convolution fusion | flops 2014576640 | bytes 10747904 | tf_op jit(solution)/shard_map/dot_general | solution.py:103
  228.3 132.2 %shard_map.20 = (f32[256,1280]{1,0:T(8,128)}, f32[256,256]{1,0:T(8,128)}, f32[256,2560]{1,0:T(8,128)}, f32[256,2560]{1,0:T(8,128)}, f32[8,32,256]{2,1,0:T(8,128)}, /*index=5*/f32[1280,20,1,128]{3,2,1,0:T(1,128)}) custom-call(f32[1280,20,1,128]{3,2,1,0:T(1,128)} %bitcast.46, bf16[512,1280]{1,0:T(8,128)(2,1)} %pad_maximum_fusion.3.refs_1_, ...), custom_call_target="tpu_custom_call" | custom-call | tf_op jit(solution)/shard_map/pallas_call | solution.py:1083
  360.4 1.6 convolution_multiply_fusion
  362.1 0.0 copy-start.11
  362.1 3.7 fusion.30
  365.8 0.0 copy-start.8
  365.8 1.2 convolution_subtract_fusion.2
  367.0 0.0 copy-done.11
  367.0 0.5 copy-done.8
  367.5 2.4 convolution_subtract_fusion
  369.9 2.2 fusion
  372.1 0.4 fusion.2
  372.5 19.0 %shard_map.21 = f32[1280,20,1,128]{3,2,1,0:T(1,128)} custom-call(f32[1280,20,1,128]{3,2,1,0:T(1,128)} %get-tuple-element.55.x_ref, bf16[1280,512]{1,0:T(8,128)(2,1)S(1)} %get-tuple-element.64.left_high, bf16[1280,512]{1,0:T(8,128)(2,1)S(1)} %get-tuple-element.63.left_low, bf16[512,2560]{1,0:T(8,128)(2,1)S(1)} %get-tuple-element.62.right_high, ...), custom_call_target="tpu_custom_call" | custom-call | tf_op jit(solution)/shard_map/pallas_call | solution.py:1174
  (2 shorter events, 0.0 us)
Async XLA Ops:
  56.8 1.5 copy-start.4
  56.8 1.5 copy-start.6
  65.2 1.6 copy-start
  215.5 0.7 copy-start.5
  216.2 1.3 copy-start.1
  216.3 1.6 copy-start.2
  216.3 1.6 copy-start.3
  216.3 1.6 copy-start.7
  219.5 2.2 copy-start.10
  221.7 2.5 copy-start.9
  221.7 2.5 copy-start.12
  362.1 4.9 %copy-start.11 = (f32[256,2560]{1,0:T(8,128)S(1)}, f32[256,2560]{1,0:T(8,128)}, u32[]{:S(2)}) copy-start(f32[256,2560]{1,0:T(8,128)} %get-tuple-element.59) | copy-start | bytes 7864324
  365.8 1.7 copy-start.8

commit v4 on v3

--- a/solution.py
+++ b/solution.py
@@ -96,7 +96,16 @@
     rows = lax.broadcasted_iota(jnp.int32, (size, size), 0)
     cols = lax.broadcasted_iota(jnp.int32, (size, size), 1)
     sign_column = jnp.sum(jnp.where(rows == cols, signs, 0.0), axis=1, keepdims=True)
-    return -sign_column * mm(mm(shifted, outer, 1, 1), outer, 1, 0)
+    return -mm(outer, mm(outer, shifted * sign_column, 1, 1), 0, 0)
+
+
+def mm3(a, b, ca=1, cb=0):
+    def part(x, y):
+        return lax.dot_general(
+            x, y, (((ca,), (cb,)), ((), ())), preferred_element_type=jnp.float32
+        )
+
+    return part(a[0], b[0]) + (part(a[0], b[1]) + part(a[1], b[0]))
 
 
 def multiply(first, second, first_dim=1, second_dim=0, precision=HI):
@@ -562,33 +571,33 @@
     chain.start()
     place.greet()
     chain.share()
-    chain.spread(0, 2 * EARLY)
+    chain.spread(0, EARLY)
+    half_full = 0.5 * mm(transform_ref[...], inner_ref[...], 1, 0)
+    half = split(half_full)
+    old = old_ref[...]
+    ahead = applied_next[...] - mm(half_full, old, 0, 1)
+    ahead_ref[...] = ahead
+    vec = vec_rows[...]
+    vec_parts = split(vec)
+    change = applied_rows[...] - mm3(vec_parts, half)
+    panel = later_ref[...] - mm(vec, ahead, 1, 0) - mm(change, old, 1, 1)
+    lines = lax.broadcasted_iota(jnp.int32, panel.shape, 0)
+    above = (below + BAND) // tile
+    limit = (above // rows + jnp.where(place.row < above % rows, 1, 0)) * tile
+    panel = jnp.where(lines >= limit, panel, 0.0)
+    panel_ref[...] = panel
+    gram_sum[...] = mm(panel, panel, 0, 0)
+    change_parts = split(change)
+    for start, value in ((0, vec_parts), (BAND, change_parts)):
+        old_high[:, start : start + BAND] = value[0]
+        old_low[:, start : start + BAND] = value[1]
     size = BAND
-    half = 0.5 * mm(transform_ref[...], inner_ref[...], 0, 0)
-    ahead_ref[...] = applied_next[...] - mm(half, old_ref[...], 0, 1)
-    gram_sum[...] = jnp.zeros_like(gram_sum)
-
-    def own_rows(index, carry):
-        here = pl.ds(pl.multiple_of(index * tile, tile), tile)
-        vec = vec_rows[here, :]
-        change = applied_rows[here, :] - mm(vec, half, 1, 0)
-        panel = later_ref[here, :] - mm(vec, ahead_ref[...], 1, 0) - mm(change, old_ref[...], 1, 1)
-        first = (index * rows + place.row) * tile
-        panel = jnp.where(first >= below + BAND, panel, 0.0)
-        panel_ref[here, :] = panel
-        gram_sum[...] += mm(panel, panel, 0, 0)
-        for start, value in ((0, vec), (size, change)):
-            high, low = split(value)
-            old_high[here, start : start + size] = high
-            old_low[here, start : start + size] = low
-        return carry
-
-    lax.fori_loop(0, panel_ref.shape[0] // tile, own_rows, 0)
     height = gram_in.shape[2]
     for col in range(cols):
         for core in range(2):
             start = (2 * col + core) * height
             gram_in[col, core] = gram_sum[start : start + height, :]
+    chain.step(0)
     swap = remote(
         gram_in.at[place.col, 1 - place.core], near.at[0], near_send.at[0], near_recv.at[0],
         place.other, place.col,
@@ -630,20 +639,24 @@
         top_first.start()
         target[...] = block[...]
 
-    chain.spread(2 * EARLY, chain.chunks)
+    chain.spread(EARLY, chain.chunks)
+    chain.step(1)
+    group = 5 if x_ref.shape[1] % 10 == 0 else 1
+    wide = x_ref.shape[1] // group * tile
+    half_t = split(half_full.T)
 
     def own_cols(index, carry):
-        here = pl.ds(pl.multiple_of(index * 2 * tile, 2 * tile), 2 * tile)
-        vec = vec_cols[:, here]
-        change = applied[:, here] - mm(half, vec, 0, 0)
+        here = pl.ds(pl.multiple_of(index * wide, wide), wide)
+        vec = split(vec_cols[:, here])
+        change = applied[:, here] - mm3(half_t, vec)
         update_ref[:, here] = change
-        for start, value in ((0, change), (size, vec)):
-            high, low = split(value)
-            new_high[start : start + size, here] = high
-            new_low[start : start + size, here] = low
+        for start, value in ((0, split(change)), (size, vec)):
+            new_high[start : start + size, here] = value[0]
+            new_low[start : start + size, here] = value[1]
         return carry
 
-    lax.fori_loop(0, x_ref.shape[1] // 2, own_cols, 0)
+    lax.fori_loop(0, group, own_cols, 0)
+    chain.step(2)
     total = near_sum[0]
     for slot, copy in enumerate(line):
         copy.wait_recv()
@@ -666,7 +679,7 @@
 
     orthogonal_top(
         gram_ref[...].reshape(size, size), top, 1, inverse_ref, shifted_ref, sign_ref,
-        later_steps(chain, 0, 3),
+        later_steps(chain, 3, 2),
     )
     swap.wait_send()
     for copy in line:
@@ -750,13 +763,13 @@
     return jnp.dot(a, b, preferred_element_type=jnp.float32)
 
 
-def apply_kernel(rows, cols, below, tiles, fixed, *refs):
+def apply_kernel(rows, cols, tiles, fixed, *refs):
     place = Place(rows, cols)
     refs = list(refs)
     take = lambda count: [refs.pop(0) for _ in range(count)]
-    x_ref, left_ref, shifted_ref, sign_ref, inverse_ref, panel_ref = take(6)
+    x_ref, left_ref, shifted_ref, sign_ref, vec_ref = take(5)
     old_high, old_low, new_high, new_low = take(4) if fixed else [None] * 4
-    row_ref, transform_ref, vec_ref, applied_ref, inner_ref = take(5)
+    row_ref, transform_ref, applied_ref, inner_ref = take(4)
     next_ref = take(1)[0] if tiles else None
     kept_ref = take(1)[0] if fixed else None
     block, part, near, pair, left_in, right_in, left_out, right_out, out_ref = take(9)
@@ -856,13 +869,12 @@
         def _():
             joined(chunk - 1)
 
+        for piece in range(pieces):
+            chain((chunk - BEHIND) * pieces + piece, 0)
         return carry
 
-    lax.fori_loop(0, chunks, product, 0)
-    joined(chunks - 1)
-
-    left_lag = jnp.maximum(plane - 1, 0)
-    right_lag = jnp.maximum(planes - 2 - plane, 0)
+    left_lag = HOP * jnp.maximum(plane - 1, 0)
+    right_lag = HOP * jnp.maximum(planes - 2 - plane, 0)
     last_lag = jnp.maximum(left_lag, right_lag)
     held = cols * core + place.col
     source = held // 2 == plane
@@ -948,59 +960,45 @@
 
         return carry
 
-    steps = subs + planes - 2
-    count = [0, 0]
+    lax.fori_loop(0, chunks, product, 0)
+    joined(chunks - 1)
+    steps = subs + HOP * (planes - 2)
+    count = [0, max(chunks - BEHIND, 0) * pieces]
 
     def hook():
         count[0] += 1
-        if count[0] % 3 == 0 and count[1] < steps:
+        if count[0] % 2 == 0 and count[1] < steps:
             chain(count[1], 0)
             count[1] += 1
 
     transform_ref[...] = block_transform(shifted_ref[...], sign_ref[...], hook)
+    if count[1] < steps:
+        lax.fori_loop(count[1], steps, chain, 0)
     total_ref[...] = jnp.zeros_like(total_ref)
-    diagonal = lax.broadcasted_iota(jnp.int32, (size, size), 0)
-    lane = lax.broadcasted_iota(jnp.int32, (size, 2 * tile), 1)
-    band = lax.broadcasted_iota(jnp.int32, (size, 2 * tile), 0)
-    sign_column = jnp.sum(
-        jnp.where(diagonal == lax.broadcasted_iota(jnp.int32, (size, size), 1), sign_ref[...], 0.0),
-        axis=1,
-        keepdims=True,
-    )
-
-    def finished(chunk):
-        for piece in range(pieces):
-            both_of(chunk * pieces + piece).wait_recv()
-        here = pl.ds(pl.multiple_of(chunk * 2 * tile, 2 * tile), 2 * tile)
-        second = jnp.where(lane >= tile, 1, 0)
-        place_of = ((2 * chunk + second) * cols + place.col) * tile + lane - second * tile - below
-        vec = mm(inverse_ref[...], jnp.where(place_of >= 0, panel_ref[:, here], 0.0), 1, 0)
-        vec = vec - jnp.where(place_of == band, sign_column, 0.0)
-        vec_ref[:, here] = vec
-        applied = mm(transform_ref[...], out_ref[:, here], 0, 0)
+    transform = split(transform_ref[...])
+
+    def finished(number, carry):
+        for index in range(2 * pieces):
+            both_of(2 * pieces * number + index).wait_recv()
+        here = pl.ds(pl.multiple_of(number * 4 * tile, 4 * tile), 4 * tile)
+        applied = mm3(transform, split(out_ref[:, here]))
         applied_ref[:, here] = applied
-        total_ref[...] += mm(vec, applied, 1, 1)
-
-    done_steps = count[1]
-    early = 0
-    while early < chunks and pieces * (early + 1) + planes - 2 <= done_steps + early + 1 and done_steps + early < steps:
-        early += 1
-
-    def paired(chunk, carry):
-        chain(done_steps + chunk, 0)
-        finished(chunk)
+        total_ref[...] += mm3(split(vec_ref[:, here]), split(applied), 1, 1)
         return carry
 
-    def alone(chunk, carry):
-        finished(chunk)
+    def finished_one(number, carry):
+        for index in range(pieces):
+            both_of(pieces * number + index).wait_recv()
+        here = pl.ds(pl.multiple_of(number * 2 * tile, 2 * tile), 2 * tile)
+        applied = mm3(transform, split(out_ref[:, here]))
+        applied_ref[:, here] = applied
+        total_ref[...] += mm3(split(vec_ref[:, here]), split(applied), 1, 1)
         return carry
 
-    lax.fori_loop(0, early, paired, 0)
-    if done_steps + early < steps:
-        lax.fori_loop(done_steps + early, steps, chain, 0)
-    if early < chunks:
-        lax.fori_loop(early, chunks, alone, 0)
-
+    if chunks % 2 == 0:
+        lax.fori_loop(0, chunks // 2, finished, 0)
+    else:
+        lax.fori_loop(0, chunks, finished_one, 0)
     height = stack.shape[1]
     for piece in range(stack.shape[0]):
         stack[piece] = total_ref[piece * height : (piece + 1) * height, :]
@@ -1054,9 +1052,11 @@
 
 
 PIECES = 2
-
-
-def apply(x4, left, shifted, signs, inverse, panel_cols, below, tiles, more, collective_id):
+HOP = 3
+BEHIND = 3
+
+
+def apply(x4, left, shifted, signs, vec_cols, tiles, more, collective_id):
     rows, cols = lax.axis_size("row"), lax.axis_size("col")
     row_count, held_tiles, _, tile = x4.shape
     width = held_tiles * tile
@@ -1076,14 +1076,13 @@
         jax.ShapeDtypeStruct((BAND, row_count), f32),
         square,
         wide,
-        wide,
         jax.ShapeDtypeStruct(sums, f32),
     )
     shapes += (square,) if tiles else ()
     out = pl.pallas_call(
-        functools.partial(apply_kernel, rows, cols, below, tiles, kept),
+        functools.partial(apply_kernel, rows, cols, tiles, kept),
         out_shape=shapes + ((jax.ShapeDtypeStruct(x4.shape, x4.dtype),) if kept else ()),
-        in_specs=[hbm] + [vmem] * (5 + len(more)),
+        in_specs=[hbm] + [vmem] * (4 + len(more)),
         out_specs=(vmem,) * len(shapes) + ((hbm,) if kept else ()),
         scratch_shapes=[
             pltpu.VMEM((chunks, row_count, 2 * tile), f32),
@@ -1107,9 +1106,9 @@
         compiler_params=pltpu.CompilerParams(
             collective_id=collective_id, has_side_effects=True, vmem_limit_bytes=(60 if kept else 48) * MIB
         ),
-    )(x4, left, shifted, signs, inverse, panel_cols, *more)
+    )(x4, left, shifted, signs, vec_cols, *more)
     out = list(out)
-    out[4] = out[4].reshape(BAND, BAND)
+    out[3] = out[3].reshape(BAND, BAND)
     return out
 
 
@@ -1199,6 +1198,7 @@
         return (place // tile_size * devices + index) * tile_size + place % tile_size
 
     global_rows = positions(row_count, row_devices, row_index)
+    global_cols = positions(col_count, lax.axis_size("col"), lax.axis_index("col"))
     band = jnp.arange(BAND, dtype=jnp.int32)
     inverse, shifted, signs, rows_held, panel_cols = first_panel(x4, 0)
     panel_rows = rows_held[0]
@@ -1211,20 +1211,21 @@
         unit_rows_t = (band[:, None] == global_rows[None, :] - below).astype(jnp.float32)
         vec_rows = multiply(panel_rows, inverse, 1, 1) - unit_rows * signs
         vec_rows_t = multiply(inverse, panel_rows, 1, 1) - unit_rows_t * signs.reshape(BAND, 1)
+        panel_cols = jnp.where((global_cols >= below)[None, :], panel_cols, 0.0)
+        unit_cols = (band[:, None] == global_cols[None, :] - below).astype(jnp.float32)
+        vec_cols = multiply(inverse, panel_cols) - unit_cols * signs.reshape(BAND, 1)
         first = below // tile_size
-        sums_rows, transform, vec_cols, applied, inner, *rest = apply(
+        sums_rows, transform, applied, inner, *rest = apply(
             kept,
             jnp.concatenate(split_outside(vec_rows_t), 0),
             shifted,
             signs,
-            inverse,
-            panel_cols,
-            below,
+            vec_cols,
             () if last else tuple(range(first, first + panel_tiles)),
             more,
             1 + panel_index,
         )
-        applied_rows = multiply(sums_rows, transform, 0, 0)
+        applied_rows = multiply(sums_rows, transform, 0, 1)
         if last:
             break
         old_shifted, old_cols = shifted, vec_cols
@@ -1244,7 +1245,7 @@
         panel_cols = (
             panel_cols - multiply(update_next, old_cols, 0, 0) - multiply(old_shifted, update_cols)
         )
-    half_inner = 0.5 * multiply(transform, inner, 0, 0)
+    half_inner = 0.5 * multiply(transform, inner)
     update_rows = applied_rows - multiply(vec_rows, half_inner)
     update_cols = applied - multiply(half_inner, vec_cols, 0, 0)
     left = split_outside(jnp.concatenate([vec_rows, update_rows], 1))

time: 398 us -> 339 us (0.85)
  Pallas kernels: 354 us -> 288 us
  matrix products: 24.5 us -> 32.8 us
    pallas_call x2, Pallas kernels: 234 us -> 161 us  [apply(): pl.pallas_call(functools.partial(apply_kernel, rows, cols, tiles, kept),...]
    dot_general x10 -> x12, matrix products: 24.5 us -> 32.8 us  [multiply(): lax.dot_general(first, second, (((first_dim,), (second_dim,)), ((), ())),...]
    pallas_call x1, Pallas kernels: 44.9 us -> 50.7 us  [next_panel(): pl.pallas_call(functools.partial(next_kernel, rows, cols, below), out_sha...]
where the time goes in v4:
time: 339 us; the launch traced here: 333 us
  Pallas kernels  288 us (85%)
  matrix products  32.8 us (10%)
  local copies, waits for them, and re-layouts  5.63 us (2%)
  other arithmetic  5.51 us (2%)
    pallas_call x2, Pallas kernels, apply(): pl.pallas_call(functools.partial(apply_kernel, rows, cols, tiles, kept),...  161 us
    pallas_call x1, Pallas kernels, first_panel(): pl.pallas_call(functools.partial(first_kernel, rows, cols), out_shape=(sq...  56.8 us
    pallas_call x1, Pallas kernels, next_panel(): pl.pallas_call(functools.partial(next_kernel, rows, cols, below), out_sha...  50.7 us
    dot_general x12, matrix products, multiply(): lax.dot_general(first, second, (((first_dim,), (second_dim,)), ((), ())),...  32.8 us
    pallas_call x1, Pallas kernels, update(): pl.pallas_call(update_kernel, out_shape=jax.ShapeDtypeStruct(x4.shape, x4...  19.1 us

profile of v4, /device:TPU:0, one launch (start us, length us, event | category | flops | bytes accessed | tf_op | source)
XLA Modules:
  0.0 332.7 jit_solution(1619895335401872399)
XLA Ops:
  0.1 56.8 %shard_map.17 = (f32[256,256]{1,0:T(8,128)}, f32[256,256]{1,0:T(8,128)}, f32[1,256]{1,0:T(1,128)}, f32[2,1280,256]{2,1,0:T(8,128)}, f32[256,2560]{1,0:T(8,128)}) custom-call(f32[1280,20,1,128]{3,2,1,0:T(1,128)} %bitcast.52), custom_call_target="tpu_custom_call" | custom-call | tf_op jit(solution)/shard_map/pallas_call | solution.py:518
  56.9 0.0 copy-start.10
  56.9 6.4 %fusion.3.refs_4_.refs_2_ = f32[256,2560]{1,0:T(8,128)} fusion(f32[256,256]{1,0:T(8,128)} %get-tuple-element.32, f32[256,2560]{1,0:T(8,128)} %get-tuple-element.35, f32[256]{0:T(256)} %bitcast.46, s32[2560]{0:T(1024)S(1)} %get-tuple-element.71, pred[2560]{0:T(1024)(128)(4,1)S(1)} %get-tuple-element.73), kind=kOutput, calls=%fused_computation.11 | convolution fusion | flops 2015887360 | bytes 5518848 | tf_op jit(solution)/shard_map/dot_general | solution.py:112
  63.3 0.0 copy-done.10
  63.3 0.0 copy-start.4
  63.3 0.0 copy-start.12
  63.3 0.1 slice_bitcast_fusion.refs_8_
  63.4 0.6 copy-done.4
  64.0 0.3 copy-done.12
  64.2 2.6 reduce-precision_convert_fusion.3
  66.9 0.1 pad_maximum_fusion.2.refs_1_
  67.0 2.8 copy.2
  69.8 0.0 copy-start
  69.8 1.6 select_subtract_fusion.refs_0_
  71.4 0.0 copy-done
  71.4 76.4 %shard_map.18 = (f32[256,1280]{1,0:T(8,128)S(1)}, f32[256,256]{1,0:T(8,128)S(1)}, f32[256,2560]{1,0:T(8,128)}, f32[8,32,256]{2,1,0:T(8,128)S(1)}, f32[256,256]{1,0:T(8,128)S(1)}) custom-call(f32[1280,20,1,128]{3,2,1,0:T(1,128)} %bitcast.53, bf16[512,1280]{1,0:T(8,128)(2,1)S(1)} %pad_maximum_fusion.2.refs_1_, f32[256,256]{1,0:T(8,128)S(1)} %copy-done, ...), custom_call_target="tpu_custom_call" | custom-call | tf_op jit(solution)/shard_map/pallas_call | solution.py:1082
  147.8 2.3 fusion.46.refs_1_
  150.1 50.7 %shard_map.19 = (f32[256,256]{1,0:T(8,128)S(1)}, f32[256,256]{1,0:T(8,128)S(1)}, f32[1,256]{1,0:T(1,128)S(1)}, f32[1280,256]{1,0:T(8,128)S(1)}, f32[256,2560]{1,...) custom-call(f32[1280,256]{1,0:T(8,128)S(1)} %select_subtract_fusion., ...), custom_call_target="tpu_custom_call" | custom-call | tf_op jit(solution)/shard_map/pallas_call | solution.py:709
  200.8 0.0 copy-start.1
  200.8 0.0 copy-start.2
  200.8 0.0 copy-start.3
  200.8 0.0 copy-start.5
  200.9 1.2 convolution_subtract_fusion.4
  202.1 0.0 copy-done.1
  202.1 0.2 copy-done.2
  202.3 0.1 copy-done.3
  202.4 1.6 reduce-precision_convert_fusion.2
  204.0 0.0 copy-start.8
  204.0 1.2 pad_maximum_fusion.3.refs_1_
  205.2 1.0 copy-done.8
  206.2 2.6 convolution_bitcast_fusion
  208.9 0.0 copy-done.7
  208.9 0.0 copy-done.11
  208.9 3.0 fusion.2
  211.9 0.0 copy-done.5
  211.9 4.3 %convolution_subtract_fusion.1.refs_4_ = f32[256,2560]{1,0:T(8,128)} fusion(f32[256,256]{1,0:T(8,128)S(1)} %get-tuple-element.41, f32[256,2560]{1,0:T(8,128)S(1)} %fusion.2, f32[256]{0:T(256)S(1)} %bitcast.51, s32[2560]{0:T(1024)S(1)} %get-tuple-element.70), kind=kOutput, calls=%fused_computation.5 | convolution fusion | flops 2015232000 | bytes 5516288 | tf_op jit(solution)/shard_map/dot_general | solution.py:112
  216.2 85.0 %shard_map.20 = (f32[256,1280]{1,0:T(8,128)}, f32[256,256]{1,0:T(8,128)}, f32[256,2560]{1,0:T(8,128)}, f32[8,32,256]{2,1,0:T(8,128)}, f32[1280,20,1,128]{3,2,1,0:T(1,128)}) custom-call(f32[1280,20,1,128]{3,2,1,0:T(1,128)} %bitcast.55, bf16[512,1280]{1,0:T(8,128)(2,1)} %pad_maximum_fusion.3.refs_1_, f32[256,256]{1,0:T(8,128)} %copy-done.3, ...), custom_call_target="tpu_custom_call" | custom-call | tf_op jit(solution)/shard_map/pallas_call | solution.py:1082
  301.2 1.4 convolution_multiply_fusion
  302.6 0.0 copy-start.9
  302.6 3.7 %fusion.47 = f32[1280,256]{1,0:T(8,128)S(1)} fusion(f32[256,1280]{1,0:T(8,128)} %get-tuple-element.53, f32[256,256]{1,0:T(8,128)} %get-tuple-element.54), kind=kOutput, calls=%fused_computation.94 | convolution fusion | flops 1006632960 | bytes 2883584 | tf_op jit(solution)/shard_map/dot_general | solution.py:112
  306.3 0.0 copy-start.6
  306.3 1.2 convolution_subtract_fusion.3
  307.5 0.0 copy-done.9
  307.6 0.5 copy-done.6
  308.1 2.4 convolution_subtract_fusion
  310.5 2.2 fusion
  312.7 0.4 fusion.4
  313.1 19.1 %shard_map.21 = f32[1280,20,1,128]{3,2,1,0:T(1,128)} custom-call(f32[1280,20,1,128]{3,2,1,0:T(1,128)} %get-tuple-element.52.x_ref, bf16[1280,512]{1,0:T(8,128)(2,1)S(1)} %get-tuple-element.60.left_high, bf16[1280,512]{1,0:T(8,128)(2,1)S(1)} %get-tuple-element.59.left_low, bf16[512,2560]{1,0:T(8,128)(2,1)S(1)} %get-tuple-element.58.right_high, ...), custom_call_target="tpu_custom_call" | custom-call | tf_op jit(solution)/shard_map/pallas_call | solution.py:1173
  (6 shorter events, 0.1 us)
Async XLA Ops:
  56.9 6.4 %copy-start.10 = (f32[2,1280,256]{2,1,0:T(8,128)S(1)}, f32[2,1280,256]{2,1,0:T(8,128)}, u32[]{:S(2)}) copy-start(f32[2,1280,256]{2,1,0:T(8,128)} %get-tuple-element.31) | copy-start | bytes 7864324
  63.3 0.7 copy-start.4
  63.3 1.0 copy-start.12
  69.8 1.6 copy-start
  200.8 1.3 copy-start.1
  200.8 1.5 copy-start.2
  200.8 1.6 copy-start.3
  200.8 11.0 %copy-start.5 = (f32[1,256]{1,0:T(1,128)}, f32[1,256]{1,0:T(1,128)S(1)}, u32[]{:S(2)}) copy-start(f32[1,256]{1,0:T(1,128)S(1)} %get-tuple-element.43.refs_3_) | copy-start | bytes 3076
  204.0 2.2 copy-start.8
  206.2 2.6 copy-start.7
  206.2 2.7 copy-start.11
  302.6 4.9 %copy-start.9 = (f32[256,2560]{1,0:T(8,128)S(1)}, f32[256,2560]{1,0:T(8,128)}, u32[]{:S(2)}) copy-start(f32[256,2560]{1,0:T(8,128)} %get-tuple-element.56) | copy-start | bytes 7864324
  306.3 1.7 copy-start.6

commit v5 on v4

--- a/solution.py
+++ b/solution.py
@@ -458,12 +458,21 @@
 
     chain.spread(EARLY, chain.chunks)
 
+    for chunk in range(EARLY):
+        @pl.when(place.plane <= EARLY - chunk)
+        def _():
+            chain.step(chunk)
+
     @pl.when(place.plane > 0)
     def _():
         line[0].wait_recv()
 
     gathers = plane_gather(place, gram_ref.at[place.me], send_two, recv_two)
-    chain.step(0)
+    for chunk in range(EARLY):
+        @pl.when(place.plane > EARLY - chunk)
+        def _():
+            chain.step(chunk)
+
     spread.send()
 
     @pl.when(has)
@@ -482,7 +491,7 @@
     size = inverse_ref.shape[0]
     orthogonal_top(
         gram_ref[...].reshape(size, size), top, 0, inverse_ref, shifted_ref, sign_ref,
-        later_steps(chain, 1, 3),
+        later_steps(chain, EARLY, 2),
     )
 
     @pl.when(first)
@@ -580,7 +589,7 @@
     vec = vec_rows[...]
     vec_parts = split(vec)
     change = applied_rows[...] - mm3(vec_parts, half)
-    panel = later_ref[...] - mm(vec, ahead, 1, 0) - mm(change, old, 1, 1)
+    panel = later_ref[1] - mm(vec, ahead, 1, 0) - mm(change, old, 1, 1)
     lines = lax.broadcasted_iota(jnp.int32, panel.shape, 0)
     above = (below + BAND) // tile
     limit = (above // rows + jnp.where(place.row < above % rows, 1, 0)) * tile
@@ -670,6 +679,9 @@
         top_line(1).wait_recv()
         top_near.start()
 
+    ready = min(6, chain.chunks)
+    for chunk in range(3, ready):
+        chain.step(chunk)
     for copy in gathers:
         copy.wait()
 
@@ -679,7 +691,7 @@
 
     orthogonal_top(
         gram_ref[...].reshape(size, size), top, 1, inverse_ref, shifted_ref, sign_ref,
-        later_steps(chain, 3, 2),
+        later_steps(chain, ready, 2),
     )
     swap.wait_send()
     for copy in line:
@@ -769,10 +781,10 @@
     take = lambda count: [refs.pop(0) for _ in range(count)]
     x_ref, left_ref, shifted_ref, sign_ref, vec_ref = take(5)
     old_high, old_low, new_high, new_low = take(4) if fixed else [None] * 4
-    row_ref, transform_ref, applied_ref, inner_ref = take(4)
+    applied_row_ref, transform_ref, applied_ref, inner_ref = take(4)
     next_ref = take(1)[0] if tiles else None
     kept_ref = take(1)[0] if fixed else None
-    block, part, near, pair, left_in, right_in, left_out, right_out, out_ref = take(9)
+    block, part, near, pair, left_in, right_in, left_out, right_out, out_ref, row_ref = take(10)
     total_ref, stack, parts = take(3)
     (
         load, near_send, near_recv, left_send, left_recv, right_send, right_recv,
@@ -1044,6 +1056,7 @@
 
     lax.fori_loop(0, subs, drain, 0)
     lax.fori_loop(0, chunks, drain_chunk, 0)
+    applied_row_ref[...] = mm3(split(row_ref[...].T), split(transform_ref[...]), 1, 1)
     for copy in gathers:
         copy.wait()
     if tiles:
@@ -1073,7 +1086,7 @@
     square = jax.ShapeDtypeStruct((BAND, BAND), f32)
     wide = jax.ShapeDtypeStruct((BAND, width), f32)
     shapes = (
-        jax.ShapeDtypeStruct((BAND, row_count), f32),
+        jax.ShapeDtypeStruct((row_count, BAND), f32),
         square,
         wide,
         jax.ShapeDtypeStruct(sums, f32),
@@ -1092,6 +1105,7 @@
         + [pltpu.VMEM((subs,) + piece, f32)] * 5
         + [
             pltpu.VMEM((BAND, width), f32),
+            pltpu.VMEM((BAND, row_count), f32),
             pltpu.VMEM((BAND, BAND), f32),
             pltpu.VMEM(sums, f32),
             pltpu.VMEM((cols - 1,) + sums[1:], f32),
@@ -1215,7 +1229,7 @@
         unit_cols = (band[:, None] == global_cols[None, :] - below).astype(jnp.float32)
         vec_cols = multiply(inverse, panel_cols) - unit_cols * signs.reshape(BAND, 1)
         first = below // tile_size
-        sums_rows, transform, applied, inner, *rest = apply(
+        applied_rows, transform, applied, inner, *rest = apply(
             kept,
             jnp.concatenate(split_outside(vec_rows_t), 0),
             shifted,
@@ -1225,7 +1239,6 @@
             more,
             1 + panel_index,
         )
-        applied_rows = multiply(sums_rows, transform, 0, 1)
         if last:
             break
         old_shifted, old_cols = shifted, vec_cols
@@ -1235,7 +1248,7 @@
         ) = next_panel(
             (
                 vec_rows, applied_rows, vec_cols, applied, transform, inner, rest[0], shifted,
-                rows_held[panel_index + 1],
+                rows_held,
             ),
             x4,
             below,

time: 339 us -> 329 us (0.971)
  matrix products: 32.8 us -> 27.5 us
  local copies, waits for them, and re-layouts: 5.63 us -> 1.52 us
    dot_general x12 -> x10, matrix products: 32.8 us -> 27.5 us  [multiply(): lax.dot_general(first, second, (((first_dim,), (second_dim,)), ((), ())),...]
where the time goes in v5:
time: 329 us; the launch traced here: 325 us
  Pallas kernels  290 us (88%)
  matrix products  27.5 us (8%)
  other arithmetic  5.47 us (2%)
    pallas_call x2, Pallas kernels, apply(): pl.pallas_call(functools.partial(apply_kernel, rows, cols, tiles, kept),...  160 us
    pallas_call x1, Pallas kernels, first_panel(): pl.pallas_call(functools.partial(first_kernel, rows, cols), out_shape=(sq...  56.8 us
    pallas_call x1, Pallas kernels, next_panel(): pl.pallas_call(functools.partial(next_kernel, rows, cols, below), out_sha...  53.9 us
    dot_general x10, matrix products, multiply(): lax.dot_general(first, second, (((first_dim,), (second_dim,)), ((), ())),...  27.5 us
    pallas_call x1, Pallas kernels, update(): pl.pallas_call(update_kernel, out_shape=jax.ShapeDtypeStruct(x4.shape, x4...  19 us

profile of v5, /device:TPU:0, one launch (start us, length us, event | category | flops | bytes accessed | tf_op | source)
XLA Modules:
  0.0 325.2 jit_solution(12918999908943665549)
XLA Ops:
  0.1 56.8 %shard_map.17 = (f32[256,256]{1,0:T(8,128)}, f32[256,256]{1,0:T(8,128)}, f32[1,256]{1,0:T(1,128)}, f32[2,1280,256]{2,1,0:T(8,128)}, f32[256,2560]{1,0:T(8,128)}) custom-call(f32[1280,20,1,128]{3,2,1,0:T(1,128)} %bitcast.46), custom_call_target="tpu_custom_call" | custom-call | tf_op jit(solution)/shard_map/pallas_call | solution.py:527
  56.9 0.0 copy-start.4
  56.9 0.0 copy-start.8
  56.9 0.0 copy-start.12
  56.9 6.4 %fusion.3.refs_4_.refs_2_ = f32[256,2560]{1,0:T(8,128)} fusion(f32[256,256]{1,0:T(8,128)} %get-tuple-element.32, f32[256,2560]{1,0:T(8,128)} %get-tuple-element.35, f32[256]{0:T(256)} %bitcast.40, s32[2560]{0:T(1024)S(1)} %get-tuple-element.71, pred[2560]{0:T(1024)(128)(4,1)S(1)} %get-tuple-element.73), kind=kOutput, calls=%fused_computation.11 | convolution fusion | flops 2015887360 | bytes 5518848 | tf_op jit(solution)/shard_map/dot_general | solution.py:112
  63.4 0.0 copy-done.4
  63.4 0.0 copy-done.8
  63.4 0.0 copy-done.12
  63.4 1.6 reduce-precision_convert_fusion.3
  65.0 0.1 pad_maximum_fusion.2.refs_1_
  65.1 0.0 copy-start
  65.1 1.5 copy.2
  66.5 1.5 select_subtract_fusion.refs_0_
  68.1 0.0 copy-done
  68.1 77.9 %shard_map.18 = (f32[1280,256]{1,0:T(8,128)S(1)}, f32[256,256]{1,0:T(8,128)S(1)}, f32[256,2560]{1,0:T(8,128)}, f32[8,32,256]{2,1,0:T(8,128)S(1)}, f32[256,256]{1,0:T(8,128)S(1)}) custom-call(f32[1280,20,1,128]{3,2,1,0:T(1,128)} %bitcast.47, bf16[512,1280]{1,0:T(8,128)(2,1)S(1)} %pad_maximum_fusion.2.refs_1_, f32[256,256]{1,0:T(8,128)S(1)} %copy-done, ...), custom_call_target="tpu_custom_call" | custom-call | tf_op jit(solution)/shard_map/pallas_call | solution.py:1095
  146.0 53.9 %shard_map.19 = (f32[256,256]{1,0:T(8,128)S(1)}, f32[256,256]{1,0:T(8,128)S(1)}, f32[1,256]{1,0:T(1,128)S(1)}, f32[1280,256]{1,0:T(8,128)S(1)}, f32[256,2560]{1,...) custom-call(f32[1280,256]{1,0:T(8,128)S(1)} %select_subtract_fusion., ...), custom_call_target="tpu_custom_call" | custom-call | tf_op jit(solution)/shard_map/pallas_call | solution.py:721
  199.9 0.0 copy-start.1
  199.9 0.0 copy-start.2
  199.9 0.0 copy-start.3
  199.9 0.0 copy-start.5
  200.0 1.2 convolution_subtract_fusion.4
  201.2 0.0 copy-start.9
  201.2 1.6 reduce-precision_convert_fusion.2
  202.8 0.0 copy-done.1
  202.8 0.0 copy-done.2
  202.8 0.0 copy-done.3
  202.8 1.2 pad_maximum_fusion.3.refs_1_
  204.0 0.0 copy-done.9
  204.0 0.0 copy-start.7
  204.0 0.0 copy-start.10
  204.0 2.6 convolution_bitcast_fusion
  206.6 0.0 copy-done.7
  206.7 0.0 copy-done.10
  206.7 3.0 fusion.2
  209.7 0.0 copy-done.5
  209.7 4.3 %convolution_subtract_fusion.1.refs_4_ = f32[256,2560]{1,0:T(8,128)} fusion(f32[256,256]{1,0:T(8,128)S(1)} %get-tuple-element.41, f32[256,2560]{1,0:T(8,128)S(1)} %fusion.2, f32[256]{0:T(256)S(1)} %bitcast.45, s32[2560]{0:T(1024)S(1)} %get-tuple-element.70), kind=kOutput, calls=%fused_computation.5 | convolution fusion | flops 2015232000 | bytes 5516288 | tf_op jit(solution)/shard_map/dot_general | solution.py:112
  214.0 0.0 copy-start.6
  214.0 82.2 %shard_map.20 = (f32[1280,256]{1,0:T(8,128)}, f32[256,256]{1,0:T(8,128)}, f32[256,2560]{1,0:T(8,128)}, f32[8,32,256]{2,1,0:T(8,128)}, f32[1280,20,1,128]{3,2,1,0:T(1,128)}) custom-call(f32[1280,20,1,128]{3,2,1,0:T(1,128)} %bitcast.49, bf16[512,1280]{1,0:T(8,128)(2,1)} %pad_maximum_fusion.3.refs_1_, f32[256,256]{1,0:T(8,128)} %copy-done.3, ...), custom_call_target="tpu_custom_call" | custom-call | tf_op jit(solution)/shard_map/pallas_call | solution.py:1095
  296.2 1.4 convolution_multiply_fusion
  297.6 0.0 copy-done.6
  297.6 0.0 copy-start.11
  297.6 4.2 %convolution_subtract_fusion = f32[256,2560]{1,0:T(8,128)S(1)} fusion(f32[256,2560]{1,0:T(8,128)} %get-tuple-element.56, f32[256,256]{1,0:T(8,128)S(1)} %convolution_multiply_fusion, f32[256,2560]{1,0:T(8,128)S(1)} %copy-done.6), kind=kOutput, calls=%fused_computation.4 | convolution fusion | flops 2013921280 | bytes 8126464 | tf_op jit(solution)/shard_map/dot_general | solution.py:112
  301.8 0.0 copy-done.11
  301.8 1.2 convolution_subtract_fusion.3
  303.0 0.4 fusion.4
  303.4 2.2 fusion
  305.6 19.0 %shard_map.21 = f32[1280,20,1,128]{3,2,1,0:T(1,128)} custom-call(f32[1280,20,1,128]{3,2,1,0:T(1,128)} %get-tuple-element.52.x_ref, bf16[1280,512]{1,0:T(8,128)(2,1)S(1)} %get-tuple-element.60.left_high, bf16[1280,512]{1,0:T(8,128)(2,1)S(1)} %get-tuple-element.59.left_low, bf16[512,2560]{1,0:T(8,128)(2,1)S(1)} %get-tuple-element.58.right_high, ...), custom_call_target="tpu_custom_call" | custom-call | tf_op jit(solution)/shard_map/pallas_call | solution.py:1187
  (4 shorter events, 0.0 us)
Async XLA Ops:
  56.9 6.4 %copy-start.4 = (f32[1,256]{1,0:T(1,128)S(1)}, f32[1,256]{1,0:T(1,128)}, u32[]{:S(2)}) copy-start(f32[1,256]{1,0:T(1,128)} %get-tuple-element.33.refs_3_) | copy-start | bytes 3076
  56.9 6.4 %copy-start.8 = (f32[2,1280,256]{2,1,0:T(8,128)S(1)}, f32[2,1280,256]{2,1,0:T(8,128)}, u32[]{:S(2)}) copy-start(f32[2,1280,256]{2,1,0:T(8,128)} %get-tuple-element.31.refs_8_) | copy-start | bytes 7864324
  56.9 6.4 %copy-start.12 = (f32[256,256]{1,0:T(8,128)S(1)}, f32[256,256]{1,0:T(8,128)}, u32[]{:S(2)}) copy-start(f32[256,256]{1,0:T(8,128)} %get-tuple-element.32) | copy-start | bytes 786436
  65.1 3.0 copy-start
  199.9 2.9 copy-start.1
  199.9 2.9 copy-start.2
  199.9 2.9 copy-start.3
  199.9 9.8 %copy-start.5 = (f32[1,256]{1,0:T(1,128)}, f32[1,256]{1,0:T(1,128)S(1)}, u32[]{:S(2)}) copy-start(f32[1,256]{1,0:T(1,128)S(1)} %get-tuple-element.43.refs_3_) | copy-start | bytes 3076
  201.2 2.8 copy-start.9
  204.0 2.6 copy-start.7
  204.0 2.7 copy-start.10
  214.0 83.6 %copy-start.6 = (f32[256,2560]{1,0:T(8,128)S(1)}, f32[256,2560]{1,0:T(8,128)}, u32[]{:S(2)}) copy-start(f32[256,2560]{1,0:T(8,128)} %convolution_subtract_fusion.1.refs_4_) | copy-start | bytes 7864324
  297.6 4.2 %copy-start.11 = (f32[1280,256]{1,0:T(8,128)S(1)}, f32[1280,256]{1,0:T(8,128)}, u32[]{:S(2)}) copy-start(f32[1280,256]{1,0:T(8,128)} %get-tuple-element.53) | copy-start | bytes 3932164

commit v6 on v5

--- a/solution.py
+++ b/solution.py
@@ -278,7 +278,10 @@
 
     def part(self, chunk):
         start = pl.multiple_of(self.place.core * self.tile, self.tile)
-        return self.ref.at[pl.ds(start, self.tile), pl.ds(chunk * self.width, self.width)]
+        here = chunk * self.width
+        if not isinstance(here, int):
+            here = pl.multiple_of(here, self.width)
+        return self.ref.at[pl.ds(start, self.tile), pl.ds(here, self.width)]
 
     def hop(self, chunk, step, sem):
         part = self.part(chunk)
@@ -341,6 +344,13 @@
     def join(self):
         for chunk in range(self.chunks):
             self.shared(chunk).wait_recv()
+
+    def late_step(self, chunk):
+        index = chunk - jnp.where(jnp.abs(self.place.plane - self.source) > 1, 1, 0)
+
+        @pl.when((index >= 0) & (index < self.chunks))
+        def _():
+            self.step(index)
 
     def finish(self, joined=False):
         place = self.place
@@ -371,19 +381,23 @@
 CHUNK = 256
 
 
-def later_steps(chain, first, every):
+def later_steps(chain, first, every, late=False):
     count = [0]
 
     def hook():
         count[0] += 1
         chunk = first + count[0] // every - 1
-        if count[0] % every == 0 and first <= chunk < chain.chunks:
-            chain.step(chunk)
+        if count[0] % every == 0 and first <= chunk < chain.chunks + late:
+            if late:
+                chain.late_step(chunk)
+            else:
+                chain.step(chunk)
 
     return hook
 
 
 EARLY = 3
+PARTS = 4
 
 
 def first_kernel(rows, cols, x_ref, inverse_ref, shifted_ref, sign_ref, rows_ref, cols_ref, *refs):
@@ -400,13 +414,18 @@
     )
     first = place.plane == 0
 
-    def spot(col):
+    share = rows_ref.shape[1] // PARTS
+
+    def spot(col, index):
         start = pl.multiple_of(lax.rem(col, panel_tiles) * tile, tile)
-        return rows_ref.at[col // panel_tiles, :, pl.ds(start, tile)]
+        return rows_ref.at[col // panel_tiles, pl.ds(index * share, share), pl.ds(start, tile)]
 
     has = place.col < held
-    own = spot(lax.rem(place.col, held))
-    fill = pltpu.make_async_copy(x_ref.at[:, 0, 0, :], own, load.at[0])
+    holder = lax.rem(place.col, held)
+    begin = pl.multiple_of(lax.rem(holder, panel_tiles) * tile, tile)
+    fill = pltpu.make_async_copy(
+        x_ref.at[:, 0, 0, :], rows_ref.at[holder // panel_tiles, :, pl.ds(begin, tile)], load.at[0]
+    )
 
     @pl.when(has)
     def _():
@@ -414,17 +433,20 @@
 
     chain.start()
     place.greet()
-    copies = [
-        remote(
-            own,
-            own,
-            send_row.at[step - 1],
-            recv_row.at[lax.rem(place.col, held)],
-            place.row,
-            lax.rem(place.col + step, cols),
-        )
-        for step in range(1, cols)
-    ]
+    def row_copies(first, last):
+        return [
+            remote(
+                spot(holder, index),
+                spot(holder, index),
+                send_row.at[index, step - 1],
+                recv_row.at[index, holder],
+                place.row,
+                lax.rem(place.col + step, cols),
+            )
+            for index in range(first, last)
+            for step in range(1, cols)
+        ]
+
     line = [
         remote(
             gram_ref.at[place.me],
@@ -438,6 +460,17 @@
     ]
     chain.share()
     chain.spread(0, EARLY)
+
+    @pl.when(has)
+    def _():
+        fill.wait()
+        for copy in row_copies(0, 1):
+            copy.start()
+
+        @pl.when(place.plane > 0)
+        def _():
+            for copy in row_copies(1, 2):
+                copy.start()
 
     @pl.when(first)
     def _():
@@ -477,8 +510,12 @@
 
     @pl.when(has)
     def _():
-        fill.wait()
-        for copy in copies:
+        @pl.when(first)
+        def _():
+            for copy in row_copies(1, 2):
+                copy.start()
+
+        for copy in row_copies(2, PARTS):
             copy.start()
 
     for copy in gathers:
@@ -503,13 +540,17 @@
 
     @pl.when(has)
     def _():
-        for copy in copies:
+        for copy in row_copies(0, PARTS):
             copy.wait_send()
 
     for col in range(held):
         @pl.when(place.col != col)
         def _():
-            remote(spot(col), spot(col), send_row.at[0], recv_row.at[col], place.row, place.col).wait_recv()
+            for index in range(PARTS):
+                remote(
+                    spot(col, index), spot(col, index), send_row.at[index, 0],
+                    recv_row.at[index, col], place.row, place.col,
+                ).wait_recv()
 
     chain.finish(True)
 
@@ -547,8 +588,8 @@
             dma((count - 1,)),
             dma((count - 1,)),
             dma((1,)),
-            dma((cols - 1,)),
-            dma((PANELS * panel_tiles,)),
+            dma((PARTS, cols - 1)),
+            dma((PARTS, PANELS * panel_tiles)),
             dma((panel_tiles, count - 1)),
             dma((panel_tiles, 2)),
         ]
@@ -580,12 +621,13 @@
     chain.start()
     place.greet()
     chain.share()
-    chain.spread(0, EARLY)
+    chain.spread(0, EARLY + 2)
     half_full = 0.5 * mm(transform_ref[...], inner_ref[...], 1, 0)
     half = split(half_full)
     old = old_ref[...]
     ahead = applied_next[...] - mm(half_full, old, 0, 1)
     ahead_ref[...] = ahead
+    chain.late_step(0)
     vec = vec_rows[...]
     vec_parts = split(vec)
     change = applied_rows[...] - mm3(vec_parts, half)
@@ -606,7 +648,7 @@
         for core in range(2):
             start = (2 * col + core) * height
             gram_in[col, core] = gram_sum[start : start + height, :]
-    chain.step(0)
+    chain.late_step(1)
     swap = remote(
         gram_in.at[place.col, 1 - place.core], near.at[0], near_send.at[0], near_recv.at[0],
         place.other, place.col,
@@ -648,8 +690,8 @@
         top_first.start()
         target[...] = block[...]
 
-    chain.spread(EARLY, chain.chunks)
-    chain.step(1)
+    chain.spread(EARLY + 2, chain.chunks)
+    chain.late_step(2)
     group = 5 if x_ref.shape[1] % 10 == 0 else 1
     wide = x_ref.shape[1] // group * tile
     half_t = split(half_full.T)
@@ -665,7 +707,7 @@
         return carry
 
     lax.fori_loop(0, group, own_cols, 0)
-    chain.step(2)
+    chain.late_step(3)
     total = near_sum[0]
     for slot, copy in enumerate(line):
         copy.wait_recv()
@@ -679,9 +721,8 @@
         top_line(1).wait_recv()
         top_near.start()
 
-    ready = min(6, chain.chunks)
-    for chunk in range(3, ready):
-        chain.step(chunk)
+    for chunk in range(4, 6):
+        chain.late_step(chunk)
     for copy in gathers:
         copy.wait()
 
@@ -691,7 +732,7 @@
 
     orthogonal_top(
         gram_ref[...].reshape(size, size), top, 1, inverse_ref, shifted_ref, sign_ref,
-        later_steps(chain, ready, 2),
+        later_steps(chain, 6, 2, True),
     )
     swap.wait_send()
     for copy in line:
@@ -892,6 +933,13 @@
     source = held // 2 == plane
     target_row = 2 * plane + lax.rem(place.col, 2)
     to_self = target_row == place.row
+    square = cols == 4
+    beside = place.col + 1 - 2 * lax.rem(place.col, 2)
+    across = lax.rem(place.col + 2, 4)
+    targets = (place.col, beside, across) if square else tuple(
+        lax.rem(place.col + step, cols) for step in range(cols)
+    )
+    relays = (lax.rem(place.row, cols) == across) if square else None
 
     def depths(index):
         return pl.ds(pl.multiple_of(lax.rem(index, pieces) * depth, depth), depth)
@@ -913,8 +961,18 @@
             row_send.at[index, step],
             row_recv.at[index],
             target_row,
-            lax.rem(place.col + step, cols),
-        )
+            targets[step],
+        )
+
+    def relay_of(index):
+        spot = row_ref.at[depths(index), row_lanes(index)]
+        return remote(spot, spot, row_send.at[index, 3], row_recv.at[index], place.row, beside)
+
+    def relay(index):
+        @pl.when(relays & (index >= 0) & (index < subs))
+        def _():
+            relay_of(index).wait_recv()
+            relay_of(index).start()
 
     def chain(step, carry):
         index = step - left_lag
@@ -959,7 +1017,7 @@
 
             @pl.when(source)
             def _():
-                for step in range(1, cols):
+                for step in range(1, len(targets)):
                     row_of(done, step).start()
 
                 @pl.when(to_self)
@@ -970,11 +1028,13 @@
                 def _():
                     row_of(done, 0).start()
 
+        if square:
+            relay(done - HOP)
         return carry
 
     lax.fori_loop(0, chunks, product, 0)
     joined(chunks - 1)
-    steps = subs + HOP * (planes - 2)
+    steps = subs + HOP * (planes - 2 + square)
     count = [0, max(chunks - BEHIND, 0) * pieces]
 
     def hook():
@@ -1020,6 +1080,8 @@
     plane_scatter(place, place.peers()[: cols - 1], stack, parts, inner_ref, send_one, recv_one)
     gathers = plane_gather(place, inner_ref.at[place.me], send_two, recv_two)
     gets = jnp.logical_not(source & to_self)
+    if square:
+        gets = gets & jnp.logical_not(relays)
 
     def drain(index, carry):
         both_of(index).wait_send()
@@ -1034,7 +1096,7 @@
 
         @pl.when(source)
         def _():
-            for step in range(1, cols):
+            for step in range(1, len(targets)):
                 row_of(index, step).wait_send()
 
             @pl.when(jnp.logical_not(to_self))
@@ -1044,6 +1106,11 @@
         @pl.when(gets)
         def _():
             row_of(index, 0).wait_recv()
+
+        if square:
+            @pl.when(relays)
+            def _():
+                relay_of(index).wait_send()
 
         return carry
 

time: 329 us -> 330 us (level)
    pallas_call x2, Pallas kernels: 160 us -> 165 us  [apply(): pl.pallas_call(functools.partial(apply_kernel, rows, cols, tiles, kept),...]
    pallas_call x1, Pallas kernels: 56.8 us -> 52.7 us  [first_panel(): pl.pallas_call(functools.partial(first_kernel, rows, cols), out_shape=(sq...]
where the time goes in v6:
time: 330 us; the launch traced here: 325 us
  Pallas kernels  290 us (88%)
  matrix products  27.5 us (8%)
  other arithmetic  5.47 us (2%)
    pallas_call x2, Pallas kernels, apply(): pl.pallas_call(functools.partial(apply_kernel, rows, cols, tiles, kept),...  165 us
    pallas_call x1, Pallas kernels, next_panel(): pl.pallas_call(functools.partial(next_kernel, rows, cols, below), out_sha...  53.4 us
    pallas_call x1, Pallas kernels, first_panel(): pl.pallas_call(functools.partial(first_kernel, rows, cols), out_shape=(sq...  52.7 us
    dot_general x10, matrix products, multiply(): lax.dot_general(first, second, (((first_dim,), (second_dim,)), ((), ())),...  27.5 us
    pallas_call x1, Pallas kernels, update(): pl.pallas_call(update_kernel, out_shape=jax.ShapeDtypeStruct(x4.shape, x4...  19 us

profile of v6, /device:TPU:0, one launch (start us, length us, event | category | flops | bytes accessed | tf_op | source)
XLA Modules:
  0.0 325.3 jit_solution(5123782526983682622)
XLA Ops:
  0.1 52.7 %shard_map.17 = (f32[256,256]{1,0:T(8,128)}, f32[256,256]{1,0:T(8,128)}, f32[1,256]{1,0:T(1,128)}, f32[2,1280,256]{2,1,0:T(8,128)}, f32[256,2560]{1,0:T(8,128)}) custom-call(f32[1280,20,1,128]{3,2,1,0:T(1,128)} %bitcast.46), custom_call_target="tpu_custom_call" | custom-call | tf_op jit(solution)/shard_map/pallas_call | solution.py:568
  52.8 0.0 copy-start.4
  52.8 0.0 copy-start.8
  52.8 0.0 copy-start.12
  52.8 6.4 %fusion.3.refs_4_.refs_2_ = f32[256,2560]{1,0:T(8,128)} fusion(f32[256,256]{1,0:T(8,128)} %get-tuple-element.32, f32[256,2560]{1,0:T(8,128)} %get-tuple-element.35, f32[256]{0:T(256)} %bitcast.40, s32[2560]{0:T(1024)S(1)} %get-tuple-element.71, pred[2560]{0:T(1024)(128)(4,1)S(1)} %get-tuple-element.73), kind=kOutput, calls=%fused_computation.11 | convolution fusion | flops 2015887360 | bytes 5518848 | tf_op jit(solution)/shard_map/dot_general | solution.py:112
  59.2 0.0 copy-done.4
  59.2 0.0 copy-done.8
  59.2 0.0 copy-done.12
  59.2 1.6 reduce-precision_convert_fusion.3
  60.8 0.1 pad_maximum_fusion.2.refs_1_
  60.9 0.0 copy-start
  61.0 1.5 copy.2
  62.4 1.5 select_subtract_fusion.refs_0_
  64.0 0.0 copy-done
  64.0 80.3 %shard_map.18 = (f32[1280,256]{1,0:T(8,128)S(1)}, f32[256,256]{1,0:T(8,128)S(1)}, f32[256,2560]{1,0:T(8,128)}, f32[8,32,256]{2,1,0:T(8,128)S(1)}, f32[256,256]{1,0:T(8,128)S(1)}) custom-call(f32[1280,20,1,128]{3,2,1,0:T(1,128)} %bitcast.47, bf16[512,1280]{1,0:T(8,128)(2,1)S(1)} %pad_maximum_fusion.2.refs_1_, f32[256,256]{1,0:T(8,128)S(1)} %copy-done, ...), custom_call_target="tpu_custom_call" | custom-call | tf_op jit(solution)/shard_map/pallas_call | solution.py:1162
  144.3 53.4 %shard_map.19 = (f32[256,256]{1,0:T(8,128)S(1)}, f32[256,256]{1,0:T(8,128)S(1)}, f32[1,256]{1,0:T(1,128)S(1)}, f32[1280,256]{1,0:T(8,128)S(1)}, f32[256,2560]{1,...) custom-call(f32[1280,256]{1,0:T(8,128)S(1)} %select_subtract_fusion., ...), custom_call_target="tpu_custom_call" | custom-call | tf_op jit(solution)/shard_map/pallas_call | solution.py:762
  197.6 0.0 copy-start.1
  197.7 0.0 copy-start.2
  197.7 0.0 copy-start.3
  197.7 0.0 copy-start.5
  197.7 1.2 convolution_subtract_fusion.4
  198.9 0.0 copy-start.9
  198.9 1.6 reduce-precision_convert_fusion.2
  200.5 0.0 copy-done.1
  200.5 0.0 copy-done.2
  200.5 0.0 copy-done.3
  200.6 1.2 pad_maximum_fusion.3.refs_1_
  201.7 0.0 copy-done.9
  201.7 0.0 copy-start.7
  201.7 0.0 copy-start.10
  201.7 2.6 convolution_bitcast_fusion
  204.4 0.0 copy-done.7
  204.4 0.0 copy-done.10
  204.4 3.0 fusion.2
  207.4 0.0 copy-done.5
  207.4 4.3 %convolution_subtract_fusion.1.refs_4_ = f32[256,2560]{1,0:T(8,128)} fusion(f32[256,256]{1,0:T(8,128)S(1)} %get-tuple-element.41, f32[256,2560]{1,0:T(8,128)S(1)} %fusion.2, f32[256]{0:T(256)S(1)} %bitcast.45, s32[2560]{0:T(1024)S(1)} %get-tuple-element.70), kind=kOutput, calls=%fused_computation.5 | convolution fusion | flops 2015232000 | bytes 5516288 | tf_op jit(solution)/shard_map/dot_general | solution.py:112
  211.7 0.0 copy-start.6
  211.7 84.6 %shard_map.20 = (f32[1280,256]{1,0:T(8,128)}, f32[256,256]{1,0:T(8,128)}, f32[256,2560]{1,0:T(8,128)}, f32[8,32,256]{2,1,0:T(8,128)}, f32[1280,20,1,128]{3,2,1,0:T(1,128)}) custom-call(f32[1280,20,1,128]{3,2,1,0:T(1,128)} %bitcast.49, bf16[512,1280]{1,0:T(8,128)(2,1)} %pad_maximum_fusion.3.refs_1_, f32[256,256]{1,0:T(8,128)} %copy-done.3, ...), custom_call_target="tpu_custom_call" | custom-call | tf_op jit(solution)/shard_map/pallas_call | solution.py:1162
  296.3 1.4 convolution_multiply_fusion
  297.8 0.0 copy-done.6
  297.8 0.0 copy-start.11
  297.8 4.2 %convolution_subtract_fusion = f32[256,2560]{1,0:T(8,128)S(1)} fusion(f32[256,2560]{1,0:T(8,128)} %get-tuple-element.56, f32[256,256]{1,0:T(8,128)S(1)} %convolution_multiply_fusion, f32[256,2560]{1,0:T(8,128)S(1)} %copy-done.6), kind=kOutput, calls=%fused_computation.4 | convolution fusion | flops 2013921280 | bytes 8126464 | tf_op jit(solution)/shard_map/dot_general | solution.py:112
  302.0 0.0 copy-done.11
  302.0 1.2 convolution_subtract_fusion.3
  303.2 0.4 fusion.4
  303.6 2.2 fusion
  305.8 19.0 %shard_map.21 = f32[1280,20,1,128]{3,2,1,0:T(1,128)} custom-call(f32[1280,20,1,128]{3,2,1,0:T(1,128)} %get-tuple-element.52.x_ref, bf16[1280,512]{1,0:T(8,128)(2,1)S(1)} %get-tuple-element.60.left_high, bf16[1280,512]{1,0:T(8,128)(2,1)S(1)} %get-tuple-element.59.left_low, bf16[512,2560]{1,0:T(8,128)(2,1)S(1)} %get-tuple-element.58.right_high, ...), custom_call_target="tpu_custom_call" | custom-call | tf_op jit(solution)/shard_map/pallas_call | solution.py:1254
  (4 shorter events, 0.0 us)
Async XLA Ops:
  52.8 6.4 %copy-start.4 = (f32[1,256]{1,0:T(1,128)S(1)}, f32[1,256]{1,0:T(1,128)}, u32[]{:S(2)}) copy-start(f32[1,256]{1,0:T(1,128)} %get-tuple-element.33.refs_3_) | copy-start | bytes 3076
  52.8 6.4 %copy-start.8 = (f32[2,1280,256]{2,1,0:T(8,128)S(1)}, f32[2,1280,256]{2,1,0:T(8,128)}, u32[]{:S(2)}) copy-start(f32[2,1280,256]{2,1,0:T(8,128)} %get-tuple-element.31.refs_8_) | copy-start | bytes 7864324
  52.8 6.4 %copy-start.12 = (f32[256,256]{1,0:T(8,128)S(1)}, f32[256,256]{1,0:T(8,128)}, u32[]{:S(2)}) copy-start(f32[256,256]{1,0:T(8,128)} %get-tuple-element.32) | copy-start | bytes 786436
  60.9 3.0 copy-start
  197.6 2.9 copy-start.1
  197.7 2.9 copy-start.2
  197.7 2.9 copy-start.3
  197.7 9.7 %copy-start.5 = (f32[1,256]{1,0:T(1,128)}, f32[1,256]{1,0:T(1,128)S(1)}, u32[]{:S(2)}) copy-start(f32[1,256]{1,0:T(1,128)S(1)} %get-tuple-element.43.refs_3_) | copy-start | bytes 3076
  198.9 2.8 copy-start.9
  201.7 2.6 copy-start.7
  201.7 2.7 copy-start.10
  211.7 86.1 %copy-start.6 = (f32[256,2560]{1,0:T(8,128)S(1)}, f32[256,2560]{1,0:T(8,128)}, u32[]{:S(2)}) copy-start(f32[256,2560]{1,0:T(8,128)} %convolution_subtract_fusion.1.refs_4_) | copy-start | bytes 7864324
  297.8 4.2 %copy-start.11 = (f32[1280,256]{1,0:T(8,128)S(1)}, f32[1280,256]{1,0:T(8,128)}, u32[]{:S(2)}) copy-start(f32[1280,256]{1,0:T(8,128)} %get-tuple-element.53) | copy-start | bytes 3932164
